TPU v7x, 512 devices: a whole 4x4x16 slice. The times are simulated.
512 devices in a mesh: lon: 32 (over y, x, core), lat: 16 (over z).
Axes of the slice: x: 4, y: 4, z: 16, core: 2. Of those that a mesh axis runs over, the one named last changes fastest.
Arguments:
- direction: float32 [75, 128, 4096], P(None, 'lat', 'lon'), may hold values from -40 to 40
- residual: float32 [75, 128, 4096], P(None, 'lat', 'lon'), may hold values from -40 to 40
- eof_basis: float32 [75, 75], replicated, may hold values from -0.75 to 0.75
- kappa_east: float32 [128, 4096], P('lat', 'lon'), may hold values from 0.02 to 0.24
- kappa_north: float32 [128, 4096], P('lat', 'lon'), may hold values from 0.02 to 0.24
- wet_mask: int32 [128, 4096], P('lat', 'lon'), may hold values 0 or 1
- obs_base: int32 [16, 32, 256], P('lat', 'lon'), may hold values from 0 to 1023, as said below
- obs_frac: float32 [2, 16, 32, 256], P(None, 'lat', 'lon'), may hold values from 0 to 1
- obs_rinv: float32 [75, 16, 32, 256], P(None, 'lat', 'lon'), may hold values from 0.25 to 4
Outputs:
- new_residual: float32 [75, 128, 4096], P(None, 'lat', 'lon')
- new_direction: float32 [75, 128, 4096], P(None, 'lat', 'lon')
- step_length: float32 [], replicated
Inputs may be any that keep to these rules, and one draw needn't show every extreme that they name: `obs_base`: s // 128 and s % 128 are the row and column of the square's south-west cell within the tile; no profile of the top tile row has its south-west cell in the grid's top row.
All inputs are finite; a program needn't handle non-finite values. No bound on the sum of `wet_mask` on one device may be relied on, other than what follows from the above.
Results may differ from a plain program's by a relative error of at most 0.000066.
Values sent between devices are 32-bit elements; how exact they have to be, the bound alone decides.
No kernel may reach another device: no remote copies, remote signals or barrier semaphores. Data moves between devices by JAX's collectives and lax.ppermute only.
A program may use at most 64 MiB of HBM per device.

v0:
```python
import jax
import jax.numpy as jnp
from jax import lax
from jax.sharding import PartitionSpec as P


def padded_2(array, sides, width):
    for axis, dim in sides:
        peers, length = (lax.axis_size(axis), array.shape[dim])
        up = [(i, (i + 1) % peers) for i in range(peers)]
        down = [(j, i) for i, j in up]
        last = lax.slice_in_dim(array, length - width, length, axis=dim)
        leading = lax.slice_in_dim(array, 0, width, axis=dim)
        before = lax.ppermute(last, axis, up)
        after = lax.ppermute(leading, axis, down)
        array = jnp.concatenate([before, array, after], axis=dim)
    return array


def swapped(array, axis, stride):
    return lax.ppermute(array, axis, [(i, i ^ 1 << stride) for i in range(lax.axis_size(axis))])


def passed_along(value, axis, steps):
    count = lax.axis_size(axis)
    pairs = [(source, (source + steps) % count) for source in range(count)]
    return lax.ppermute(value, axis, pairs)


def passed_along_2(value, axis, steps):
    count = lax.axis_size(axis)
    leading, last = (max(0, -steps), min(count, count - steps))
    return lax.ppermute(value, axis, [(source, source + steps) for source in range(leading, last)])


def with_rims(values):
    padded = padded_2(values, (("lon", 2), ("lat", 1)), 1)
    row_total = values.shape[1] + 2
    lat_index = lax.axis_index("lat")
    lat_count = lax.axis_size("lat")
    row_ids = jnp.arange(row_total)
    outside = (row_ids == 0) & (lat_index == 0) | (row_ids == row_total - 1) & (
        lat_index == lat_count - 1
    )
    return padded * jnp.where(outside, 0.0, 1.0).astype(jnp.float32)[None, :, None]


def mirror_row(top_rows):
    moved = top_rows
    for bit_index in range(lax.axis_size("lon").bit_length() - 1):
        moved = swapped(moved, "lon", bit_index)
    return moved[:, ::-1]


def diffuse(values, faces):
    east_face, west_face, north_face, south_face, fold_face = faces
    padded = with_rims(values)
    mirrored = mirror_row(values[:, -1, :])
    change = east_face * (padded[:, 1:-1, 2:] - values)
    change = change + west_face * (padded[:, 1:-1, :-2] - values)
    change = change + north_face * (padded[:, 2:, 1:-1] - values)
    change = change + south_face * (padded[:, :-2, 1:-1] - values)
    change = change.at[:, -1, :].add(fold_face * (mirrored - values[:, -1, :]))
    return values + change


def per_device(
    direction, residual, eof_basis, kappa_east, kappa_north, wet_mask, obs_base, obs_frac, obs_rinv
):
    levels, lat_cells, lon_cells = direction.shape
    old_norm = lax.psum(jnp.sum(residual * residual), ("lon", "lat"))
    wet_float = wet_mask.astype(jnp.float32)
    static = with_rims(jnp.stack([kappa_east, kappa_north, wet_float]))
    east_rim, north_rim, wet_rim = (static[0], static[1], static[2])
    east_full = east_rim[:, :-1] * wet_rim[:, :-1] * wet_rim[:, 1:]
    north_full = north_rim[:-1] * wet_rim[:-1] * wet_rim[1:]
    top_pair = mirror_row(jnp.stack([kappa_north[-1], wet_float[-1]]))
    is_top = jnp.where(lax.axis_index("lat") == lax.axis_size("lat") - 1, 1.0, 0.0).astype(
        jnp.float32
    )
    fold_face = is_top * 0.5 * (kappa_north[-1] + top_pair[0]) * wet_float[-1] * top_pair[1]
    faces = (
        east_full[1:-1, 1:],
        east_full[1:-1, :-1],
        north_full[1:, 1:-1],
        north_full[:-1, 1:-1],
        fold_face,
    )
    physical = jnp.dot(
        eof_basis,
        direction.reshape(levels, -1),
        precision=lax.Precision.HIGHEST,
        preferred_element_type=jnp.float32,
    ).reshape(direction.shape)
    for step_index in range(3):
        physical = diffuse(physical, faces)
    padded = with_rims(physical)
    row_width = lon_cells + 2
    flat_field = padded.reshape(levels, -1)
    base_flat = obs_base.reshape(-1)
    south_west = (base_flat // lon_cells + 1) * row_width + base_flat % lon_cells + 1
    corner_index = (south_west, south_west + 1, south_west + row_width, south_west + row_width + 1)
    frac_flat = obs_frac.reshape(2, -1)
    lat_frac = frac_flat[0]
    lon_frac = frac_flat[1]
    corner_weight = (
        (1.0 - lat_frac) * (1.0 - lon_frac),
        (1.0 - lat_frac) * lon_frac,
        lat_frac * (1.0 - lon_frac),
        lat_frac * lon_frac,
    )
    profiles = jnp.zeros((levels, base_flat.shape[0]), jnp.float32)
    for corner in range(4):
        profiles = profiles + corner_weight[corner][None, :] * jnp.take(
            flat_field, corner_index[corner], axis=1
        )
    weighted = obs_rinv.reshape(levels, -1) * profiles
    spread = jnp.zeros_like(flat_field)
    for corner in range(4):
        spread = spread.at[:, corner_index[corner]].add(corner_weight[corner][None, :] * weighted)
    spread = spread.reshape(padded.shape)
    east_part = spread[:, 1 : lat_cells + 2, lon_cells + 1]
    spread = spread.at[:, 1 : lat_cells + 2, 1].add(passed_along(east_part, "lon", 1))
    top_line = spread[:, lat_cells + 1, 1 : lon_cells + 1]
    adjoint = spread[:, 1 : lat_cells + 1, 1 : lon_cells + 1]
    adjoint = adjoint.at[:, 0, :].add(passed_along_2(top_line, "lat", 1))
    for step_index in range(3):
        adjoint = diffuse(adjoint, faces)
    back_term = jnp.dot(
        eof_basis.T,
        adjoint.reshape(levels, -1),
        precision=lax.Precision.HIGHEST,
        preferred_element_type=jnp.float32,
    )
    image = direction + back_term.reshape(direction.shape)
    curvature = lax.psum(jnp.sum(direction * image), ("lon", "lat"))
    step_length = old_norm / curvature
    new_residual = residual - step_length * image
    new_norm = lax.psum(jnp.sum(new_residual * new_residual), ("lon", "lat"))
    new_direction = new_residual + new_norm / old_norm * direction
    return (new_residual, new_direction, step_length)


def solution(mesh):
    return jax.shard_map(
        per_device,
        mesh=mesh,
        in_specs=(
            P(None, "lat", "lon"),
            P(None, "lat", "lon"),
            P(),
            P("lat", "lon"),
            P("lat", "lon"),
            P("lat", "lon"),
            P("lat", "lon", None),
            P(None, "lat", "lon", None),
            P(None, "lat", "lon", None),
        ),
        out_specs=(P(None, "lat", "lon"), P(None, "lat", "lon"), P()),
        check_vma=False,
    )
```

profile of v0, /device:TPU:1, one launch (start us, length us, event | category | flops | bytes accessed | tf_op | source)
XLA Modules:
  0.0 572.6 jit_solution(7379510770444932142)
XLA Ops:
  2.1 4.5 collective-permute-start
  6.6 6.2 %collective-permute-start.1 = (f32[3,8,1]{2,1,0:T(8,128)S(1)}, f32[3,8,1]{2,1,0:T(8,128)S(1)}, u32[]{:S(2)}, u32[]{:S(2)}) collective-permute-start(f32[3,8,1]{2,1,0:T(8,128)S(1)} %get-tuple-element.145), channel_id=1, source_target_pairs={{16,0},{32,16},{48,32},{64,48},{80,64},{96,80},{112,96},{128,112},... | collective-permute-start | bytes 296 | tf_op jit(solution)/shard_map/ppermute | solution.py:15
  16.3 7.0 %collective-permute-start.5 = (f32[75,8,1]{2,0,1:T(8,128)S(1)}, f32[75,8,1]{2,0,1:T(8,128)S(1)}, u32[]{:S(2)}, u32[]{:S(2)}) collective-permute-start(f32[75,8,1]{2,0,1:T(8,128)S(1)} %get-tuple-element.135), channel_id=1, source_target_pairs={{16,0},{32,16},{48,32},{64,48},{80,64},{96,80},{112,96},{128,112},... | collective-permute-start | bytes 7208 | tf_op jit(solution)/shard_map/ppermute | solution.py:15
  23.4 7.0 %collective-permute-start.8 = (f32[2,128]{1,0:T(2,128)S(1)}, f32[2,128]{1,0:T(2,128)S(1)}, u32[]{:S(2)}, u32[]{:S(2)}) collective-permute-start(f32[2,128]{1,0:T(2,128)S(1)} %pad_maximum_fusion.28), channel_id=1, source_target_pairs={{0,16},{16,0},{32,48},{48,32},{64,80},{80,64},{96,112},{112,96},{1... | collective-permute-start | bytes 3080 | tf_op jit(solution)/shard_map/ppermute | solution.py:21
  33.1 5.8 %collective-permute-start.3 = (f32[3,1,130]{2,1,0:T(1,128)S(1)}, f32[3,1,130]{2,1,0:T(1,128)S(1)}, u32[]{:S(2)}, u32[]{:S(2)}) collective-permute-start(f32[3,1,130]{2,1,0:T(1,128)S(1)} %get-tuple-element.139), channel_id=1, source_target_pairs={{1,0},{2,1},{3,2},{4,3},{5,4},{6,5},{7,6},{8,7},{9,8},{10,9},{11,1... | collective-permute-start | bytes 4688 | tf_op jit(solution)/shard_map/ppermute | solution.py:15
  60.1 4.6 collective-permute-start.7
  71.7 4.3 collective-permute-done.15
  80.7 4.4 collective-permute-start.17
  87.2 10.4 %collective-permute-start.18 = (f32[75,8,1]{2,0,1:T(8,128)S(1)}, f32[75,8,1]{2,0,1:T(8,128)S(1)}, u32[]{:S(2)}, u32[]{:S(2)}) collective-permute-start(f32[75,8,1]{2,0,1:T(8,128)S(1)} %get-tuple-element.132), channel_id=1, source_target_pairs={{0,16},{16,32},{32,48},{48,64},{64,80},{80,96},{96,112},{112,128},... | collective-permute-start | bytes 7208 | tf_op jit(solution)/shard_map/ppermute | solution.py:14
  99.9 7.0 %collective-permute-start.22 = (f32[75,128]{1,0:T(8,128)S(1)}, f32[75,128]{1,0:T(8,128)S(1)}, u32[]{:S(2)}, u32[]{:S(2)}) collective-permute-start(f32[75,128]{1,0:T(8,128)S(1)} %slice_bitcast_fusion.6), channel_id=1, source_target_pairs={{0,16},{16,0},{32,48},{48,32},{64,80},{80,64},{96,112},{112,96},{1... | collective-permute-start | bytes 115208 | tf_op jit(solution)/shard_map/ppermute | solution.py:21
  111.7 4.6 collective-permute-start.21
  118.3 4.3 collective-permute-done.24
  133.9 7.9 %collective-permute-start.27 = (f32[75,8,1]{2,0,1:T(8,128)S(1)}, f32[75,8,1]{2,0,1:T(8,128)S(1)}, u32[]{:S(2)}, u32[]{:S(2)}) collective-permute-start(f32[75,8,1]{2,0,1:T(8,128)S(1)} %get-tuple-element.130), channel_id=1, source_target_pairs={{0,16},{16,32},{32,48},{48,64},{64,80},{80,96},{96,112},{112,128},... | collective-permute-start | bytes 7208 | tf_op jit(solution)/shard_map/ppermute | solution.py:14
  143.7 5.3 collective-permute-start.31
  153.9 4.6 collective-permute-start.30
  160.4 4.3 collective-permute-done.33
  176.0 7.9 %collective-permute-start.36 = (f32[75,8,1]{2,0,1:T(8,128)S(1)}, f32[75,8,1]{2,0,1:T(8,128)S(1)}, u32[]{:S(2)}, u32[]{:S(2)}) collective-permute-start(f32[75,8,1]{2,0,1:T(8,128)S(1)} %get-tuple-element.128), channel_id=1, source_target_pairs={{0,16},{16,32},{32,48},{48,64},{64,80},{80,96},{96,112},{112,128},... | collective-permute-start | bytes 7208 | tf_op jit(solution)/shard_map/ppermute | solution.py:14
  187.9 4.4 collective-permute-done.37
  194.3 4.6 collective-permute-start.39
  225.1 8.2 %collective-permute-start.46 = (f32[75,128]{1,0:T(8,128)S(1)}, f32[75,128]{1,0:T(8,128)S(1)}, u32[]{:S(2)}, u32[]{:S(2)}) collective-permute-start(f32[75,128]{1,0:T(8,128)S(1)} %slice_bitcast_fusion.3), channel_id=1, source_target_pairs={{0,16},{16,0},{32,48},{48,32},{64,80},{80,64},{96,112},{112,96},{1... | collective-permute-start | bytes 115208 | tf_op jit(solution)/shard_map/ppermute | solution.py:21
  239.7 4.8 collective-permute-done.43
  248.6 6.1 %collective-permute-start.45 = (f32[75,1,130]{2,0,1:T(8,128)S(1)}, f32[75,1,130]{2,0,1:T(8,128)S(1)}, u32[]{:S(2)}, u32[]{:S(2)}) collective-permute-start(f32[75,1,130]{2,0,1:T(8,128)S(1)} %get-tuple-element.113), channel_id=1, source_target_pairs={{1,0},{2,1},{3,2},{4,3},{5,4},{6,5},{7,6},{8,7},{9,8},{10,9},{11,1... | collective-permute-start | bytes 117008 | tf_op jit(solution)/shard_map/ppermute | solution.py:15
  256.7 4.3 collective-permute-done.48
  272.1 8.1 %collective-permute-start.55 = (f32[75,128]{1,0:T(8,128)S(1)}, f32[75,128]{1,0:T(8,128)S(1)}, u32[]{:S(2)}, u32[]{:S(2)}) collective-permute-start(f32[75,128]{1,0:T(8,128)S(1)} %slice_bitcast_fusion.2), channel_id=1, source_target_pairs={{0,16},{16,0},{32,48},{48,32},{64,80},{80,64},{96,112},{112,96},{1... | collective-permute-start | bytes 115208 | tf_op jit(solution)/shard_map/ppermute | solution.py:21
  286.7 4.8 collective-permute-done.52
  293.5 4.6 collective-permute-start.54
  300.0 4.3 collective-permute-done.57
  315.5 8.3 %collective-permute-start.64 = (f32[75,128]{1,0:T(8,128)S(1)}, f32[75,128]{1,0:T(8,128)S(1)}, u32[]{:S(2)}, u32[]{:S(2)}) collective-permute-start(f32[75,128]{1,0:T(8,128)S(1)} %slice_bitcast_fusion.1), channel_id=1, source_target_pairs={{0,16},{16,0},{32,48},{48,32},{64,80},{80,64},{96,112},{112,96},{1... | collective-permute-start | bytes 115208 | tf_op jit(solution)/shard_map/ppermute | solution.py:21
  330.4 4.8 collective-permute-done.61
  337.2 4.6 collective-permute-start.63
  361.5 105.6 %all-reduce = (f32[]{:T(128)}, f32[]{:T(128)}) all-reduce(f32[]{:T(128)} %multiply_reduce_fusion.2, f32[]{:T(128)} %multiply_reduce_fusion.1), channel_id=1, replica_groups=mesh['lon'=32,'lat'=16] {'lon','lat'}, use_global_device_ids=true, to_apply=%region_1.0 | all-reduce | flops 2 | bytes 16 | tf_op jit(solution)/shard_map/psum | solution.py:71
  469.1 100.4 %psum.23 = f32[]{:T(128)} all-reduce(f32[]{:T(128)} %get-tuple-element.102), channel_id=1, replica_groups=mesh['lon'=32,'lat'=16] {'lon','lat'}, use_global_device_ids=true, to_apply=%region_9.11 | all-reduce | flops 1 | bytes 8 | tf_op jit(solution)/shard_map/psum | solution.py:139
  (239 shorter events, 189.2 us)
Async XLA Ops:
  2.1 29.0 %collective-permute-start = (f32[3,8,1]{2,1,0:T(8,128)S(1)}, f32[3,8,1]{2,1,0:T(8,128)S(1)}, u32[]{:S(2)}, u32[]{:S(2)}) collective-permute-start(f32[3,8,1]{2,1,0:T(8,128)S(1)} %get-tuple-element.144), channel_id=1, source_target_pairs={{0,16},{16,32},{32,48},{48,64},{64,80},{80,96},{96,112},{112,128},... | collective-permute-start | bytes 296 | tf_op jit(solution)/shard_map/ppermute | solution.py:14
  6.6 24.5 %collective-permute-start.1 = (f32[3,8,1]{2,1,0:T(8,128)S(1)}, f32[3,8,1]{2,1,0:T(8,128)S(1)}, u32[]{:S(2)}, u32[]{:S(2)}) collective-permute-start(f32[3,8,1]{2,1,0:T(8,128)S(1)} %get-tuple-element.145), channel_id=1, source_target_pairs={{16,0},{32,16},{48,32},{64,48},{80,64},{96,80},{112,96},{128,112},... | collective-permute-start | bytes 296 | tf_op jit(solution)/shard_map/ppermute | solution.py:15
  14.4 43.6 %collective-permute-start.4 = (f32[75,8,1]{2,0,1:T(8,128)S(1)}, f32[75,8,1]{2,0,1:T(8,128)S(1)}, u32[]{:S(2)}, u32[]{:S(2)}) collective-permute-start(f32[75,8,1]{2,0,1:T(8,128)S(1)} %get-tuple-element.134), channel_id=1, source_target_pairs={{0,16},{16,32},{32,48},{48,64},{64,80},{80,96},{96,112},{112,128},... | collective-permute-start | bytes 7208 | tf_op jit(solution)/shard_map/ppermute | solution.py:14
  16.3 41.7 %collective-permute-start.5 = (f32[75,8,1]{2,0,1:T(8,128)S(1)}, f32[75,8,1]{2,0,1:T(8,128)S(1)}, u32[]{:S(2)}, u32[]{:S(2)}) collective-permute-start(f32[75,8,1]{2,0,1:T(8,128)S(1)} %get-tuple-element.135), channel_id=1, source_target_pairs={{16,0},{32,16},{48,32},{64,48},{80,64},{96,80},{112,96},{128,112},... | collective-permute-start | bytes 7208 | tf_op jit(solution)/shard_map/ppermute | solution.py:15
  23.4 15.6 %collective-permute-start.8 = (f32[2,128]{1,0:T(2,128)S(1)}, f32[2,128]{1,0:T(2,128)S(1)}, u32[]{:S(2)}, u32[]{:S(2)}) collective-permute-start(f32[2,128]{1,0:T(2,128)S(1)} %pad_maximum_fusion.28), channel_id=1, source_target_pairs={{0,16},{16,0},{32,48},{48,32},{64,80},{80,64},{96,112},{112,96},{1... | collective-permute-start | bytes 3080 | tf_op jit(solution)/shard_map/ppermute | solution.py:21
  31.2 10.0 %collective-permute-start.2 = (f32[3,1,130]{2,1,0:T(1,128)S(1)}, f32[3,1,130]{2,1,0:T(1,128)S(1)}, u32[]{:S(2)}, u32[]{:S(2)}) collective-permute-start(f32[3,1,130]{2,1,0:T(1,128)S(1)} %get-tuple-element.138), channel_id=1, source_target_pairs={{0,1},{1,2},{2,3},{3,4},{4,5},{5,6},{6,7},{7,8},{8,9},{9,10},{10,1... | collective-permute-start | bytes 4688 | tf_op jit(solution)/shard_map/ppermute | solution.py:14
  33.1 10.0 %collective-permute-start.3 = (f32[3,1,130]{2,1,0:T(1,128)S(1)}, f32[3,1,130]{2,1,0:T(1,128)S(1)}, u32[]{:S(2)}, u32[]{:S(2)}) collective-permute-start(f32[3,1,130]{2,1,0:T(1,128)S(1)} %get-tuple-element.139), channel_id=1, source_target_pairs={{1,0},{2,1},{3,2},{4,3},{5,4},{6,5},{7,6},{8,7},{9,8},{10,9},{11,1... | collective-permute-start | bytes 4688 | tf_op jit(solution)/shard_map/ppermute | solution.py:15
  39.0 25.7 %collective-permute-start.13 = (f32[75,128]{1,0:T(8,128)S(1)}, f32[75,128]{1,0:T(8,128)S(1)}, u32[]{:S(2)}, u32[]{:S(2)}) collective-permute-start(f32[75,128]{1,0:T(8,128)S(1)} %slice_bitcast_fusion.7), channel_id=1, source_target_pairs={{0,16},{16,0},{32,48},{48,32},{64,80},{80,64},{96,112},{112,96},{1... | collective-permute-start | bytes 115208 | tf_op jit(solution)/shard_map/ppermute | solution.py:21
  55.6 11.0 %collective-permute-start.12 = (f32[2,128]{1,0:T(2,128)S(1)}, f32[2,128]{1,0:T(2,128)S(1)}, u32[]{:S(2)}, u32[]{:S(2)}) collective-permute-start(f32[2,128]{1,0:T(2,128)S(1)} %collective-permute-done.11), channel_id=1, source_target_pairs={{0,256},{16,272},{32,288},{48,304},{64,320},{80,336},{96,352},{112... | collective-permute-start | bytes 3080 | tf_op jit(solution)/shard_map/ppermute | solution.py:21
  58.2 20.1 %collective-permute-start.6 = (f32[75,1,130]{2,0,1:T(8,128)S(1)}, f32[75,1,130]{2,0,1:T(8,128)S(1)}, u32[]{:S(2)}, u32[]{:S(2)}) collective-permute-start(f32[75,1,130]{2,0,1:T(8,128)S(1)} %get-tuple-element.120), channel_id=1, source_target_pairs={{0,1},{1,2},{2,3},{3,4},{4,5},{5,6},{6,7},{7,8},{8,9},{9,10},{10,1... | collective-permute-start | bytes 117008 | tf_op jit(solution)/shard_map/ppermute | solution.py:14
  60.1 18.2 %collective-permute-start.7 = (f32[75,1,130]{2,0,1:T(8,128)S(1)}, f32[75,1,130]{2,0,1:T(8,128)S(1)}, u32[]{:S(2)}, u32[]{:S(2)}) collective-permute-start(f32[75,1,130]{2,0,1:T(8,128)S(1)} %get-tuple-element.121), channel_id=1, source_target_pairs={{1,0},{2,1},{3,2},{4,3},{5,4},{6,5},{7,6},{8,7},{9,8},{10,9},{11,1... | collective-permute-start | bytes 117008 | tf_op jit(solution)/shard_map/ppermute | solution.py:15
  87.2 22.4 %collective-permute-start.18 = (f32[75,8,1]{2,0,1:T(8,128)S(1)}, f32[75,8,1]{2,0,1:T(8,128)S(1)}, u32[]{:S(2)}, u32[]{:S(2)}) collective-permute-start(f32[75,8,1]{2,0,1:T(8,128)S(1)} %get-tuple-element.132), channel_id=1, source_target_pairs={{0,16},{16,32},{32,48},{48,64},{64,80},{80,96},{96,112},{112,128},... | collective-permute-start | bytes 7208 | tf_op jit(solution)/shard_map/ppermute | solution.py:14
  97.7 12.0 %collective-permute-start.19 = (f32[75,8,1]{2,0,1:T(8,128)S(1)}, f32[75,8,1]{2,0,1:T(8,128)S(1)}, u32[]{:S(2)}, u32[]{:S(2)}) collective-permute-start(f32[75,8,1]{2,0,1:T(8,128)S(1)} %get-tuple-element.133), channel_id=1, source_target_pairs={{16,0},{32,16},{48,32},{64,48},{80,64},{96,80},{112,96},{128,112},... | collective-permute-start | bytes 7208 | tf_op jit(solution)/shard_map/ppermute | solution.py:15
  109.8 14.7 %collective-permute-start.20 = (f32[75,1,130]{2,0,1:T(8,128)S(1)}, f32[75,1,130]{2,0,1:T(8,128)S(1)}, u32[]{:S(2)}, u32[]{:S(2)}) collective-permute-start(f32[75,1,130]{2,0,1:T(8,128)S(1)} %get-tuple-element.118), channel_id=1, source_target_pairs={{0,1},{1,2},{2,3},{3,4},{4,5},{5,6},{6,7},{7,8},{8,9},{9,10},{10,1... | collective-permute-start | bytes 117008 | tf_op jit(solution)/shard_map/ppermute | solution.py:14
  111.7 12.8 %collective-permute-start.21 = (f32[75,1,130]{2,0,1:T(8,128)S(1)}, f32[75,1,130]{2,0,1:T(8,128)S(1)}, u32[]{:S(2)}, u32[]{:S(2)}) collective-permute-start(f32[75,1,130]{2,0,1:T(8,128)S(1)} %get-tuple-element.119), channel_id=1, source_target_pairs={{1,0},{2,1},{3,2},{4,3},{5,4},{6,5},{7,6},{8,7},{9,8},{10,9},{11,1... | collective-permute-start | bytes 117008 | tf_op jit(solution)/shard_map/ppermute | solution.py:15
  133.9 17.9 %collective-permute-start.27 = (f32[75,8,1]{2,0,1:T(8,128)S(1)}, f32[75,8,1]{2,0,1:T(8,128)S(1)}, u32[]{:S(2)}, u32[]{:S(2)}) collective-permute-start(f32[75,8,1]{2,0,1:T(8,128)S(1)} %get-tuple-element.130), channel_id=1, source_target_pairs={{0,16},{16,32},{32,48},{48,64},{64,80},{80,96},{96,112},{112,128},... | collective-permute-start | bytes 7208 | tf_op jit(solution)/shard_map/ppermute | solution.py:14
  141.7 10.1 %collective-permute-start.28 = (f32[75,8,1]{2,0,1:T(8,128)S(1)}, f32[75,8,1]{2,0,1:T(8,128)S(1)}, u32[]{:S(2)}, u32[]{:S(2)}) collective-permute-start(f32[75,8,1]{2,0,1:T(8,128)S(1)} %get-tuple-element.131), channel_id=1, source_target_pairs={{16,0},{32,16},{48,32},{64,48},{80,64},{96,80},{112,96},{128,112},... | collective-permute-start | bytes 7208 | tf_op jit(solution)/shard_map/ppermute | solution.py:15
  152.0 14.7 %collective-permute-start.29 = (f32[75,1,130]{2,0,1:T(8,128)S(1)}, f32[75,1,130]{2,0,1:T(8,128)S(1)}, u32[]{:S(2)}, u32[]{:S(2)}) collective-permute-start(f32[75,1,130]{2,0,1:T(8,128)S(1)} %get-tuple-element.116), channel_id=1, source_target_pairs={{0,1},{1,2},{2,3},{3,4},{4,5},{5,6},{6,7},{7,8},{8,9},{9,10},{10,1... | collective-permute-start | bytes 117008 | tf_op jit(solution)/shard_map/ppermute | solution.py:14
  153.9 12.8 %collective-permute-start.30 = (f32[75,1,130]{2,0,1:T(8,128)S(1)}, f32[75,1,130]{2,0,1:T(8,128)S(1)}, u32[]{:S(2)}, u32[]{:S(2)}) collective-permute-start(f32[75,1,130]{2,0,1:T(8,128)S(1)} %get-tuple-element.117), channel_id=1, source_target_pairs={{1,0},{2,1},{3,2},{4,3},{5,4},{6,5},{7,6},{8,7},{9,8},{10,9},{11,1... | collective-permute-start | bytes 117008 | tf_op jit(solution)/shard_map/ppermute | solution.py:15
  176.0 11.9 %collective-permute-start.36 = (f32[75,8,1]{2,0,1:T(8,128)S(1)}, f32[75,8,1]{2,0,1:T(8,128)S(1)}, u32[]{:S(2)}, u32[]{:S(2)}) collective-permute-start(f32[75,8,1]{2,0,1:T(8,128)S(1)} %get-tuple-element.128), channel_id=1, source_target_pairs={{0,16},{16,32},{32,48},{48,64},{64,80},{80,96},{96,112},{112,128},... | collective-permute-start | bytes 7208 | tf_op jit(solution)/shard_map/ppermute | solution.py:14
  225.1 12.7 %collective-permute-start.46 = (f32[75,128]{1,0:T(8,128)S(1)}, f32[75,128]{1,0:T(8,128)S(1)}, u32[]{:S(2)}, u32[]{:S(2)}) collective-permute-start(f32[75,128]{1,0:T(8,128)S(1)} %slice_bitcast_fusion.3), channel_id=1, source_target_pairs={{0,16},{16,0},{32,48},{48,32},{64,80},{80,64},{96,112},{112,96},{1... | collective-permute-start | bytes 115208 | tf_op jit(solution)/shard_map/ppermute | solution.py:21
  237.8 16.9 %collective-permute-start.47 = (f32[75,128]{1,0:T(8,128)S(1)}, f32[75,128]{1,0:T(8,128)S(1)}, u32[]{:S(2)}, u32[]{:S(2)}) collective-permute-start(f32[75,128]{1,0:T(8,128)S(1)} %collective-permute-done.46), channel_id=1, source_target_pairs={{0,32},{16,48},{32,0},{48,16},{64,96},{80,112},{96,64},{112,80},{1... | collective-permute-start | bytes 115208 | tf_op jit(solution)/shard_map/ppermute | solution.py:21
  244.6 18.3 %collective-permute-start.44 = (f32[75,1,130]{2,0,1:T(8,128)S(1)}, f32[75,1,130]{2,0,1:T(8,128)S(1)}, u32[]{:S(2)}, u32[]{:S(2)}) collective-permute-start(f32[75,1,130]{2,0,1:T(8,128)S(1)} %get-tuple-element.112), channel_id=1, source_target_pairs={{0,1},{1,2},{2,3},{3,4},{4,5},{5,6},{6,7},{7,8},{8,9},{9,10},{10,1... | collective-permute-start | bytes 117008 | tf_op jit(solution)/shard_map/ppermute | solution.py:14
  248.6 14.3 %collective-permute-start.45 = (f32[75,1,130]{2,0,1:T(8,128)S(1)}, f32[75,1,130]{2,0,1:T(8,128)S(1)}, u32[]{:S(2)}, u32[]{:S(2)}) collective-permute-start(f32[75,1,130]{2,0,1:T(8,128)S(1)} %get-tuple-element.113), channel_id=1, source_target_pairs={{1,0},{2,1},{3,2},{4,3},{5,4},{6,5},{7,6},{8,7},{9,8},{10,9},{11,1... | collective-permute-start | bytes 117008 | tf_op jit(solution)/shard_map/ppermute | solution.py:15
  272.1 12.6 %collective-permute-start.55 = (f32[75,128]{1,0:T(8,128)S(1)}, f32[75,128]{1,0:T(8,128)S(1)}, u32[]{:S(2)}, u32[]{:S(2)}) collective-permute-start(f32[75,128]{1,0:T(8,128)S(1)} %slice_bitcast_fusion.2), channel_id=1, source_target_pairs={{0,16},{16,0},{32,48},{48,32},{64,80},{80,64},{96,112},{112,96},{1... | collective-permute-start | bytes 115208 | tf_op jit(solution)/shard_map/ppermute | solution.py:21
  284.7 13.4 %collective-permute-start.56 = (f32[75,128]{1,0:T(8,128)S(1)}, f32[75,128]{1,0:T(8,128)S(1)}, u32[]{:S(2)}, u32[]{:S(2)}) collective-permute-start(f32[75,128]{1,0:T(8,128)S(1)} %collective-permute-done.55), channel_id=1, source_target_pairs={{0,32},{16,48},{32,0},{48,16},{64,96},{80,112},{96,64},{112,80},{1... | collective-permute-start | bytes 115208 | tf_op jit(solution)/shard_map/ppermute | solution.py:21
  291.6 14.7 %collective-permute-start.53 = (f32[75,1,130]{2,0,1:T(8,128)S(1)}, f32[75,1,130]{2,0,1:T(8,128)S(1)}, u32[]{:S(2)}, u32[]{:S(2)}) collective-permute-start(f32[75,1,130]{2,0,1:T(8,128)S(1)} %get-tuple-element.110), channel_id=1, source_target_pairs={{0,1},{1,2},{2,3},{3,4},{4,5},{5,6},{6,7},{7,8},{8,9},{9,10},{10,1... | collective-permute-start | bytes 117008 | tf_op jit(solution)/shard_map/ppermute | solution.py:14
  293.5 12.8 %collective-permute-start.54 = (f32[75,1,130]{2,0,1:T(8,128)S(1)}, f32[75,1,130]{2,0,1:T(8,128)S(1)}, u32[]{:S(2)}, u32[]{:S(2)}) collective-permute-start(f32[75,1,130]{2,0,1:T(8,128)S(1)} %get-tuple-element.111), channel_id=1, source_target_pairs={{1,0},{2,1},{3,2},{4,3},{5,4},{6,5},{7,6},{8,7},{9,8},{10,9},{11,1... | collective-permute-start | bytes 117008 | tf_op jit(solution)/shard_map/ppermute | solution.py:15
  315.5 13.0 %collective-permute-start.64 = (f32[75,128]{1,0:T(8,128)S(1)}, f32[75,128]{1,0:T(8,128)S(1)}, u32[]{:S(2)}, u32[]{:S(2)}) collective-permute-start(f32[75,128]{1,0:T(8,128)S(1)} %slice_bitcast_fusion.1), channel_id=1, source_target_pairs={{0,16},{16,0},{32,48},{48,32},{64,80},{80,64},{96,112},{112,96},{1... | collective-permute-start | bytes 115208 | tf_op jit(solution)/shard_map/ppermute | solution.py:21
  328.5 13.4 %collective-permute-start.65 = (f32[75,128]{1,0:T(8,128)S(1)}, f32[75,128]{1,0:T(8,128)S(1)}, u32[]{:S(2)}, u32[]{:S(2)}) collective-permute-start(f32[75,128]{1,0:T(8,128)S(1)} %collective-permute-done.64), channel_id=1, source_target_pairs={{0,32},{16,48},{32,0},{48,16},{64,96},{80,112},{96,64},{112,80},{1... | collective-permute-start | bytes 115208 | tf_op jit(solution)/shard_map/ppermute | solution.py:21
  335.3 14.7 %collective-permute-start.62 = (f32[75,1,130]{2,0,1:T(8,128)S(1)}, f32[75,1,130]{2,0,1:T(8,128)S(1)}, u32[]{:S(2)}, u32[]{:S(2)}) collective-permute-start(f32[75,1,130]{2,0,1:T(8,128)S(1)} %get-tuple-element.108), channel_id=1, source_target_pairs={{0,1},{1,2},{2,3},{3,4},{4,5},{5,6},{6,7},{7,8},{8,9},{9,10},{10,1... | collective-permute-start | bytes 117008 | tf_op jit(solution)/shard_map/ppermute | solution.py:14
  337.2 12.8 %collective-permute-start.63 = (f32[75,1,130]{2,0,1:T(8,128)S(1)}, f32[75,1,130]{2,0,1:T(8,128)S(1)}, u32[]{:S(2)}, u32[]{:S(2)}) collective-permute-start(f32[75,1,130]{2,0,1:T(8,128)S(1)} %get-tuple-element.109), channel_id=1, source_target_pairs={{1,0},{2,1},{3,2},{4,3},{5,4},{6,5},{7,6},{8,7},{9,8},{10,9},{11,1... | collective-permute-start | bytes 117008 | tf_op jit(solution)/shard_map/ppermute | solution.py:15
  (46 other events, 373.4 us)
where the time goes:
time: 575 us; the launch traced here: 573 us
  starting transfers between devices  230 us (40%)
  blocking collectives  206 us (36%)
  waiting for transfers between devices  97.3 us (17%)
  other arithmetic  19 us (3%)
  local copies, waits for them, and re-layouts  13.5 us (2%)
  between operations  5.83 us (1%)
    psum x1, blocking collectives, per_device(): old_norm = lax.psum(jnp.sum(residual * residual), ('lon', 'lat'))  106 us
    ppermute x35, starting transfers between devices, swapped(): lax.ppermute(array, axis, [(i, i ^ 1 << stride) for i in range(lax.axis_s...  104 us
    psum x1, blocking collectives, per_device(): new_norm = lax.psum(jnp.sum(new_residual * new_residual), ('lon', 'lat'))  100 us
    ppermute x35, waiting for transfers between devices, swapped(): lax.ppermute(array, axis, [(i, i ^ 1 << stride) for i in range(lax.axis_s...  72.5 us
    ppermute x16, starting transfers between devices, padded_2(): after = lax.ppermute(leading, axis, down)  65.9 us
    ppermute x16, starting transfers between devices, padded_2(): before = lax.ppermute(last, axis, up)  55.8 us
    ppermute x16, waiting for transfers between devices, padded_2(): after = lax.ppermute(leading, axis, down)  19.9 us
  transfers between devices with their start and end apart: 69, of which 32 were waited for; matrix products, arithmetic and copies ran while one was open for 2% of the time, Pallas kernels for 0%

commit v1 on v0

v1 whole, which is shorter than its diff:
```python
import functools

import jax
import jax.numpy as jnp
from jax import lax
from jax.experimental import pallas as pl
from jax.experimental.pallas import tpu as pltpu
from jax.sharding import PartitionSpec as P

HIGHEST = lax.Precision.HIGHEST
LANES = 128
ROWS = 8
PAD = 80
BAND = 3 * ROWS
HALO = 7
SLOTS = 12
SOUTH, OWN, NORTH = 0, 1, 2

SMEM = pl.BlockSpec(memory_space=pltpu.SMEM)
VMEM = pl.BlockSpec(memory_space=pltpu.VMEM)


def split(x):
    high = x.astype(jnp.bfloat16)
    return high, (x - high.astype(jnp.float32)).astype(jnp.bfloat16)


def dot3(left, right, dims):
    (lh, ll), (rh, rl) = left, right
    mul = functools.partial(
        lax.dot_general, dimension_numbers=(dims, ((), ())), preferred_element_type=jnp.float32
    )
    return mul(lh, rh) + (mul(lh, rl) + mul(ll, rh))


def pack_tile(eof_ref, dir_ref, ke_ref, kn_ref, wet_ref, base_ref, frac_ref, rinv_ref, out_ref):
    levels = dir_ref.shape[0]
    zeros = jnp.zeros((PAD - levels - 3, LANES), jnp.float32)
    eof = eof_ref[...]
    for row in range(ROWS):
        out_ref[row, :levels, :] = jnp.dot(
            eof, dir_ref[:, row, :], precision=HIGHEST, preferred_element_type=jnp.float32
        )
        out_ref[row, levels : levels + 1, :] = ke_ref[row : row + 1, :]
        out_ref[row, levels + 1 : levels + 2, :] = kn_ref[row : row + 1, :]
        out_ref[row, levels + 2 : levels + 3, :] = wet_ref[row : row + 1, :].astype(jnp.float32)
        out_ref[row, levels + 3 :, :] = zeros
    for half in range(2):
        cut = slice(half * LANES, (half + 1) * LANES)
        out_ref[ROWS + half, :levels, :] = rinv_ref[:, cut]
        out_ref[ROWS + half, levels : levels + 1, :] = base_ref[:, cut].astype(jnp.float32)
        out_ref[ROWS + half, levels + 1 : levels + 3, :] = frac_ref[:, cut]
        out_ref[ROWS + half, levels + 3 :, :] = zeros


def pack_columns(flags, own_ref, ra_ref, rb_ref, ns_ref, pa_ref, pb_ref):
    lat_even, lon_even, is_top = flags[0] == 1, flags[1] == 1, flags[2] == 1

    @pl.when(lat_even)
    def _():
        ns_ref[0] = ra_ref[...]
        ns_ref[1] = rb_ref[...]

    @pl.when(jnp.logical_not(lat_even))
    def _():
        ns_ref[0] = rb_ref[...]
        ns_ref[1] = ra_ref[...]

    @pl.when(is_top)
    def _():
        first = lax.broadcasted_iota(jnp.int32, (LANES, LANES), 0)
        second = lax.broadcasted_iota(jnp.int32, (LANES, LANES), 1)
        flip = jnp.where(first + second == LANES - 1, 1.0, 0.0).astype(jnp.float32)
        for row in range(ROWS):
            ns_ref[0, row] = jnp.dot(
                rb_ref[ROWS - 1 - row], flip, precision=HIGHEST, preferred_element_type=jnp.float32
            )

    lane = lax.broadcasted_iota(jnp.int32, (8, LANES), 1)

    def one(step, _):
        cut = pl.ds(pl.multiple_of(step * 8, 8), 8)
        for group in range(2):
            west = jnp.zeros((8, LANES), jnp.float32)
            east = jnp.zeros((8, LANES), jnp.float32)
            for slot in range(SLOTS):
                index = group * SLOTS + slot
                if index < ROWS:
                    tile = ns_ref[1, index, cut, :]
                elif index < 2 * ROWS:
                    tile = own_ref[index - ROWS, cut, :]
                else:
                    tile = ns_ref[0, index - 2 * ROWS, cut, :]
                start = HALO * slot
                here = (lane >= start) & (lane < start + HALO)
                west = jnp.where(here, pltpu.roll(tile, start, 1) if start else tile, west)
                east = jnp.where(here, pltpu.roll(tile, (start + HALO) % LANES, 1), east)
            pa_ref[group, cut, :] = jnp.where(lon_even, east, west)
            pb_ref[group, cut, :] = jnp.where(lon_even, west, east)
        return 0

    lax.fori_loop(0, PAD // 8, one, 0)
    for half in range(2):
        for ref in (pa_ref, pb_ref):
            ref[2 + 2 * SOUTH + half] = ns_ref[1, ROWS + half]
            ref[2 + 2 * OWN + half] = own_ref[ROWS + half]
            ref[2 + 2 * NORTH + half] = ns_ref[0, ROWS + half]


def diffuse_row(src, dst, coef, index, cut):
    centre = src[index, cut, :]
    width = centre.shape[1]
    wide = lambda k: jnp.broadcast_to(coef[k, pl.ds(index, 1), :], centre.shape)
    out = centre * wide(0)
    out = out + wide(1) * pltpu.roll(centre, width - 1, 1)
    out = out + wide(2) * pltpu.roll(centre, 1, 1)
    out = out + wide(3) * src[index + 1, cut, :]
    out = out + wide(4) * src[index - 1, cut, :]
    dst[index, cut, :] = out


def diffuse_all(one, two, coef, low, high):
    def body(step, _):
        cut = pl.ds(pl.multiple_of(step * 8, 8), 8)
        for src, dst, trim in ((one, two, 0), (two, one, 1), (one, two, 2)):
            for index in range(low + trim, high - trim):
                diffuse_row(src, dst, coef, index, cut)
        return 0

    lax.fori_loop(0, PAD // 8, body, 0)


def local_image(
    flags,
    own_ref,
    ns_ref,
    qa_ref,
    qb_ref,
    dir_ref,
    res_ref,
    eoft_ref,
    img_ref,
    part_ref,
    field,
    other,
    adj,
    coef,
    obs,
):
    lon_even, is_top = flags[1] == 1, flags[2] == 1
    levels = dir_ref.shape[0]
    width = 2 * LANES
    lane = lax.broadcasted_iota(jnp.int32, (8, LANES), 1)

    def unpack(step, _):
        cut = pl.ds(pl.multiple_of(step * 8, 8), 8)
        for group in range(2):
            first, second = qa_ref[group, cut, :], qb_ref[group, cut, :]
            east = jnp.where(lon_even, first, second)
            west = jnp.where(lon_even, second, first)
            for slot in range(SLOTS):
                index = group * SLOTS + slot
                if index < ROWS:
                    tile = ns_ref[1, index, cut, :]
                elif index < 2 * ROWS:
                    tile = own_ref[index - ROWS, cut, :]
                else:
                    tile = ns_ref[0, index - 2 * ROWS, cut, :]
                start = HALO * slot
                from_east = pltpu.roll(east, (LANES - start) % LANES, 1) if start else east
                from_west = pltpu.roll(west, (LANES - HALO - start) % LANES, 1)
                halo = jnp.where(
                    lane < HALO, from_east, jnp.where(lane >= LANES - HALO, from_west, 0.0)
                )
                field[index, cut, :LANES] = tile
                field[index, cut, LANES:] = halo
        return 0

    lax.fori_loop(0, PAD // 8, unpack, 0)

    ke, kn, wet = field[:, levels, :], field[:, levels + 1, :], field[:, levels + 2, :]
    row = lax.broadcasted_iota(jnp.int32, (BAND, width), 0)
    up = lambda x: jnp.concatenate([x[1:], x[:1]], 0)
    down = lambda x: jnp.concatenate([x[-1:], x[:-1]], 0)
    right = lambda x: pltpu.roll(x, width - 1, 1)
    left = lambda x: pltpu.roll(x, 1, 1)
    seam = 2 * ROWS - 1
    top = jnp.where(is_top, 1, 0)
    ke = jnp.where((row > seam) & (top == 1), right(ke), ke)
    kn_up = up(kn)
    kn = jnp.where(
        top == 1, jnp.where(row > seam, kn_up, jnp.where(row == seam, 0.5 * (kn + kn_up), kn)), kn
    )
    east_face = ke * wet * right(wet)
    north_face = kn * wet * up(wet)
    west_face, south_face = left(east_face), down(north_face)
    coef[0] = 1.0 - east_face - west_face - north_face - south_face
    coef[1] = east_face
    coef[2] = west_face
    coef[3] = north_face
    coef[4] = south_face

    diffuse_all(field, other, coef, 2, BAND - 2)
    physical = other

    keep = lax.broadcasted_iota(jnp.int32, (PAD, LANES), 0) < levels
    for band in range(3):
        for half in range(2):
            cut = slice(half * LANES, (half + 1) * LANES)
            slot = 2 + 2 * band + half
            first, second = qa_ref[slot], qb_ref[slot]
            mid = (ns_ref[1, ROWS + half], own_ref[ROWS + half], ns_ref[0, ROWS + half])[band]
            obs[0, band, :, cut] = jnp.where(lon_even, second, first)
            obs[1, band, :, cut] = mid
            obs[2, band, :, cut] = jnp.where(lon_even, first, second)
    adj[...] = jnp.zeros(adj.shape, jnp.float32)
    cells = lax.broadcasted_iota(jnp.int32, (width, width), 0)
    keep = lax.broadcasted_iota(jnp.int32, (PAD, width), 0) < levels
    spans = ((4, 9, 5), (8, 17, 8), (16, 20, 16))
    ends = (9, 17, 19)
    for band in range(3):
        begin, stop, adj_begin = spans[band]
        adj_stop = ends[band]
        lhs = split(physical[begin:stop].reshape((stop - begin) * PAD, width))

        def tile_of(t, _, band=band, lhs=lhs, begin=begin, stop=stop, lo=adj_begin, hi=adj_stop):
            base = obs[t, band, levels : levels + 1, :].astype(jnp.int32)
            p = obs[t, band, levels + 1 : levels + 2, :]
            q = obs[t, band, levels + 2 : levels + 3, :]
            j, i = base >> 7, base & (LANES - 1)
            rows, cols = j + ROWS * band, i
            a0, a1, b0, b1 = 1.0 - p, p, 1.0 - q, q
            if band == NORTH:
                turned = top == 1
                rows = jnp.where(turned, 22 - j, rows)
                cols = jnp.where(turned, 126 - i, cols)
                a0, a1 = jnp.where(turned, a1, a0), jnp.where(turned, a0, a1)
                b0, b1 = jnp.where(turned, b1, b0), jnp.where(turned, b0, b1)
            near = jnp.where(t == 1, 1, jnp.where(t == 0, jnp.where(cols >= 64, 1, 0), jnp.where(cols < 64, 1, 0)))
            b0, b1 = jnp.where(near == 1, b0, 0.0), jnp.where(near == 1, b1, 0.0)
            lane0 = (cols + jnp.where(t == 1, 0, LANES)) & (width - 1)
            lane1 = (lane0 + 1) & (width - 1)
            weight = jnp.where(cells == lane0, b0, jnp.where(cells == lane1, b1, 0.0))
            rhs = split(weight)
            taken = dot3(lhs, rhs, ((1,), (0,)))
            row_weight = [
                jnp.where(rows == r, a0, jnp.where(rows == r - 1, a1, 0.0))
                for r in range(begin, stop)
            ]
            profile = jnp.zeros((PAD, width), jnp.float32)
            for k in range(stop - begin):
                profile = profile + row_weight[k] * taken[k * PAD : (k + 1) * PAD]
            weighted = jnp.where(keep, obs[t, band] * profile, 0.0)
            spread = jnp.concatenate(
                [row_weight[r - begin] * weighted for r in range(lo, hi)], 0
            )
            added = dot3(split(spread), rhs, ((1,), (1,)))
            adj[lo:hi] += added.reshape(hi - lo, PAD, width)
            return 0

        lax.fori_loop(0, 3, tile_of, 0)

    diffuse_all(adj, other, coef, 6, BAND - 6)

    eoft = eoft_ref[...]
    rr = dim = rim = imim = jnp.zeros((levels, LANES), jnp.float32)
    for r in range(ROWS):
        back = jnp.dot(
            eoft, other[ROWS + r, :levels, :LANES], precision=HIGHEST, preferred_element_type=jnp.float32
        )
        d, res = dir_ref[:, r, :], res_ref[:, r, :]
        image = d + back
        img_ref[:, r, :] = image
        rr, dim, rim, imim = rr + res * res, dim + d * image, rim + res * image, imim + image * image
    lane = lax.broadcasted_iota(jnp.int32, part_ref.shape, 1)
    out = jnp.zeros(part_ref.shape, jnp.float32)
    for k, value in enumerate((rr, dim, rim, imim)):
        out = jnp.where(lane == k, jnp.sum(value), out)
    part_ref[...] = out


def finish(part_ref, img_ref, res_ref, dir_ref, new_res_ref, new_dir_ref, step_ref):
    total = jnp.sum(part_ref[...], axis=0, keepdims=True)
    lane = lax.broadcasted_iota(jnp.int32, total.shape, 1)
    rr, dim, rim, imim = (
        jnp.sum(jnp.where(lane == k, total, 0.0), axis=1, keepdims=True) for k in range(4)
    )
    step = rr / dim
    new_norm = rr + step * (step * imim - 2.0 * rim)
    beta = new_norm / rr
    step_ref[...] = step
    new_res = res_ref[...] - step[None] * img_ref[...]
    new_res_ref[...] = new_res
    new_dir_ref[...] = new_res + beta[None] * dir_ref[...]


def lat_pairs(lon_count, lat_count):
    index = lambda lon, lat: lon * lat_count + lat
    first, second = [], []
    for lon in range(lon_count):
        for lat in range(lat_count):
            first.append((index(lon, lat), index(lon, lat ^ 1)))
            other = lat + 1 if lat % 2 else lat - 1
            if other == lat_count:
                second.append((index(lon, lat), index(lon_count - 1 - lon, lat)))
            elif other >= 0:
                second.append((index(lon, lat), index(lon, other)))
    return first, second


def lon_pairs(lon_count):
    first = [(lon, lon ^ 1) for lon in range(lon_count)]
    second = [(lon, (lon + 1 if lon % 2 else lon - 1) % lon_count) for lon in range(lon_count)]
    return first, second


def per_device(
    direction, residual, eof_basis, kappa_east, kappa_north, wet_mask, obs_base, obs_frac, obs_rinv
):
    levels = direction.shape[0]
    shape = functools.partial(jax.ShapeDtypeStruct, dtype=jnp.float32)
    lon_count, lat_count = lax.axis_size("lon"), lax.axis_size("lat")
    lon, lat = lax.axis_index("lon"), lax.axis_index("lat")
    flags = jnp.stack([1 - lat % 2, 1 - lon % 2, (lat == lat_count - 1).astype(jnp.int32)])
    flags = flags.astype(jnp.int32)
    own = pl.pallas_call(
        pack_tile, out_shape=shape((ROWS + 2, PAD, LANES)), in_specs=[VMEM] * 8, out_specs=VMEM
    )(
        eof_basis,
        direction,
        kappa_east,
        kappa_north,
        wet_mask,
        obs_base.reshape(1, -1),
        obs_frac.reshape(2, -1),
        obs_rinv.reshape(levels, -1),
    )
    first, second = lat_pairs(lon_count, lat_count)
    lat_b = lax.ppermute(own, ("lon", "lat"), second)
    lat_a = lax.ppermute(own, ("lon", "lat"), first)
    north_south, to_a, to_b = pl.pallas_call(
        pack_columns,
        out_shape=(shape((2, ROWS + 2, PAD, LANES)), shape((8, PAD, LANES)), shape((8, PAD, LANES))),
        in_specs=[SMEM] + [VMEM] * 3,
        out_specs=(VMEM,) * 3,
    )(flags, own, lat_a, lat_b)
    first, second = lon_pairs(lon_count)
    lon_b = lax.ppermute(to_b, "lon", second)
    lon_a = lax.ppermute(to_a, "lon", first)
    image, part = pl.pallas_call(
        local_image,
        out_shape=(shape(direction.shape), shape((lon_count, LANES))),
        in_specs=[SMEM] + [VMEM] * 7,
        out_specs=(VMEM,) * 2,
        scratch_shapes=[
            pltpu.VMEM((BAND, PAD, 2 * LANES), jnp.float32),
            pltpu.VMEM((BAND, PAD, 2 * LANES), jnp.float32),
            pltpu.VMEM((BAND, PAD, 2 * LANES), jnp.float32),
            pltpu.VMEM((5, BAND, 2 * LANES), jnp.float32),
            pltpu.VMEM((3, 3, PAD, 2 * LANES), jnp.float32),
        ],
    )(flags, own, north_south, lon_a, lon_b, direction, residual, eof_basis.T)
    part = lax.all_to_all(part, "lon", 0, 0, tiled=True)
    part = jnp.broadcast_to(jnp.sum(part, axis=0, keepdims=True), (lat_count, LANES))
    part = lax.all_to_all(part, "lat", 0, 0, tiled=True)
    new_residual, new_direction, step_length = pl.pallas_call(
        finish,
        out_shape=(shape(direction.shape), shape(direction.shape), shape((1, 1))),
        in_specs=[VMEM] * 4,
        out_specs=(VMEM,) * 3,
    )(part, image, residual, direction)
    return new_residual, new_direction, step_length.reshape(())


def solution(mesh):
    return jax.shard_map(
        per_device,
        mesh=mesh,
        in_specs=(
            P(None, "lat", "lon"),
            P(None, "lat", "lon"),
            P(),
            P("lat", "lon"),
            P("lat", "lon"),
            P("lat", "lon"),
            P("lat", "lon", None),
            P(None, "lat", "lon", None),
            P(None, "lat", "lon", None),
        ),
        out_specs=(P(None, "lat", "lon"), P(None, "lat", "lon"), P()),
        check_vma=False,
    )
```

time: 575 us -> 105 us (0.18)
  starting transfers between devices: 230 us -> 15.8 us
  blocking collectives: 206 us -> 43.8 us
  waiting for transfers between devices: 97.3 us -> 10.4 us
  Pallas kernels: 0 us -> 28.4 us
  other arithmetic: 19 us -> 0.7 us
  local copies, waits for them, and re-layouts: 13.5 us -> 5.1 us
    ppermute x69 -> x4, starting transfers between devices: 230 us -> 15.8 us  [the longest x1 8.88 us: per_device(): lon_a = lax.ppermute(to_a, 'lon', first)]
    psum x2 -> x0, blocking collectives: 206 us -> none  [the longest x1 106 us: per_device(): old_norm = lax.psum(jnp.sum(residual * residual), ('lon', 'lat'))]
    ppermute x69 -> x4, waiting for transfers between devices: 97.3 us -> 10.4 us  [the longest x1 6.24 us: per_device(): lon_b = lax.ppermute(to_b, 'lon', second)]
    all_to_all x0 -> x2, blocking collectives: none -> 43.8 us  [the longest x1 29.1 us: per_device(): part = lax.all_to_all(part, 'lat', 0, 0, tiled=True)]
    pallas_call x0 -> x4, Pallas kernels: none -> 28.4 us  [the longest x1 20.5 us: per_device(): pl.pallas_call(local_image, out_shape=(shape(direction.shape), shape((lon...]
    scatter-add x11 -> x0, other arithmetic: 8.73 us -> none  [the longest x4 8.57 us: per_device(): spread.at[:, corner_index[corner]]]
  transfers between devices with their start and end apart: 69 -> 4, of which waited for: 32 -> 2; matrix products, arithmetic and copies ran while one was open for 2% -> 1% of each run, Pallas kernels for 0% -> 0%
where the time goes in v1:
time: 105 us
  blocking collectives  43.8 us (42%)
  Pallas kernels  28.4 us (27%)
  starting transfers between devices  15.8 us (15%)
  waiting for transfers between devices  10.4 us (10%)
  local copies, waits for them, and re-layouts  5.1 us (5%)
    all_to_all x1, blocking collectives, per_device(): part = lax.all_to_all(part, 'lat', 0, 0, tiled=True)  29.1 us
    pallas_call x1, Pallas kernels, per_device(): pl.pallas_call(local_image, out_shape=(shape(direction.shape), shape((lon...  20.5 us
    all_to_all x1, blocking collectives, per_device(): part = lax.all_to_all(part, 'lon', 0, 0, tiled=True)  14.8 us
    ppermute x1, starting transfers between devices, per_device(): lon_a = lax.ppermute(to_a, 'lon', first)  8.88 us
    ppermute x1, waiting for transfers between devices, per_device(): lon_b = lax.ppermute(to_b, 'lon', second)  6.24 us
    unnamed x15, local copies, waits for them, and re-layouts  5.09 us
    ppermute x1, starting transfers between devices, per_device(): lat_a = lax.ppermute(own, ('lon', 'lat'), first)  4.35 us
    ppermute x1, waiting for transfers between devices, per_device(): lat_a = lax.ppermute(own, ('lon', 'lat'), first)  4.17 us
  transfers between devices with their start and end apart: 4, of which 2 were waited for; matrix products, arithmetic and copies ran while one was open for 1% of the time, Pallas kernels for 0%

profile of v1, /device:TPU:1, one launch (start us, length us, event | category | flops | bytes accessed | tf_op | source)
XLA Modules:
  0.0 105.0 jit_solution(3218914726162744913)
XLA Ops:
  0.6 0.0 copy-start.5
  0.6 1.5 %copy.19 = f32[75,1,1,256]{3,0,1,2:T(8,128)} copy(f32[75,1,1,256]{3,2,1,0:T(1,128)} %param.17) | data formatting | bytes 153600
  2.2 0.0 copy-done.5
  2.2 0.6 copy.20
  2.8 2.3 %shard_map.112.own_ref = f32[10,80,128]{2,1,0:T(8,128)} custom-call(f32[75,75]{1,0:T(8,128)} %eof_ref.1, f32[75,8,128]{2,1,0:T(8,128)} %dir_ref.5, f32[8,128]{1,0:T(8,128)} %ke_ref.1, f32[8,128]{1,0:T(8,128)} %kn_ref.1, s32[8,128]{1,0:T(8,128)} %wet_ref.1, s32[1,256]{1,0:T(1,128)} %bitcast.21, f32[2,256]{1,0:T(2,128)} %bitcast.20, f32[75,256]{1,0:T(8,128)} %bitcast.16), custom_call_target="tpu_custom_call" | custom-call | tf_op jit(solution)/shard_map/pallas_call | solution.py:326
  5.0 4.4 %collective-permute-start = (f32[10,80,128]{2,1,0:T(8,128)}, f32[10,80,128]{2,1,0:T(8,128)S(1)}, u32[]{:S(2)}, u32[]{:S(2)}) collective-permute-start(f32[10,80,128]{2,1,0:T(8,128)} %shard_map.112.own_ref), channel_id=1, source_target_pairs={{0,1},{1,0},{2,3},{3,2},{4,5},{5,4},{6,7},{7,6},{8,9},{9,8},{10,11... | collective-permute-start | bytes 1228808 | tf_op jit(solution)/shard_map/ppermute | solution.py:340
  9.4 0.7 collective-permute-start.1
  10.1 0.7 pad_add_fusion.flags
  10.8 0.0 copy-start.4
  10.8 4.2 %collective-permute-done.ra_ref = f32[10,80,128]{2,1,0:T(8,128)S(1)} collective-permute-done((f32[10,80,128]{2,1,0:T(8,128)}, f32[10,80,128]{2,1,0:T(8,128)S(1)}, u32[]{:S(2)}, u32[]{:S(2)}) %collective-permute-start) | collective-permute-done | bytes 409632 | tf_op jit(solution)/shard_map/ppermute | solution.py:340
  14.9 0.0 copy-start
  14.9 0.0 collective-permute-done.1.rb_ref
  14.9 0.8 copy-done
  15.7 0.0 copy-start.1
  15.7 0.7 copy-done.1
  16.5 3.5 %shard_map.113 = (f32[2,10,80,128]{3,2,1,0:T(8,128)}, f32[8,80,128]{2,1,0:T(8,128)}, f32[8,80,128]{2,1,0:T(8,128)}) custom-call(s32[3]{0:T(128)} %pad_add_fusion.flags, f32[10,80,128]{2,1,0:T(8,128)} %shard_map.112.own_ref, f32[10,80,128]{2,1,0:T(8,128)} %copy-done, f32[10,80,128]{2,1,0:T(8,128)} %copy-done.1), custom_call_target="tpu_custom_call" | custom-call | tf_op jit(solution)/shard_map/pallas_call | solution.py:341
  20.0 8.9 %collective-permute-start.2 = (f32[8,80,128]{2,1,0:T(8,128)}, f32[8,80,128]{2,1,0:T(8,128)S(1)}, u32[]{:S(2)}, u32[]{:S(2)}) collective-permute-start(f32[8,80,128]{2,1,0:T(8,128)} %get-tuple-element.12), channel_id=1, source_target_pairs={{0,16},{16,0},{32,48},{48,32},{64,80},{80,64},{96,112},{112,96},{1... | collective-permute-start | bytes 983048 | tf_op jit(solution)/shard_map/ppermute | solution.py:349
  28.9 1.9 %collective-permute-start.3 = (f32[8,80,128]{2,1,0:T(8,128)}, f32[8,80,128]{2,1,0:T(8,128)S(1)}, u32[]{:S(2)}, u32[]{:S(2)}) collective-permute-start(f32[8,80,128]{2,1,0:T(8,128)} %get-tuple-element.13), channel_id=1, source_target_pairs={{0,496},{16,32},{32,16},{48,64},{64,48},{80,96},{96,80},{112,128},... | collective-permute-start | bytes 983048 | tf_op jit(solution)/shard_map/ppermute | solution.py:348
  30.8 0.0 copy-done.4
  30.8 0.7 copy.13
  31.5 0.0 collective-permute-done.2.qa_ref
  31.5 0.0 copy-start.2
  31.6 6.2 %collective-permute-done.3.qb_ref = f32[8,80,128]{2,1,0:T(8,128)S(1)} collective-permute-done((f32[8,80,128]{2,1,0:T(8,128)}, f32[8,80,128]{2,1,0:T(8,128)S(1)}, u32[]{:S(2)}, u32[]{:S(2)}) %collective-permute-start.3) | collective-permute-done | bytes 327712 | tf_op jit(solution)/shard_map/ppermute | solution.py:348
  37.8 0.0 copy-start.3
  37.8 0.0 copy-done.2
  37.8 0.7 copy-done.3
  38.5 20.5 %shard_map.114 = (f32[75,8,128]{2,1,0:T(8,128)}, f32[32,128]{1,0:T(8,128)}) custom-call(s32[3]{0:T(128)} %pad_add_fusion.flags, f32[10,80,128]{2,1,0:T(8,128)} %shard_map.112.own_ref, f32[2,10,80,128]{3,2,1,0:T(8,128)} %get-tuple-element.11.ns_ref, f32[8,80,128]{2,1,0:T(8,128)} %copy-done.2, f32[8,80,128]{2,1,0:T(8,128)} %copy-done.3, ...), custom_call_target="tpu_custom_call" | custom-call | tf_op jit(solution)/shard_map/pallas_call | solution.py:350
  59.0 14.8 %all_to_all.17 = f32[32,1,128]{2,1,0:T(1,128)S(1)} all-to-all(f32[32,1,128]{2,1,0:T(1,128)} %bitcast.19), channel_id=1, replica_groups=mesh['lon'=32,'lat'=16] {'lon'}, dimensions={0} | all-to-all | bytes 32768 | tf_op jit(solution)/shard_map/all_to_all | solution.py:363
  73.8 0.1 reduce_sum.9
  73.8 29.1 %all_to_all.18 = f32[16,1,128]{2,1,0:T(1,128)} all-to-all(f32[16,1,128]{2,1,0:T(1,128)S(1)} %broadcast_in_dim.2), channel_id=1, replica_groups=mesh['lon'=32,'lat'=16] {'lat'}, dimensions={0} | all-to-all | bytes 16384 | tf_op jit(solution)/shard_map/all_to_all | solution.py:365
  102.9 2.1 %shard_map.115 = (f32[75,8,128]{2,1,0:T(8,128)}, f32[75,8,128]{2,1,0:T(8,128)}, f32[1,1]{1,0:T(1,128)}) custom-call(f32[16,128]{1,0:T(8,128)} %bitcast.18, f32[75,8,128]{2,1,0:T(8,128)} %get-tuple-element.15.img_ref, f32[75,8,128]{2,1,0:T(8,128)} %res_ref.3, f32[75,8,128]{2,1,0:T(8,128)} %dir_ref.5), custom_call_target="tpu_custom_call" | custom-call | tf_op jit(solution)/shard_map/pallas_call | solution.py:366
  (1 shorter events, 0.0 us)
Async XLA Ops:
  0.6 1.5 %copy-start.5 = (f32[2,1,1,256]{3,2,1,0:T(1,128)S(1)}, f32[2,1,1,256]{3,2,1,0:T(1,128)}, u32[]{:S(2)}) copy-start(f32[2,1,1,256]{3,2,1,0:T(1,128)} %param.16) | copy-start | bytes 6148
  5.0 9.9 %collective-permute-start = (f32[10,80,128]{2,1,0:T(8,128)}, f32[10,80,128]{2,1,0:T(8,128)S(1)}, u32[]{:S(2)}, u32[]{:S(2)}) collective-permute-start(f32[10,80,128]{2,1,0:T(8,128)} %shard_map.112.own_ref), channel_id=1, source_target_pairs={{0,1},{1,0},{2,3},{3,2},{4,5},{5,4},{6,7},{7,6},{8,9},{9,8},{10,11... | collective-permute-start | bytes 1228808 | tf_op jit(solution)/shard_map/ppermute | solution.py:340
  9.4 5.5 %collective-permute-start.1 = (f32[10,80,128]{2,1,0:T(8,128)}, f32[10,80,128]{2,1,0:T(8,128)S(1)}, u32[]{:S(2)}, u32[]{:S(2)}) collective-permute-start(f32[10,80,128]{2,1,0:T(8,128)} %shard_map.112.own_ref), channel_id=1, source_target_pairs={{1,2},{2,1},{3,4},{4,3},{5,6},{6,5},{7,8},{8,7},{9,10},{10,9},{11,... | collective-permute-start | bytes 1228808 | tf_op jit(solution)/shard_map/ppermute | solution.py:339
  10.8 20.1 %copy-start.4 = (f32[75,75]{1,0:T(8,128)S(1)}, f32[75,75]{1,0:T(8,128)}, u32[]{:S(2)}) copy-start(f32[75,75]{1,0:T(8,128)} %eof_ref.1) | copy-start | bytes 67504
  14.9 0.8 copy-start
  15.7 0.7 copy-start.1
  20.0 11.5 %collective-permute-start.2 = (f32[8,80,128]{2,1,0:T(8,128)}, f32[8,80,128]{2,1,0:T(8,128)S(1)}, u32[]{:S(2)}, u32[]{:S(2)}) collective-permute-start(f32[8,80,128]{2,1,0:T(8,128)} %get-tuple-element.12), channel_id=1, source_target_pairs={{0,16},{16,0},{32,48},{48,32},{64,80},{80,64},{96,112},{112,96},{1... | collective-permute-start | bytes 983048 | tf_op jit(solution)/shard_map/ppermute | solution.py:349
  28.9 8.9 %collective-permute-start.3 = (f32[8,80,128]{2,1,0:T(8,128)}, f32[8,80,128]{2,1,0:T(8,128)S(1)}, u32[]{:S(2)}, u32[]{:S(2)}) collective-permute-start(f32[8,80,128]{2,1,0:T(8,128)} %get-tuple-element.13), channel_id=1, source_target_pairs={{0,496},{16,32},{32,16},{48,64},{64,48},{80,96},{96,80},{112,128},... | collective-permute-start | bytes 983048 | tf_op jit(solution)/shard_map/ppermute | solution.py:348
  31.5 6.2 %copy-start.2 = (f32[8,80,128]{2,1,0:T(8,128)}, f32[8,80,128]{2,1,0:T(8,128)S(1)}, u32[]{:S(2)}) copy-start(f32[8,80,128]{2,1,0:T(8,128)S(1)} %collective-permute-done.2.qa_ref) | copy-start | bytes 983044
  37.8 0.7 copy-start.3

commit v2 on v1

--- a/solution.py
+++ b/solution.py
@@ -6,6 +6,7 @@
 from jax.experimental import pallas as pl
 from jax.experimental.pallas import tpu as pltpu
 from jax.sharding import PartitionSpec as P
+
 
 HIGHEST = lax.Precision.HIGHEST
 LANES = 128
@@ -18,6 +19,14 @@
 
 SMEM = pl.BlockSpec(memory_space=pltpu.SMEM)
 VMEM = pl.BlockSpec(memory_space=pltpu.VMEM)
+
+
+def grant(mebibytes):
+    return pltpu.CompilerParams(vmem_limit_bytes=mebibytes << 20)
+
+
+def near(x):
+    return pltpu.with_memory_space_constraint(x, pltpu.VMEM)
 
 
 def split(x):
@@ -47,9 +56,11 @@
         out_ref[row, levels + 3 :, :] = zeros
     for half in range(2):
         cut = slice(half * LANES, (half + 1) * LANES)
-        out_ref[ROWS + half, :levels, :] = rinv_ref[:, cut]
+        for level in range(levels):
+            out_ref[ROWS + half, level : level + 1, :] = rinv_ref[level, :, cut]
         out_ref[ROWS + half, levels : levels + 1, :] = base_ref[:, cut].astype(jnp.float32)
-        out_ref[ROWS + half, levels + 1 : levels + 3, :] = frac_ref[:, cut]
+        out_ref[ROWS + half, levels + 1 : levels + 2, :] = frac_ref[0, :, cut]
+        out_ref[ROWS + half, levels + 2 : levels + 3, :] = frac_ref[1, :, cut]
         out_ref[ROWS + half, levels + 3 :, :] = zeros
 
 
@@ -319,12 +330,15 @@
 ):
     levels = direction.shape[0]
     shape = functools.partial(jax.ShapeDtypeStruct, dtype=jnp.float32)
+    local = functools.partial(pltpu.VMEM, dtype=jnp.float32)
     lon_count, lat_count = lax.axis_size("lon"), lax.axis_size("lat")
     lon, lat = lax.axis_index("lon"), lax.axis_index("lat")
     flags = jnp.stack([1 - lat % 2, 1 - lon % 2, (lat == lat_count - 1).astype(jnp.int32)])
     flags = flags.astype(jnp.int32)
+    direction, residual = near(direction), near(residual)
     own = pl.pallas_call(
-        pack_tile, out_shape=shape((ROWS + 2, PAD, LANES)), in_specs=[VMEM] * 8, out_specs=VMEM
+        pack_tile, out_shape=local((ROWS + 2, PAD, LANES)), in_specs=[VMEM] * 8, out_specs=VMEM,
+        compiler_params=grant(8),
     )(
         eof_basis,
         direction,
@@ -332,26 +346,29 @@
         kappa_north,
         wet_mask,
         obs_base.reshape(1, -1),
-        obs_frac.reshape(2, -1),
-        obs_rinv.reshape(levels, -1),
+        obs_frac.reshape(2, 1, -1),
+        obs_rinv.reshape(levels, 1, -1),
     )
     first, second = lat_pairs(lon_count, lat_count)
     lat_b = lax.ppermute(own, ("lon", "lat"), second)
     lat_a = lax.ppermute(own, ("lon", "lat"), first)
+    own, lat_a, lat_b = near(own), near(lat_a), near(lat_b)
     north_south, to_a, to_b = pl.pallas_call(
         pack_columns,
-        out_shape=(shape((2, ROWS + 2, PAD, LANES)), shape((8, PAD, LANES)), shape((8, PAD, LANES))),
+        out_shape=(local((2, ROWS + 2, PAD, LANES)), local((8, PAD, LANES)), local((8, PAD, LANES))),
         in_specs=[SMEM] + [VMEM] * 3,
         out_specs=(VMEM,) * 3,
+        compiler_params=grant(8),
     )(flags, own, lat_a, lat_b)
     first, second = lon_pairs(lon_count)
     lon_b = lax.ppermute(to_b, "lon", second)
     lon_a = lax.ppermute(to_a, "lon", first)
     image, part = pl.pallas_call(
         local_image,
-        out_shape=(shape(direction.shape), shape((lon_count, LANES))),
+        out_shape=(local(direction.shape), local((lon_count, LANES))),
         in_specs=[SMEM] + [VMEM] * 7,
         out_specs=(VMEM,) * 2,
+        compiler_params=grant(28),
         scratch_shapes=[
             pltpu.VMEM((BAND, PAD, 2 * LANES), jnp.float32),
             pltpu.VMEM((BAND, PAD, 2 * LANES), jnp.float32),
@@ -359,7 +376,7 @@
             pltpu.VMEM((5, BAND, 2 * LANES), jnp.float32),
             pltpu.VMEM((3, 3, PAD, 2 * LANES), jnp.float32),
         ],
-    )(flags, own, north_south, lon_a, lon_b, direction, residual, eof_basis.T)
+    )(flags, own, near(north_south), near(lon_a), near(lon_b), direction, residual, near(eof_basis.T))
     part = lax.all_to_all(part, "lon", 0, 0, tiled=True)
     part = jnp.broadcast_to(jnp.sum(part, axis=0, keepdims=True), (lat_count, LANES))
     part = lax.all_to_all(part, "lat", 0, 0, tiled=True)
@@ -368,7 +385,8 @@
         out_shape=(shape(direction.shape), shape(direction.shape), shape((1, 1))),
         in_specs=[VMEM] * 4,
         out_specs=(VMEM,) * 3,
-    )(part, image, residual, direction)
+        compiler_params=grant(8),
+    )(near(part), near(image), residual, direction)
     return new_residual, new_direction, step_length.reshape(())
 
 

time: 105 us -> 100 us (0.952)
  Pallas kernels: 28.4 us -> 22.1 us
    pallas_call x3, Pallas kernels: 26.3 us -> 21.1 us  [the longest x1 18.8 us: per_device(): pl.pallas_call(local_image, out_shape=(local(direction.shape), local((lon...]
    pallas_call x1, Pallas kernels: 2.13 us -> 0.96 us  [per_device(): pl.pallas_call(finish, out_shape=(shape(direction.shape), shape(direction...]
    unnamed x15 -> x23, local copies, waits for them, and re-layouts: 5.09 us -> 5.47 us
  transfers between devices with their start and end apart: 4 -> 4, of which waited for: 2 -> 2; matrix products, arithmetic and copies ran while one was open for 1% -> 0% of each run, Pallas kernels for 0% -> 0%
where the time goes in v2:
time: 100 us; the launch traced here: 99.8 us
  blocking collectives  44.4 us (44%)
  Pallas kernels  22.1 us (22%)
  starting transfers between devices  15.9 us (16%)
  waiting for transfers between devices  11.2 us (11%)
  local copies, waits for them, and re-layouts  5.48 us (5%)
    all_to_all x1, blocking collectives, per_device(): part = lax.all_to_all(part, 'lat', 0, 0, tiled=True)  29.7 us
    pallas_call x1, Pallas kernels, per_device(): pl.pallas_call(local_image, out_shape=(local(direction.shape), local((lon...  18.8 us
    all_to_all x1, blocking collectives, per_device(): part = lax.all_to_all(part, 'lon', 0, 0, tiled=True)  14.6 us
    ppermute x1, starting transfers between devices, per_device(): lon_a = lax.ppermute(to_a, 'lon', first)  8.9 us
    ppermute x1, waiting for transfers between devices, per_device(): lon_b = lax.ppermute(to_b, 'lon', second)  6.65 us
    unnamed x23, local copies, waits for them, and re-layouts  5.47 us
    ppermute x1, waiting for transfers between devices, per_device(): lat_a = lax.ppermute(own, ('lon', 'lat'), first)  4.53 us
    ppermute x1, starting transfers between devices, per_device(): lat_a = lax.ppermute(own, ('lon', 'lat'), first)  4.36 us
  transfers between devices with their start and end apart: 4, of which 2 were waited for; matrix products, arithmetic and copies ran while one was open for 0% of the time, Pallas kernels for 0%

profile of v2, /device:TPU:1, one launch (start us, length us, event | category | flops | bytes accessed | tf_op | source)
XLA Modules:
  0.0 99.8 jit_solution(11637668277131013398)
XLA Ops:
  0.6 0.0 copy-start.6
  0.6 0.0 copy-start.10
  0.7 0.7 copy-done.6
  1.3 0.0 copy-done.10
  1.3 0.0 copy-start
  1.3 1.0 copy-done
  2.3 0.0 copy-start.3
  2.3 0.8 copy-done.3
  3.1 0.9 copy-done.5
  4.0 0.7 copy-done.7
  4.6 0.7 copy-done.8
  5.3 0.7 copy-done.9
  6.0 0.5 shard_map.112.own_ref
  6.5 4.4 %collective-permute-start = (f32[10,80,128]{2,1,0:T(8,128)S(1)}, f32[10,80,128]{2,1,0:T(8,128)S(1)}, u32[]{:S(2)}, u32[]{:S(2)}) collective-permute-start(f32[10,80,128]{2,1,0:T(8,128)S(1)} %shard_map.112.own_ref), channel_id=1, source_target_pairs={{0,1},{1,0},{2,3},{3,2},{4,5},{5,4},{6,7},{7,6},{8,9},{9,8},{10,11... | collective-permute-start | bytes 1228808 | tf_op jit(solution)/shard_map/ppermute | solution.py:354
  10.9 0.7 collective-permute-start.1
  11.6 0.1 pad_add_fusion.flags
  11.7 4.5 %collective-permute-done.ra_ref = f32[10,80,128]{2,1,0:T(8,128)S(1)} collective-permute-done((f32[10,80,128]{2,1,0:T(8,128)S(1)}, f32[10,80,128]{2,1,0:T(8,128)S(1)}, u32[]{:S(2)}, u32[]{:S(2)}) %collective-permute-start) | collective-permute-done | bytes 409632 | tf_op jit(solution)/shard_map/ppermute | solution.py:354
  16.2 0.0 collective-permute-done.1.rb_ref
  16.2 1.8 %shard_map.113 = (f32[2,10,80,128]{3,2,1,0:T(8,128)S(1)}, f32[8,80,128]{2,1,0:T(8,128)S(1)}, f32[8,80,128]{2,1,0:T(8,128)S(1)}) custom-call(s32[3]{0:T(128)S(1)} %pad_add_fusion.flags, f32[10,80,128]{2,1,0:T(8,128)S(1)} %shard_map.112.own_ref, f32[10,80,128]{2,1,0:T(8,128)S(1)} %collective-permute-done.ra_ref, f32[10,80,128]{2,1,0:T(8,128)S(1)} %collective-permute-done.1.rb_ref), custom_call_target="tpu_custom_call" | custom-call | tf_op jit(solution)/shard_map/pallas_call | solution.py:356
  18.0 8.9 %collective-permute-start.2 = (f32[8,80,128]{2,1,0:T(8,128)S(1)}, f32[8,80,128]{2,1,0:T(8,128)S(1)}, u32[]{:S(2)}, u32[]{:S(2)}) collective-permute-start(f32[8,80,128]{2,1,0:T(8,128)S(1)} %get-tuple-element.12), channel_id=1, source_target_pairs={{0,16},{16,0},{32,48},{48,32},{64,80},{80,64},{96,112},{112,96},{1... | collective-permute-start | bytes 983048 | tf_op jit(solution)/shard_map/ppermute | solution.py:365
  26.9 1.9 %collective-permute-start.3 = (f32[8,80,128]{2,1,0:T(8,128)S(1)}, f32[8,80,128]{2,1,0:T(8,128)S(1)}, u32[]{:S(2)}, u32[]{:S(2)}) collective-permute-start(f32[8,80,128]{2,1,0:T(8,128)S(1)} %get-tuple-element.13), channel_id=1, source_target_pairs={{0,496},{16,32},{32,16},{48,64},{64,48},{80,96},{96,80},{112,128},... | collective-permute-start | bytes 983048 | tf_op jit(solution)/shard_map/ppermute | solution.py:364
  28.9 0.0 copy-done.4
  28.9 0.1 copy.13
  29.0 0.0 collective-permute-done.2.qa_ref
  29.0 6.6 %collective-permute-done.3.qb_ref = f32[8,80,128]{2,1,0:T(8,128)S(1)} collective-permute-done((f32[8,80,128]{2,1,0:T(8,128)S(1)}, f32[8,80,128]{2,1,0:T(8,128)S(1)}, u32[]{:S(2)}, u32[]{:S(2)}) %collective-permute-start.3) | collective-permute-done | bytes 327712 | tf_op jit(solution)/shard_map/ppermute | solution.py:364
  35.6 0.0 copy-done.1
  35.6 0.0 copy-done.2
  35.6 18.8 %shard_map.114 = (f32[75,8,128]{2,1,0:T(8,128)S(1)}, f32[32,128]{1,0:T(8,128)S(1)}) custom-call(s32[3]{0:T(128)S(1)} %pad_add_fusion.flags, f32[10,80,128]{2,1,0:T(8,128)S(1)} %shard_map.112.own_ref, f32[2,10,80,128]{3,2,1,0:T(8,128)S(1)} %get-tuple-element.11.ns_ref, f32[8,80,128]{2,1,0:T(8,128)S(1)} %collective-permute-done.2.qa_ref, ...), custom_call_target="tpu_custom_call" | custom-call | tf_op jit(solution)/shard_map/pallas_call | solution.py:366
  54.4 14.6 %all_to_all.17 = f32[32,1,128]{2,1,0:T(1,128)S(1)} all-to-all(f32[32,1,128]{2,1,0:T(1,128)S(1)} %bitcast.15), channel_id=1, replica_groups=mesh['lon'=32,'lat'=16] {'lon'}, dimensions={0} | all-to-all | bytes 32768 | tf_op jit(solution)/shard_map/all_to_all | solution.py:380
  69.1 0.1 reduce_sum.9
  69.1 29.7 %all_to_all.18 = f32[16,1,128]{2,1,0:T(1,128)S(1)} all-to-all(f32[16,1,128]{2,1,0:T(1,128)S(1)} %broadcast_in_dim.2), channel_id=1, replica_groups=mesh['lon'=32,'lat'=16] {'lat'}, dimensions={0} | all-to-all | bytes 16384 | tf_op jit(solution)/shard_map/all_to_all | solution.py:382
  98.9 1.0 shard_map.115
  (8 shorter events, 0.0 us)
Async XLA Ops:
  0.6 0.7 copy-start.6
  0.6 0.7 copy-start.10
  1.3 1.0 copy-start
  2.3 0.8 copy-start.3
  3.1 0.9 copy-start.5
  4.0 0.7 copy-start.7
  4.6 0.7 copy-start.8
  5.3 0.7 copy-start.9
  6.5 9.7 %collective-permute-start = (f32[10,80,128]{2,1,0:T(8,128)S(1)}, f32[10,80,128]{2,1,0:T(8,128)S(1)}, u32[]{:S(2)}, u32[]{:S(2)}) collective-permute-start(f32[10,80,128]{2,1,0:T(8,128)S(1)} %shard_map.112.own_ref), channel_id=1, source_target_pairs={{0,1},{1,0},{2,3},{3,2},{4,5},{5,4},{6,7},{7,6},{8,9},{9,8},{10,11... | collective-permute-start | bytes 1228808 | tf_op jit(solution)/shard_map/ppermute | solution.py:354
  10.9 5.3 %collective-permute-start.1 = (f32[10,80,128]{2,1,0:T(8,128)S(1)}, f32[10,80,128]{2,1,0:T(8,128)S(1)}, u32[]{:S(2)}, u32[]{:S(2)}) collective-permute-start(f32[10,80,128]{2,1,0:T(8,128)S(1)} %shard_map.112.own_ref), channel_id=1, source_target_pairs={{1,2},{2,1},{3,4},{4,3},{5,6},{6,5},{7,8},{8,7},{9,10},{10,9},{11,... | collective-permute-start | bytes 1228808 | tf_op jit(solution)/shard_map/ppermute | solution.py:353
  11.7 17.2 %copy-start.4 = (f32[75,75]{1,0:T(8,128)S(1)}, f32[75,75]{1,0:T(8,128)}, u32[]{:S(2)}) copy-start(f32[75,75]{1,0:T(8,128)} %eof_ref.1) | copy-start | bytes 67504
  11.7 23.9 %copy-start.1 = (f32[75,8,128]{2,1,0:T(8,128)S(1)}, f32[75,8,128]{2,1,0:T(8,128)}, u32[]{:S(2)}) copy-start(f32[75,8,128]{2,1,0:T(8,128)} %dir_ref.5) | copy-start | bytes 921604
  11.7 23.9 %copy-start.2 = (f32[75,8,128]{2,1,0:T(8,128)S(1)}, f32[75,8,128]{2,1,0:T(8,128)}, u32[]{:S(2)}) copy-start(f32[75,8,128]{2,1,0:T(8,128)} %res_ref.3) | copy-start | bytes 921604
  18.0 10.9 %collective-permute-start.2 = (f32[8,80,128]{2,1,0:T(8,128)S(1)}, f32[8,80,128]{2,1,0:T(8,128)S(1)}, u32[]{:S(2)}, u32[]{:S(2)}) collective-permute-start(f32[8,80,128]{2,1,0:T(8,128)S(1)} %get-tuple-element.12), channel_id=1, source_target_pairs={{0,16},{16,0},{32,48},{48,32},{64,80},{80,64},{96,112},{112,96},{1... | collective-permute-start | bytes 983048 | tf_op jit(solution)/shard_map/ppermute | solution.py:365
  26.9 8.7 %collective-permute-start.3 = (f32[8,80,128]{2,1,0:T(8,128)S(1)}, f32[8,80,128]{2,1,0:T(8,128)S(1)}, u32[]{:S(2)}, u32[]{:S(2)}) collective-permute-start(f32[8,80,128]{2,1,0:T(8,128)S(1)} %get-tuple-element.13), channel_id=1, source_target_pairs={{0,496},{16,32},{32,16},{48,64},{64,48},{80,96},{96,80},{112,128},... | collective-permute-start | bytes 983048 | tf_op jit(solution)/shard_map/ppermute | solution.py:364

commit v3 on v2

--- a/solution.py
+++ b/solution.py
@@ -42,7 +42,18 @@
     return mul(lh, rh) + (mul(lh, rl) + mul(ll, rh))
 
 
-def pack_tile(eof_ref, dir_ref, ke_ref, kn_ref, wet_ref, base_ref, frac_ref, rinv_ref, out_ref):
+def pack_tile(*refs):
+    count = (len(refs) - 2) // 2
+    sources, out_ref, held, sems = refs[:count], refs[count], refs[count + 1 : -1], refs[-1]
+    copies = [
+        pltpu.make_async_copy(source, target, sems.at[k])
+        for k, (source, target) in enumerate(zip(sources, held))
+    ]
+    for copy in copies:
+        copy.start()
+    for copy in copies:
+        copy.wait()
+    dir_ref, eof_ref, ke_ref, kn_ref, wet_ref, base_ref, frac_ref, rinv_ref = held
     levels = dir_ref.shape[0]
     zeros = jnp.zeros((PAD - levels - 3, LANES), jnp.float32)
     eof = eof_ref[...]
@@ -132,13 +143,13 @@
 
 def diffuse_all(one, two, coef, low, high):
     def body(step, _):
-        cut = pl.ds(pl.multiple_of(step * 8, 8), 8)
+        cut = pl.ds(pl.multiple_of(step * 16, 16), 16)
         for src, dst, trim in ((one, two, 0), (two, one, 1), (one, two, 2)):
             for index in range(low + trim, high - trim):
                 diffuse_row(src, dst, coef, index, cut)
         return 0
 
-    lax.fori_loop(0, PAD // 8, body, 0)
+    lax.fori_loop(0, PAD // 16, body, 0)
 
 
 def local_image(
@@ -335,13 +346,9 @@
     lon, lat = lax.axis_index("lon"), lax.axis_index("lat")
     flags = jnp.stack([1 - lat % 2, 1 - lon % 2, (lat == lat_count - 1).astype(jnp.int32)])
     flags = flags.astype(jnp.int32)
-    direction, residual = near(direction), near(residual)
-    own = pl.pallas_call(
-        pack_tile, out_shape=local((ROWS + 2, PAD, LANES)), in_specs=[VMEM] * 8, out_specs=VMEM,
-        compiler_params=grant(8),
-    )(
+    inputs = (
+        direction,
         eof_basis,
-        direction,
         kappa_east,
         kappa_north,
         wet_mask,
@@ -349,6 +356,16 @@
         obs_frac.reshape(2, 1, -1),
         obs_rinv.reshape(levels, 1, -1),
     )
+    own = pl.pallas_call(
+        pack_tile,
+        out_shape=local((ROWS + 2, PAD, LANES)),
+        in_specs=[pl.BlockSpec(memory_space=pltpu.HBM)] * len(inputs),
+        out_specs=VMEM,
+        scratch_shapes=[pltpu.VMEM(x.shape, x.dtype) for x in inputs]
+        + [pltpu.SemaphoreType.DMA((len(inputs),))],
+        compiler_params=grant(8),
+    )(*(pltpu.with_memory_space_constraint(x, pltpu.HBM) for x in inputs))
+    direction, residual = near(direction), near(residual)
     first, second = lat_pairs(lon_count, lat_count)
     lat_b = lax.ppermute(own, ("lon", "lat"), second)
     lat_a = lax.ppermute(own, ("lon", "lat"), first)

time: 100 us -> 94 us (0.940)
  local copies, waits for them, and re-layouts: 5.48 us -> 0.12 us
    unnamed x23 -> x7, local copies, waits for them, and re-layouts: 5.47 us -> 0.11 us
    pallas_call x1, Pallas kernels: 18.8 us -> 16.9 us  [per_device(): pl.pallas_call(local_image, out_shape=(local(direction.shape), local((lon...]
    pallas_call x1, Pallas kernels: 0.48 us -> 1.67 us  [per_device(): pl.pallas_call(pack_tile, out_shape=local((ROWS + 2, PAD, LANES)), in_spe...]
where the time goes in v3:
time: 94 us; the launch traced here: 93.7 us
  blocking collectives  44.4 us (47%)
  Pallas kernels  21.3 us (23%)
  starting transfers between devices  15.9 us (17%)
  waiting for transfers between devices  11.2 us (12%)
    all_to_all x1, blocking collectives, per_device(): part = lax.all_to_all(part, 'lat', 0, 0, tiled=True)  29.7 us
    pallas_call x1, Pallas kernels, per_device(): pl.pallas_call(local_image, out_shape=(local(direction.shape), local((lon...  16.9 us
    all_to_all x1, blocking collectives, per_device(): part = lax.all_to_all(part, 'lon', 0, 0, tiled=True)  14.6 us
    ppermute x1, starting transfers between devices, per_device(): lon_a = lax.ppermute(to_a, 'lon', first)  8.89 us
    ppermute x1, waiting for transfers between devices, per_device(): lon_b = lax.ppermute(to_b, 'lon', second)  6.65 us
    ppermute x1, waiting for transfers between devices, per_device(): lat_a = lax.ppermute(own, ('lon', 'lat'), first)  4.53 us
    ppermute x1, starting transfers between devices, per_device(): lat_a = lax.ppermute(own, ('lon', 'lat'), first)  4.36 us
    ppermute x1, starting transfers between devices, per_device(): lon_b = lax.ppermute(to_b, 'lon', second)  1.92 us
  transfers between devices with their start and end apart: 4, of which 2 were waited for; matrix products, arithmetic and copies ran while one was open for 0% of the time, Pallas kernels for 0%

profile of v3, /device:TPU:1, one launch (start us, length us, event | category | flops | bytes accessed | tf_op | source)
XLA Modules:
  0.0 93.7 jit_solution(10515406753619265113)
XLA Ops:
  0.6 1.7 %shard_map.112.own_ref = f32[10,80,128]{2,1,0:T(8,128)S(1)} custom-call(f32[75,8,128]{2,1,0:T(8,128)} %dir_ref.3, f32[75,75]{1,0:T(8,128)} %refs_1_.1, f32[8,128]{1,0:T(8,128)} %refs_2_.1, f32[8,128]{1,0:T(8,128)} %refs_3_.1, s32[8,128]{1,0:T(8,128)} %refs_4_.1, s32[1,256]{1,0:T(1,128)} %bitcast.17, f32[2,1,256]{2,1,0:T(1,128)} %bitcast.16, ...), custom_call_target="tpu_custom_call" | custom-call | tf_op jit(solution)/shard_map/pallas_call | solution.py:359
  2.3 4.4 %collective-permute-start = (f32[10,80,128]{2,1,0:T(8,128)S(1)}, f32[10,80,128]{2,1,0:T(8,128)S(1)}, u32[]{:S(2)}, u32[]{:S(2)}) collective-permute-start(f32[10,80,128]{2,1,0:T(8,128)S(1)} %shard_map.112.own_ref), channel_id=1, source_target_pairs={{0,1},{1,0},{2,3},{3,2},{4,5},{5,4},{6,7},{7,6},{8,9},{9,8},{10,11... | collective-permute-start | bytes 1228808 | tf_op jit(solution)/shard_map/ppermute | solution.py:371
  6.7 0.7 collective-permute-start.1
  7.4 0.1 pad_add_fusion.flags
  7.5 0.0 copy-start.2
  7.5 0.0 copy-start
  7.5 0.0 copy-start.1
  7.5 4.5 %collective-permute-done.ra_ref = f32[10,80,128]{2,1,0:T(8,128)S(1)} collective-permute-done((f32[10,80,128]{2,1,0:T(8,128)S(1)}, f32[10,80,128]{2,1,0:T(8,128)S(1)}, u32[]{:S(2)}, u32[]{:S(2)}) %collective-permute-start) | collective-permute-done | bytes 409632 | tf_op jit(solution)/shard_map/ppermute | solution.py:371
  12.0 0.0 collective-permute-done.1.rb_ref
  12.0 1.8 %shard_map.113 = (f32[2,10,80,128]{3,2,1,0:T(8,128)S(1)}, f32[8,80,128]{2,1,0:T(8,128)S(1)}, f32[8,80,128]{2,1,0:T(8,128)S(1)}) custom-call(s32[3]{0:T(128)S(1)} %pad_add_fusion.flags, f32[10,80,128]{2,1,0:T(8,128)S(1)} %shard_map.112.own_ref, f32[10,80,128]{2,1,0:T(8,128)S(1)} %collective-permute-done.ra_ref, f32[10,80,128]{2,1,0:T(8,128)S(1)} %collective-permute-done.1.rb_ref), custom_call_target="tpu_custom_call" | custom-call | tf_op jit(solution)/shard_map/pallas_call | solution.py:373
  13.8 8.9 %collective-permute-start.2 = (f32[8,80,128]{2,1,0:T(8,128)S(1)}, f32[8,80,128]{2,1,0:T(8,128)S(1)}, u32[]{:S(2)}, u32[]{:S(2)}) collective-permute-start(f32[8,80,128]{2,1,0:T(8,128)S(1)} %get-tuple-element.12), channel_id=1, source_target_pairs={{0,16},{16,0},{32,48},{48,32},{64,80},{80,64},{96,112},{112,96},{1... | collective-permute-start | bytes 983048 | tf_op jit(solution)/shard_map/ppermute | solution.py:382
  22.7 1.9 %collective-permute-start.3 = (f32[8,80,128]{2,1,0:T(8,128)S(1)}, f32[8,80,128]{2,1,0:T(8,128)S(1)}, u32[]{:S(2)}, u32[]{:S(2)}) collective-permute-start(f32[8,80,128]{2,1,0:T(8,128)S(1)} %get-tuple-element.13), channel_id=1, source_target_pairs={{0,496},{16,32},{32,16},{48,64},{64,48},{80,96},{96,80},{112,128},... | collective-permute-start | bytes 983048 | tf_op jit(solution)/shard_map/ppermute | solution.py:381
  24.7 0.0 copy-done.2
  24.7 0.1 copy.13
  24.8 0.0 collective-permute-done.2.qa_ref
  24.8 6.6 %collective-permute-done.3.qb_ref = f32[8,80,128]{2,1,0:T(8,128)S(1)} collective-permute-done((f32[8,80,128]{2,1,0:T(8,128)S(1)}, f32[8,80,128]{2,1,0:T(8,128)S(1)}, u32[]{:S(2)}, u32[]{:S(2)}) %collective-permute-start.3) | collective-permute-done | bytes 327712 | tf_op jit(solution)/shard_map/ppermute | solution.py:381
  31.4 0.0 copy-done
  31.4 0.0 copy-done.1
  31.4 16.9 %shard_map.114 = (f32[75,8,128]{2,1,0:T(8,128)S(1)}, f32[32,128]{1,0:T(8,128)S(1)}) custom-call(s32[3]{0:T(128)S(1)} %pad_add_fusion.flags, f32[10,80,128]{2,1,0:T(8,128)S(1)} %shard_map.112.own_ref, f32[2,10,80,128]{3,2,1,0:T(8,128)S(1)} %get-tuple-element.11.ns_ref, f32[8,80,128]{2,1,0:T(8,128)S(1)} %collective-permute-done.2.qa_ref, ...), custom_call_target="tpu_custom_call" | custom-call | tf_op jit(solution)/shard_map/pallas_call | solution.py:383
  48.3 14.6 %all_to_all.17 = f32[32,1,128]{2,1,0:T(1,128)S(1)} all-to-all(f32[32,1,128]{2,1,0:T(1,128)S(1)} %bitcast.14), channel_id=1, replica_groups=mesh['lon'=32,'lat'=16] {'lon'}, dimensions={0} | all-to-all | bytes 32768 | tf_op jit(solution)/shard_map/all_to_all | solution.py:397
  63.0 0.1 reduce_sum.9
  63.0 29.7 %all_to_all.18 = f32[16,1,128]{2,1,0:T(1,128)S(1)} all-to-all(f32[16,1,128]{2,1,0:T(1,128)S(1)} %broadcast_in_dim.2), channel_id=1, replica_groups=mesh['lon'=32,'lat'=16] {'lat'}, dimensions={0} | all-to-all | bytes 16384 | tf_op jit(solution)/shard_map/all_to_all | solution.py:399
  92.7 1.0 %shard_map.115 = (f32[75,8,128]{2,1,0:T(8,128)}, f32[75,8,128]{2,1,0:T(8,128)}, f32[1,1]{1,0:T(1,128)}) custom-call(f32[16,128]{1,0:T(8,128)S(1)} %bitcast.13, f32[75,8,128]{2,1,0:T(8,128)S(1)} %get-tuple-element.15.img_ref, f32[75,8,128]{2,1,0:T(8,128)S(1)} %copy-done.1, f32[75,8,128]{2,1,0:T(8,128)S(1)} %copy-done), custom_call_target="tpu_custom_call" | custom-call | tf_op jit(solution)/shard_map/pallas_call | solution.py:400
  (1 shorter events, 0.0 us)
Async XLA Ops:
  2.3 9.7 %collective-permute-start = (f32[10,80,128]{2,1,0:T(8,128)S(1)}, f32[10,80,128]{2,1,0:T(8,128)S(1)}, u32[]{:S(2)}, u32[]{:S(2)}) collective-permute-start(f32[10,80,128]{2,1,0:T(8,128)S(1)} %shard_map.112.own_ref), channel_id=1, source_target_pairs={{0,1},{1,0},{2,3},{3,2},{4,5},{5,4},{6,7},{7,6},{8,9},{9,8},{10,11... | collective-permute-start | bytes 1228808 | tf_op jit(solution)/shard_map/ppermute | solution.py:371
  6.7 5.3 %collective-permute-start.1 = (f32[10,80,128]{2,1,0:T(8,128)S(1)}, f32[10,80,128]{2,1,0:T(8,128)S(1)}, u32[]{:S(2)}, u32[]{:S(2)}) collective-permute-start(f32[10,80,128]{2,1,0:T(8,128)S(1)} %shard_map.112.own_ref), channel_id=1, source_target_pairs={{1,2},{2,1},{3,4},{4,3},{5,6},{6,5},{7,8},{8,7},{9,10},{10,9},{11,... | collective-permute-start | bytes 1228808 | tf_op jit(solution)/shard_map/ppermute | solution.py:370
  7.5 17.2 %copy-start.2 = (f32[75,75]{1,0:T(8,128)S(1)}, f32[75,75]{1,0:T(8,128)}, u32[]{:S(2)}) copy-start(f32[75,75]{1,0:T(8,128)} %refs_1_.1) | copy-start | bytes 67504
  7.5 23.9 %copy-start = (f32[75,8,128]{2,1,0:T(8,128)S(1)}, f32[75,8,128]{2,1,0:T(8,128)}, u32[]{:S(2)}) copy-start(f32[75,8,128]{2,1,0:T(8,128)} %dir_ref.3) | copy-start | bytes 921604
  7.5 23.9 %copy-start.1 = (f32[75,8,128]{2,1,0:T(8,128)S(1)}, f32[75,8,128]{2,1,0:T(8,128)}, u32[]{:S(2)}) copy-start(f32[75,8,128]{2,1,0:T(8,128)} %res_ref.3) | copy-start | bytes 921604
  13.8 10.9 %collective-permute-start.2 = (f32[8,80,128]{2,1,0:T(8,128)S(1)}, f32[8,80,128]{2,1,0:T(8,128)S(1)}, u32[]{:S(2)}, u32[]{:S(2)}) collective-permute-start(f32[8,80,128]{2,1,0:T(8,128)S(1)} %get-tuple-element.12), channel_id=1, source_target_pairs={{0,16},{16,0},{32,48},{48,32},{64,80},{80,64},{96,112},{112,96},{1... | collective-permute-start | bytes 983048 | tf_op jit(solution)/shard_map/ppermute | solution.py:382
  22.7 8.7 %collective-permute-start.3 = (f32[8,80,128]{2,1,0:T(8,128)S(1)}, f32[8,80,128]{2,1,0:T(8,128)S(1)}, u32[]{:S(2)}, u32[]{:S(2)}) collective-permute-start(f32[8,80,128]{2,1,0:T(8,128)S(1)} %get-tuple-element.13), channel_id=1, source_target_pairs={{0,496},{16,32},{32,16},{48,64},{64,48},{80,96},{96,80},{112,128},... | collective-permute-start | bytes 983048 | tf_op jit(solution)/shard_map/ppermute | solution.py:381

commit v4 on v3

--- a/solution.py
+++ b/solution.py
@@ -16,6 +16,7 @@
 HALO = 7
 SLOTS = 12
 SOUTH, OWN, NORTH = 0, 1, 2
+EDGE, EDGE_ROW = 16, 4
 
 SMEM = pl.BlockSpec(memory_space=pltpu.SMEM)
 VMEM = pl.BlockSpec(memory_space=pltpu.VMEM)
@@ -129,27 +130,22 @@
             ref[2 + 2 * NORTH + half] = ns_ref[0, ROWS + half]
 
 
-def diffuse_row(src, dst, coef, index, cut):
-    centre = src[index, cut, :]
+def diffuse_row(src, dst, coef, index):
+    centre = src[index]
     width = centre.shape[1]
     wide = lambda k: jnp.broadcast_to(coef[k, pl.ds(index, 1), :], centre.shape)
     out = centre * wide(0)
     out = out + wide(1) * pltpu.roll(centre, width - 1, 1)
     out = out + wide(2) * pltpu.roll(centre, 1, 1)
-    out = out + wide(3) * src[index + 1, cut, :]
-    out = out + wide(4) * src[index - 1, cut, :]
-    dst[index, cut, :] = out
+    out = out + wide(3) * src[index + 1]
+    out = out + wide(4) * src[index - 1]
+    dst[index] = out
 
 
 def diffuse_all(one, two, coef, low, high):
-    def body(step, _):
-        cut = pl.ds(pl.multiple_of(step * 16, 16), 16)
-        for src, dst, trim in ((one, two, 0), (two, one, 1), (one, two, 2)):
-            for index in range(low + trim, high - trim):
-                diffuse_row(src, dst, coef, index, cut)
-        return 0
-
-    lax.fori_loop(0, PAD // 16, body, 0)
+    for src, dst, trim in ((one, two, 0), (two, one, 1), (one, two, 2)):
+        for index in range(low + trim, high - trim):
+            diffuse_row(src, dst, coef, index)
 
 
 def local_image(
@@ -225,7 +221,6 @@
     diffuse_all(field, other, coef, 2, BAND - 2)
     physical = other
 
-    keep = lax.broadcasted_iota(jnp.int32, (PAD, LANES), 0) < levels
     for band in range(3):
         for half in range(2):
             cut = slice(half * LANES, (half + 1) * LANES)
@@ -233,54 +228,81 @@
             first, second = qa_ref[slot], qb_ref[slot]
             mid = (ns_ref[1, ROWS + half], own_ref[ROWS + half], ns_ref[0, ROWS + half])[band]
             obs[0, band, :, cut] = jnp.where(lon_even, second, first)
-            obs[1, band, :, cut] = mid
-            obs[2, band, :, cut] = jnp.where(lon_even, first, second)
+            obs[1, band, :, cut] = jnp.where(lon_even, first, second)
+            obs[2, band, :, cut] = mid
     adj[...] = jnp.zeros(adj.shape, jnp.float32)
     cells = lax.broadcasted_iota(jnp.int32, (width, width), 0)
     keep = lax.broadcasted_iota(jnp.int32, (PAD, width), 0) < levels
-    spans = ((4, 9, 5), (8, 17, 8), (16, 20, 16))
-    ends = (9, 17, 19)
-    for band in range(3):
-        begin, stop, adj_begin = spans[band]
-        adj_stop = ends[band]
+
+    def places(side, band):
+        base = obs[side, band, levels : levels + 1, :].astype(jnp.int32)
+        p = obs[side, band, levels + 1 : levels + 2, :]
+        q = obs[side, band, levels + 2 : levels + 3, :]
+        j, i = base >> 7, base & (LANES - 1)
+        turned = (top if band == NORTH else 0 * top) == 1
+        rows = jnp.where(turned, 22 - j, j + ROWS * band)
+        cols = jnp.where(turned, 126 - i, i)
+        a0, a1 = jnp.where(turned, p, 1.0 - p), jnp.where(turned, 1.0 - p, p)
+        b0, b1 = jnp.where(turned, q, 1.0 - q), jnp.where(turned, 1.0 - q, q)
+        return rows, cols, a0, a1, b0, b1
+
+    def weigh(side, band, profile):
+        return jnp.where(keep, obs[side, band] * profile, 0.0)
+
+    place = lax.broadcasted_iota(jnp.int32, (PAD, width), 1)
+    packed = jnp.zeros((PAD, width), jnp.float32)
+    for k in range(EDGE):
+        cell = physical[EDGE_ROW + k]
+        west = pltpu.roll(cell, (EDGE * k + 4) % width, 1)
+        east = pltpu.roll(cell, (EDGE * k + 140) % width, 1)
+        packed = jnp.where(
+            (place >= EDGE * k) & (place < EDGE * k + 8),
+            west,
+            jnp.where((place >= EDGE * k + 8) & (place < EDGE * k + EDGE), east, packed),
+        )
+    packed = split(packed)
+    edge_row, edge_col = cells >> 4, cells & (EDGE - 1)
+
+    def beside(step, total):
+        side, band = step & 1, step >> 1
+        rows, cols, a0, a1, b0, b1 = places(side, band)
+        rows = rows - EDGE_ROW
+        cols = cols + jnp.where(side == 0, -124, 12)
+        row_weight = jnp.where(edge_row == rows, a0, jnp.where(edge_row == rows + 1, a1, 0.0))
+        col_weight = jnp.where(edge_col == cols, b0, jnp.where(edge_col == cols + 1, b1, 0.0))
+        rhs = split(row_weight * col_weight)
+        weighted = weigh(side, band, dot3(packed, rhs, ((1,), (0,))))
+        return total + dot3(split(weighted), rhs, ((1,), (1,)))
+
+    total = jnp.zeros((PAD, width), jnp.float32)
+    for step in range(6):
+        total = beside(step, total)
+    for k in range(1, EDGE - 1):
+        west = pltpu.roll(total, (width - EDGE * k - 4) % width, 1)
+        east = pltpu.roll(total, (2 * width - EDGE * k - 140) % width, 1)
+        adj[EDGE_ROW + k] = jnp.where(
+            (place < 4) | (place >= width - 4),
+            west,
+            jnp.where((place >= 124) & (place < 132), east, 0.0),
+        )
+
+    for band, (begin, stop, lo, hi) in enumerate(((4, 9, 5, 9), (8, 17, 8, 17), (16, 20, 16, 19))):
         lhs = split(physical[begin:stop].reshape((stop - begin) * PAD, width))
-
-        def tile_of(t, _, band=band, lhs=lhs, begin=begin, stop=stop, lo=adj_begin, hi=adj_stop):
-            base = obs[t, band, levels : levels + 1, :].astype(jnp.int32)
-            p = obs[t, band, levels + 1 : levels + 2, :]
-            q = obs[t, band, levels + 2 : levels + 3, :]
-            j, i = base >> 7, base & (LANES - 1)
-            rows, cols = j + ROWS * band, i
-            a0, a1, b0, b1 = 1.0 - p, p, 1.0 - q, q
-            if band == NORTH:
-                turned = top == 1
-                rows = jnp.where(turned, 22 - j, rows)
-                cols = jnp.where(turned, 126 - i, cols)
-                a0, a1 = jnp.where(turned, a1, a0), jnp.where(turned, a0, a1)
-                b0, b1 = jnp.where(turned, b1, b0), jnp.where(turned, b0, b1)
-            near = jnp.where(t == 1, 1, jnp.where(t == 0, jnp.where(cols >= 64, 1, 0), jnp.where(cols < 64, 1, 0)))
-            b0, b1 = jnp.where(near == 1, b0, 0.0), jnp.where(near == 1, b1, 0.0)
-            lane0 = (cols + jnp.where(t == 1, 0, LANES)) & (width - 1)
-            lane1 = (lane0 + 1) & (width - 1)
-            weight = jnp.where(cells == lane0, b0, jnp.where(cells == lane1, b1, 0.0))
-            rhs = split(weight)
-            taken = dot3(lhs, rhs, ((1,), (0,)))
-            row_weight = [
-                jnp.where(rows == r, a0, jnp.where(rows == r - 1, a1, 0.0))
-                for r in range(begin, stop)
-            ]
-            profile = jnp.zeros((PAD, width), jnp.float32)
-            for k in range(stop - begin):
-                profile = profile + row_weight[k] * taken[k * PAD : (k + 1) * PAD]
-            weighted = jnp.where(keep, obs[t, band] * profile, 0.0)
-            spread = jnp.concatenate(
-                [row_weight[r - begin] * weighted for r in range(lo, hi)], 0
-            )
-            added = dot3(split(spread), rhs, ((1,), (1,)))
-            adj[lo:hi] += added.reshape(hi - lo, PAD, width)
-            return 0
-
-        lax.fori_loop(0, 3, tile_of, 0)
+        rows, cols, a0, a1, b0, b1 = places(2, band)
+        lane0 = cols & (width - 1)
+        lane1 = (cols + 1) & (width - 1)
+        rhs = split(jnp.where(cells == lane0, b0, jnp.where(cells == lane1, b1, 0.0)))
+        taken = dot3(lhs, rhs, ((1,), (0,)))
+        row_weight = [
+            jnp.where(rows == r, a0, jnp.where(rows == r - 1, a1, 0.0)) for r in range(begin, stop)
+        ]
+        profile = jnp.zeros((PAD, width), jnp.float32)
+        for k in range(stop - begin):
+            profile = profile + row_weight[k] * taken[k * PAD : (k + 1) * PAD]
+        weighted = weigh(2, band, profile)
+        spread = jnp.concatenate([row_weight[r - begin] * weighted for r in range(lo, hi)], 0)
+        added = dot3(split(spread), rhs, ((1,), (1,)))
+        adj[lo:hi] += added.reshape(hi - lo, PAD, width)
 
     diffuse_all(adj, other, coef, 6, BAND - 6)
 

time: 94 us -> 87.1 us (0.927)
  Pallas kernels: 21.3 us -> 14.5 us
    pallas_call x1, Pallas kernels: 16.9 us -> 10 us  [per_device(): pl.pallas_call(local_image, out_shape=(local(direction.shape), local((lon...]
where the time goes in v4:
time: 87.1 us; the launch traced here: 86.9 us
  blocking collectives  44.4 us (51%)
  starting transfers between devices  15.9 us (18%)
  Pallas kernels  14.5 us (17%)
  waiting for transfers between devices  11.2 us (13%)
    all_to_all x1, blocking collectives, per_device(): part = lax.all_to_all(part, 'lat', 0, 0, tiled=True)  29.7 us
    all_to_all x1, blocking collectives, per_device(): part = lax.all_to_all(part, 'lon', 0, 0, tiled=True)  14.6 us
    pallas_call x1, Pallas kernels, per_device(): pl.pallas_call(local_image, out_shape=(local(direction.shape), local((lon...  10 us
    ppermute x1, starting transfers between devices, per_device(): lon_a = lax.ppermute(to_a, 'lon', first)  8.89 us
    ppermute x1, waiting for transfers between devices, per_device(): lon_b = lax.ppermute(to_b, 'lon', second)  6.65 us
    ppermute x1, waiting for transfers between devices, per_device(): lat_a = lax.ppermute(own, ('lon', 'lat'), first)  4.53 us
    ppermute x1, starting transfers between devices, per_device(): lat_a = lax.ppermute(own, ('lon', 'lat'), first)  4.36 us
    ppermute x1, starting transfers between devices, per_device(): lon_b = lax.ppermute(to_b, 'lon', second)  1.92 us
  transfers between devices with their start and end apart: 4, of which 2 were waited for; matrix products, arithmetic and copies ran while one was open for 0% of the time, Pallas kernels for 0%

profile of v4, /device:TPU:1, one launch (start us, length us, event | category | flops | bytes accessed | tf_op | source)
XLA Modules:
  0.0 86.9 jit_solution(3407893370843949774)
XLA Ops:
  0.6 1.7 %shard_map.112.own_ref = f32[10,80,128]{2,1,0:T(8,128)S(1)} custom-call(f32[75,8,128]{2,1,0:T(8,128)} %dir_ref.3, f32[75,75]{1,0:T(8,128)} %refs_1_.1, f32[8,128]{1,0:T(8,128)} %refs_2_.1, f32[8,128]{1,0:T(8,128)} %refs_3_.1, s32[8,128]{1,0:T(8,128)} %refs_4_.1, s32[1,256]{1,0:T(1,128)} %bitcast.17, f32[2,1,256]{2,1,0:T(1,128)} %bitcast.16, ...), custom_call_target="tpu_custom_call" | custom-call | tf_op jit(solution)/shard_map/pallas_call | solution.py:381
  2.3 4.4 %collective-permute-start = (f32[10,80,128]{2,1,0:T(8,128)S(1)}, f32[10,80,128]{2,1,0:T(8,128)S(1)}, u32[]{:S(2)}, u32[]{:S(2)}) collective-permute-start(f32[10,80,128]{2,1,0:T(8,128)S(1)} %shard_map.112.own_ref), channel_id=1, source_target_pairs={{0,1},{1,0},{2,3},{3,2},{4,5},{5,4},{6,7},{7,6},{8,9},{9,8},{10,11... | collective-permute-start | bytes 1228808 | tf_op jit(solution)/shard_map/ppermute | solution.py:393
  6.7 0.7 collective-permute-start.1
  7.4 0.1 pad_add_fusion.flags
  7.5 0.0 copy-start.2
  7.5 0.0 copy-start
  7.5 0.0 copy-start.1
  7.5 4.5 %collective-permute-done.ra_ref = f32[10,80,128]{2,1,0:T(8,128)S(1)} collective-permute-done((f32[10,80,128]{2,1,0:T(8,128)S(1)}, f32[10,80,128]{2,1,0:T(8,128)S(1)}, u32[]{:S(2)}, u32[]{:S(2)}) %collective-permute-start) | collective-permute-done | bytes 409632 | tf_op jit(solution)/shard_map/ppermute | solution.py:393
  12.0 0.0 collective-permute-done.1.rb_ref
  12.0 1.8 %shard_map.113 = (f32[2,10,80,128]{3,2,1,0:T(8,128)S(1)}, f32[8,80,128]{2,1,0:T(8,128)S(1)}, f32[8,80,128]{2,1,0:T(8,128)S(1)}) custom-call(s32[3]{0:T(128)S(1)} %pad_add_fusion.flags, f32[10,80,128]{2,1,0:T(8,128)S(1)} %shard_map.112.own_ref, f32[10,80,128]{2,1,0:T(8,128)S(1)} %collective-permute-done.ra_ref, f32[10,80,128]{2,1,0:T(8,128)S(1)} %collective-permute-done.1.rb_ref), custom_call_target="tpu_custom_call" | custom-call | tf_op jit(solution)/shard_map/pallas_call | solution.py:395
  13.8 8.9 %collective-permute-start.2 = (f32[8,80,128]{2,1,0:T(8,128)S(1)}, f32[8,80,128]{2,1,0:T(8,128)S(1)}, u32[]{:S(2)}, u32[]{:S(2)}) collective-permute-start(f32[8,80,128]{2,1,0:T(8,128)S(1)} %get-tuple-element.12), channel_id=1, source_target_pairs={{0,16},{16,0},{32,48},{48,32},{64,80},{80,64},{96,112},{112,96},{1... | collective-permute-start | bytes 983048 | tf_op jit(solution)/shard_map/ppermute | solution.py:404
  22.7 1.9 %collective-permute-start.3 = (f32[8,80,128]{2,1,0:T(8,128)S(1)}, f32[8,80,128]{2,1,0:T(8,128)S(1)}, u32[]{:S(2)}, u32[]{:S(2)}) collective-permute-start(f32[8,80,128]{2,1,0:T(8,128)S(1)} %get-tuple-element.13), channel_id=1, source_target_pairs={{0,496},{16,32},{32,16},{48,64},{64,48},{80,96},{96,80},{112,128},... | collective-permute-start | bytes 983048 | tf_op jit(solution)/shard_map/ppermute | solution.py:403
  24.7 0.0 copy-done.2
  24.7 0.1 copy.13
  24.8 0.0 collective-permute-done.2.qa_ref
  24.8 6.6 %collective-permute-done.3.qb_ref = f32[8,80,128]{2,1,0:T(8,128)S(1)} collective-permute-done((f32[8,80,128]{2,1,0:T(8,128)S(1)}, f32[8,80,128]{2,1,0:T(8,128)S(1)}, u32[]{:S(2)}, u32[]{:S(2)}) %collective-permute-start.3) | collective-permute-done | bytes 327712 | tf_op jit(solution)/shard_map/ppermute | solution.py:403
  31.4 0.0 copy-done
  31.4 0.0 copy-done.1
  31.4 10.0 %shard_map.114 = (f32[75,8,128]{2,1,0:T(8,128)S(1)}, f32[32,128]{1,0:T(8,128)S(1)}) custom-call(s32[3]{0:T(128)S(1)} %pad_add_fusion.flags, f32[10,80,128]{2,1,0:T(8,128)S(1)} %shard_map.112.own_ref, f32[2,10,80,128]{3,2,1,0:T(8,128)S(1)} %get-tuple-element.11.ns_ref, f32[8,80,128]{2,1,0:T(8,128)S(1)} %collective-permute-done.2.qa_ref, ...), custom_call_target="tpu_custom_call" | custom-call | tf_op jit(solution)/shard_map/pallas_call | solution.py:405
  41.5 14.6 %all_to_all.17 = f32[32,1,128]{2,1,0:T(1,128)S(1)} all-to-all(f32[32,1,128]{2,1,0:T(1,128)S(1)} %bitcast.14), channel_id=1, replica_groups=mesh['lon'=32,'lat'=16] {'lon'}, dimensions={0} | all-to-all | bytes 32768 | tf_op jit(solution)/shard_map/all_to_all | solution.py:419
  56.1 0.1 reduce_sum.9
  56.2 29.7 %all_to_all.18 = f32[16,1,128]{2,1,0:T(1,128)S(1)} all-to-all(f32[16,1,128]{2,1,0:T(1,128)S(1)} %broadcast_in_dim.2), channel_id=1, replica_groups=mesh['lon'=32,'lat'=16] {'lat'}, dimensions={0} | all-to-all | bytes 16384 | tf_op jit(solution)/shard_map/all_to_all | solution.py:421
  85.9 1.0 %shard_map.115 = (f32[75,8,128]{2,1,0:T(8,128)}, f32[75,8,128]{2,1,0:T(8,128)}, f32[1,1]{1,0:T(1,128)}) custom-call(f32[16,128]{1,0:T(8,128)S(1)} %bitcast.13, f32[75,8,128]{2,1,0:T(8,128)S(1)} %get-tuple-element.15.img_ref, f32[75,8,128]{2,1,0:T(8,128)S(1)} %copy-done.1, f32[75,8,128]{2,1,0:T(8,128)S(1)} %copy-done), custom_call_target="tpu_custom_call" | custom-call | tf_op jit(solution)/shard_map/pallas_call | solution.py:422
  (1 shorter events, 0.0 us)
Async XLA Ops:
  2.3 9.7 %collective-permute-start = (f32[10,80,128]{2,1,0:T(8,128)S(1)}, f32[10,80,128]{2,1,0:T(8,128)S(1)}, u32[]{:S(2)}, u32[]{:S(2)}) collective-permute-start(f32[10,80,128]{2,1,0:T(8,128)S(1)} %shard_map.112.own_ref), channel_id=1, source_target_pairs={{0,1},{1,0},{2,3},{3,2},{4,5},{5,4},{6,7},{7,6},{8,9},{9,8},{10,11... | collective-permute-start | bytes 1228808 | tf_op jit(solution)/shard_map/ppermute | solution.py:393
  6.7 5.3 %collective-permute-start.1 = (f32[10,80,128]{2,1,0:T(8,128)S(1)}, f32[10,80,128]{2,1,0:T(8,128)S(1)}, u32[]{:S(2)}, u32[]{:S(2)}) collective-permute-start(f32[10,80,128]{2,1,0:T(8,128)S(1)} %shard_map.112.own_ref), channel_id=1, source_target_pairs={{1,2},{2,1},{3,4},{4,3},{5,6},{6,5},{7,8},{8,7},{9,10},{10,9},{11,... | collective-permute-start | bytes 1228808 | tf_op jit(solution)/shard_map/ppermute | solution.py:392
  7.5 17.2 %copy-start.2 = (f32[75,75]{1,0:T(8,128)S(1)}, f32[75,75]{1,0:T(8,128)}, u32[]{:S(2)}) copy-start(f32[75,75]{1,0:T(8,128)} %refs_1_.1) | copy-start | bytes 67504
  7.5 23.9 %copy-start = (f32[75,8,128]{2,1,0:T(8,128)S(1)}, f32[75,8,128]{2,1,0:T(8,128)}, u32[]{:S(2)}) copy-start(f32[75,8,128]{2,1,0:T(8,128)} %dir_ref.3) | copy-start | bytes 921604
  7.5 23.9 %copy-start.1 = (f32[75,8,128]{2,1,0:T(8,128)S(1)}, f32[75,8,128]{2,1,0:T(8,128)}, u32[]{:S(2)}) copy-start(f32[75,8,128]{2,1,0:T(8,128)} %res_ref.3) | copy-start | bytes 921604
  13.8 10.9 %collective-permute-start.2 = (f32[8,80,128]{2,1,0:T(8,128)S(1)}, f32[8,80,128]{2,1,0:T(8,128)S(1)}, u32[]{:S(2)}, u32[]{:S(2)}) collective-permute-start(f32[8,80,128]{2,1,0:T(8,128)S(1)} %get-tuple-element.12), channel_id=1, source_target_pairs={{0,16},{16,0},{32,48},{48,32},{64,80},{80,64},{96,112},{112,96},{1... | collective-permute-start | bytes 983048 | tf_op jit(solution)/shard_map/ppermute | solution.py:404
  22.7 8.7 %collective-permute-start.3 = (f32[8,80,128]{2,1,0:T(8,128)S(1)}, f32[8,80,128]{2,1,0:T(8,128)S(1)}, u32[]{:S(2)}, u32[]{:S(2)}) collective-permute-start(f32[8,80,128]{2,1,0:T(8,128)S(1)} %get-tuple-element.13), channel_id=1, source_target_pairs={{0,496},{16,32},{32,16},{48,64},{64,48},{80,96},{96,80},{112,128},... | collective-permute-start | bytes 983048 | tf_op jit(solution)/shard_map/ppermute | solution.py:403

commit v5 on v4

--- a/solution.py
+++ b/solution.py
@@ -44,8 +44,9 @@
 
 
 def pack_tile(*refs):
-    count = (len(refs) - 2) // 2
-    sources, out_ref, held, sems = refs[:count], refs[count], refs[count + 1 : -1], refs[-1]
+    count = (len(refs) - 4) // 2
+    sources, held, sems = refs[:count], refs[count + 3 : -1], refs[-1]
+    out_ref, far_ref, near_ref = refs[count : count + 3]
     copies = [
         pltpu.make_async_copy(source, target, sems.at[k])
         for k, (source, target) in enumerate(zip(sources, held))
@@ -74,6 +75,21 @@
         out_ref[ROWS + half, levels + 1 : levels + 2, :] = frac_ref[0, :, cut]
         out_ref[ROWS + half, levels + 2 : levels + 3, :] = frac_ref[1, :, cut]
         out_ref[ROWS + half, levels + 3 :, :] = zeros
+        far_ref[HALO + half] = out_ref[ROWS + half]
+        near_ref[HALO + half] = out_ref[ROWS + half]
+    northern = lax.axis_index("lat") % 2 == 1
+    for row in range(HALO):
+        low, high = out_ref[row], out_ref[row + 1]
+        far_ref[row] = jnp.where(northern, high, low)
+        near_ref[row] = jnp.where(northern, low, high)
+
+
+def row_tile(own_ref, ns_ref, index):
+    if index in (0, BAND - 1):
+        return None
+    if index < ROWS:
+        return ns_ref[1, index - 1]
+    return own_ref[index - ROWS] if index < 2 * ROWS else ns_ref[0, index - 2 * ROWS]
 
 
 def pack_columns(flags, own_ref, ra_ref, rb_ref, ns_ref, pa_ref, pb_ref):
@@ -94,40 +110,30 @@
         first = lax.broadcasted_iota(jnp.int32, (LANES, LANES), 0)
         second = lax.broadcasted_iota(jnp.int32, (LANES, LANES), 1)
         flip = jnp.where(first + second == LANES - 1, 1.0, 0.0).astype(jnp.float32)
-        for row in range(ROWS):
+        for row in range(HALO):
             ns_ref[0, row] = jnp.dot(
-                rb_ref[ROWS - 1 - row], flip, precision=HIGHEST, preferred_element_type=jnp.float32
+                rb_ref[HALO - 1 - row], flip, precision=HIGHEST, preferred_element_type=jnp.float32
             )
 
-    lane = lax.broadcasted_iota(jnp.int32, (8, LANES), 1)
-
-    def one(step, _):
-        cut = pl.ds(pl.multiple_of(step * 8, 8), 8)
-        for group in range(2):
-            west = jnp.zeros((8, LANES), jnp.float32)
-            east = jnp.zeros((8, LANES), jnp.float32)
-            for slot in range(SLOTS):
-                index = group * SLOTS + slot
-                if index < ROWS:
-                    tile = ns_ref[1, index, cut, :]
-                elif index < 2 * ROWS:
-                    tile = own_ref[index - ROWS, cut, :]
-                else:
-                    tile = ns_ref[0, index - 2 * ROWS, cut, :]
-                start = HALO * slot
-                here = (lane >= start) & (lane < start + HALO)
-                west = jnp.where(here, pltpu.roll(tile, start, 1) if start else tile, west)
-                east = jnp.where(here, pltpu.roll(tile, (start + HALO) % LANES, 1), east)
-            pa_ref[group, cut, :] = jnp.where(lon_even, east, west)
-            pb_ref[group, cut, :] = jnp.where(lon_even, west, east)
-        return 0
-
-    lax.fori_loop(0, PAD // 8, one, 0)
+    lane = lax.broadcasted_iota(jnp.int32, (PAD, LANES), 1)
+    for group in range(2):
+        west = jnp.zeros((PAD, LANES), jnp.float32)
+        east = jnp.zeros((PAD, LANES), jnp.float32)
+        for slot in range(SLOTS):
+            tile = row_tile(own_ref, ns_ref, group * SLOTS + slot)
+            if tile is None:
+                continue
+            start = HALO * slot
+            here = (lane >= start) & (lane < start + HALO)
+            west = jnp.where(here, pltpu.roll(tile, start, 1) if start else tile, west)
+            east = jnp.where(here, pltpu.roll(tile, (start + HALO) % LANES, 1), east)
+        pa_ref[group] = jnp.where(lon_even, east, west)
+        pb_ref[group] = jnp.where(lon_even, west, east)
     for half in range(2):
         for ref in (pa_ref, pb_ref):
-            ref[2 + 2 * SOUTH + half] = ns_ref[1, ROWS + half]
+            ref[2 + 2 * SOUTH + half] = ns_ref[1, HALO + half]
             ref[2 + 2 * OWN + half] = own_ref[ROWS + half]
-            ref[2 + 2 * NORTH + half] = ns_ref[0, ROWS + half]
+            ref[2 + 2 * NORTH + half] = ns_ref[0, HALO + half]
 
 
 def diffuse_row(src, dst, coef, index):
@@ -168,33 +174,24 @@
     lon_even, is_top = flags[1] == 1, flags[2] == 1
     levels = dir_ref.shape[0]
     width = 2 * LANES
-    lane = lax.broadcasted_iota(jnp.int32, (8, LANES), 1)
-
-    def unpack(step, _):
-        cut = pl.ds(pl.multiple_of(step * 8, 8), 8)
-        for group in range(2):
-            first, second = qa_ref[group, cut, :], qb_ref[group, cut, :]
-            east = jnp.where(lon_even, first, second)
-            west = jnp.where(lon_even, second, first)
-            for slot in range(SLOTS):
-                index = group * SLOTS + slot
-                if index < ROWS:
-                    tile = ns_ref[1, index, cut, :]
-                elif index < 2 * ROWS:
-                    tile = own_ref[index - ROWS, cut, :]
-                else:
-                    tile = ns_ref[0, index - 2 * ROWS, cut, :]
-                start = HALO * slot
-                from_east = pltpu.roll(east, (LANES - start) % LANES, 1) if start else east
-                from_west = pltpu.roll(west, (LANES - HALO - start) % LANES, 1)
-                halo = jnp.where(
-                    lane < HALO, from_east, jnp.where(lane >= LANES - HALO, from_west, 0.0)
-                )
-                field[index, cut, :LANES] = tile
-                field[index, cut, LANES:] = halo
-        return 0
-
-    lax.fori_loop(0, PAD // 8, unpack, 0)
+    lane = lax.broadcasted_iota(jnp.int32, (PAD, LANES), 1)
+    for group in range(2):
+        first, second = qa_ref[group], qb_ref[group]
+        east = jnp.where(lon_even, first, second)
+        west = jnp.where(lon_even, second, first)
+        for slot in range(SLOTS):
+            index = group * SLOTS + slot
+            tile = row_tile(own_ref, ns_ref, index)
+            if tile is None:
+                field[index] = jnp.zeros((PAD, width), jnp.float32)
+                continue
+            start = HALO * slot
+            from_east = pltpu.roll(east, (LANES - start) % LANES, 1) if start else east
+            from_west = pltpu.roll(west, (LANES - HALO - start) % LANES, 1)
+            field[index, :, :LANES] = tile
+            field[index, :, LANES:] = jnp.where(
+                lane < HALO, from_east, jnp.where(lane >= LANES - HALO, from_west, 0.0)
+            )
 
     ke, kn, wet = field[:, levels, :], field[:, levels + 1, :], field[:, levels + 2, :]
     row = lax.broadcasted_iota(jnp.int32, (BAND, width), 0)
@@ -226,7 +223,7 @@
             cut = slice(half * LANES, (half + 1) * LANES)
             slot = 2 + 2 * band + half
             first, second = qa_ref[slot], qb_ref[slot]
-            mid = (ns_ref[1, ROWS + half], own_ref[ROWS + half], ns_ref[0, ROWS + half])[band]
+            mid = (ns_ref[1, HALO + half], own_ref[ROWS + half], ns_ref[0, HALO + half])[band]
             obs[0, band, :, cut] = jnp.where(lon_even, second, first)
             obs[1, band, :, cut] = jnp.where(lon_even, first, second)
             obs[2, band, :, cut] = mid
@@ -306,12 +303,10 @@
 
     diffuse_all(adj, other, coef, 6, BAND - 6)
 
-    eoft = eoft_ref[...]
+    eoft = split(eoft_ref[...])
     rr = dim = rim = imim = jnp.zeros((levels, LANES), jnp.float32)
     for r in range(ROWS):
-        back = jnp.dot(
-            eoft, other[ROWS + r, :levels, :LANES], precision=HIGHEST, preferred_element_type=jnp.float32
-        )
+        back = dot3(eoft, split(other[ROWS + r, :levels, :LANES]), ((1,), (0,)))
         d, res = dir_ref[:, r, :], res_ref[:, r, :]
         image = d + back
         img_ref[:, r, :] = image
@@ -378,23 +373,27 @@
         obs_frac.reshape(2, 1, -1),
         obs_rinv.reshape(levels, 1, -1),
     )
-    own = pl.pallas_call(
+    own, far, close = pl.pallas_call(
         pack_tile,
-        out_shape=local((ROWS + 2, PAD, LANES)),
+        out_shape=(
+            local((ROWS + 2, PAD, LANES)),
+            local((HALO + 2, PAD, LANES)),
+            local((HALO + 2, PAD, LANES)),
+        ),
         in_specs=[pl.BlockSpec(memory_space=pltpu.HBM)] * len(inputs),
-        out_specs=VMEM,
+        out_specs=(VMEM,) * 3,
         scratch_shapes=[pltpu.VMEM(x.shape, x.dtype) for x in inputs]
         + [pltpu.SemaphoreType.DMA((len(inputs),))],
         compiler_params=grant(8),
     )(*(pltpu.with_memory_space_constraint(x, pltpu.HBM) for x in inputs))
     direction, residual = near(direction), near(residual)
     first, second = lat_pairs(lon_count, lat_count)
-    lat_b = lax.ppermute(own, ("lon", "lat"), second)
-    lat_a = lax.ppermute(own, ("lon", "lat"), first)
+    lat_b = lax.ppermute(far, ("lon", "lat"), second)
+    lat_a = lax.ppermute(close, ("lon", "lat"), first)
     own, lat_a, lat_b = near(own), near(lat_a), near(lat_b)
     north_south, to_a, to_b = pl.pallas_call(
         pack_columns,
-        out_shape=(local((2, ROWS + 2, PAD, LANES)), local((8, PAD, LANES)), local((8, PAD, LANES))),
+        out_shape=(local((2, HALO + 2, PAD, LANES)), local((8, PAD, LANES)), local((8, PAD, LANES))),
         in_specs=[SMEM] + [VMEM] * 3,
         out_specs=(VMEM,) * 3,
         compiler_params=grant(8),

time: 87.1 us -> 84.8 us (0.974)
  Pallas kernels: 14.5 us -> 13.1 us
where the time goes in v5:
time: 84.8 us; the launch traced here: 84.6 us
  blocking collectives  43.9 us (52%)
  starting transfers between devices  15.9 us (19%)
  Pallas kernels  13.1 us (15%)
  waiting for transfers between devices  10.8 us (13%)
    all_to_all x1, blocking collectives, per_device(): part = lax.all_to_all(part, 'lat', 0, 0, tiled=True)  29.7 us
    all_to_all x1, blocking collectives, per_device(): part = lax.all_to_all(part, 'lon', 0, 0, tiled=True)  14.2 us
    pallas_call x1, Pallas kernels, per_device(): pl.pallas_call(local_image, out_shape=(local(direction.shape), local((lon...  9.27 us
    ppermute x1, starting transfers between devices, per_device(): lon_a = lax.ppermute(to_a, 'lon', first)  8.9 us
    ppermute x1, waiting for transfers between devices, per_device(): lon_b = lax.ppermute(to_b, 'lon', second)  6.65 us
    ppermute x1, starting transfers between devices, per_device(): lat_a = lax.ppermute(close, ('lon', 'lat'), first)  4.36 us
    ppermute x1, waiting for transfers between devices, per_device(): lat_a = lax.ppermute(close, ('lon', 'lat'), first)  4.1 us
    ppermute x1, starting transfers between devices, per_device(): lon_b = lax.ppermute(to_b, 'lon', second)  1.92 us
  transfers between devices with their start and end apart: 4, of which 2 were waited for; matrix products, arithmetic and copies ran while one was open for 0% of the time, Pallas kernels for 0%

profile of v5, /device:TPU:1, one launch (start us, length us, event | category | flops | bytes accessed | tf_op | source)
XLA Modules:
  0.0 84.6 jit_solution(15767421174138703950)
XLA Ops:
  0.6 1.7 %shard_map.112 = (f32[10,80,128]{2,1,0:T(8,128)S(1)}, f32[9,80,128]{2,1,0:T(8,128)S(1)}, f32[9,80,128]{2,1,0:T(8,128)S(1)}) custom-call(f32[75,8,128]{2,1,0:T(8,128)} %dir_ref.3, f32[75,75]{1,0:T(8,128)} %refs_1_.1, f32[8,128]{1,0:T(8,128)} %refs_2_.1, f32[8,128]{1,0:T(8,128)} %refs_3_.1, s32[8,128]{1,0:T(8,128)} %refs_4_.1, s32[1,256]{1,0:T(1,128)} %bitcast.17, ...), custom_call_target="tpu_custom_call" | custom-call | tf_op jit(solution)/shard_map/pallas_call | solution.py:376
  2.3 4.4 %collective-permute-start = (f32[9,80,128]{2,1,0:T(8,128)S(1)}, f32[9,80,128]{2,1,0:T(8,128)S(1)}, u32[]{:S(2)}, u32[]{:S(2)}) collective-permute-start(f32[9,80,128]{2,1,0:T(8,128)S(1)} %get-tuple-element.15), channel_id=1, source_target_pairs={{0,1},{1,0},{2,3},{3,2},{4,5},{5,4},{6,7},{7,6},{8,9},{9,8},{10,11... | collective-permute-start | bytes 1105928 | tf_op jit(solution)/shard_map/ppermute | solution.py:392
  6.7 0.7 collective-permute-start.1
  7.4 0.1 pad_add_fusion.flags
  7.5 4.1 %collective-permute-done.ra_ref = f32[9,80,128]{2,1,0:T(8,128)S(1)} collective-permute-done((f32[9,80,128]{2,1,0:T(8,128)S(1)}, f32[9,80,128]{2,1,0:T(8,128)S(1)}, u32[]{:S(2)}, u32[]{:S(2)}) %collective-permute-start) | collective-permute-done | bytes 368672 | tf_op jit(solution)/shard_map/ppermute | solution.py:392
  11.6 0.0 collective-permute-done.1.rb_ref
  11.6 0.0 copy-start.2
  11.6 0.0 copy-start
  11.6 0.0 copy-start.1
  11.6 1.1 %shard_map.113 = (f32[2,9,80,128]{3,2,1,0:T(8,128)S(1)}, f32[8,80,128]{2,1,0:T(8,128)S(1)}, f32[8,80,128]{2,1,0:T(8,128)S(1)}) custom-call(s32[3]{0:T(128)S(1)} %pad_add_fusion.flags, f32[10,80,128]{2,1,0:T(8,128)S(1)} %get-tuple-element.14.own_ref, f32[9,80,128]{2,1,0:T(8,128)S(1)} %collective-permute-done.ra_ref, ...), custom_call_target="tpu_custom_call" | custom-call | tf_op jit(solution)/shard_map/pallas_call | solution.py:394
  12.7 8.9 %collective-permute-start.2 = (f32[8,80,128]{2,1,0:T(8,128)S(1)}, f32[8,80,128]{2,1,0:T(8,128)S(1)}, u32[]{:S(2)}, u32[]{:S(2)}) collective-permute-start(f32[8,80,128]{2,1,0:T(8,128)S(1)} %get-tuple-element.18), channel_id=1, source_target_pairs={{0,16},{16,0},{32,48},{48,32},{64,80},{80,64},{96,112},{112,96},{1... | collective-permute-start | bytes 983048 | tf_op jit(solution)/shard_map/ppermute | solution.py:403
  21.6 1.9 %collective-permute-start.3 = (f32[8,80,128]{2,1,0:T(8,128)S(1)}, f32[8,80,128]{2,1,0:T(8,128)S(1)}, u32[]{:S(2)}, u32[]{:S(2)}) collective-permute-start(f32[8,80,128]{2,1,0:T(8,128)S(1)} %get-tuple-element.19), channel_id=1, source_target_pairs={{0,496},{16,32},{32,16},{48,64},{64,48},{80,96},{96,80},{112,128},... | collective-permute-start | bytes 983048 | tf_op jit(solution)/shard_map/ppermute | solution.py:402
  23.6 0.0 copy-done.2
  23.6 0.1 copy.13
  23.7 0.0 collective-permute-done.2.qa_ref
  23.7 6.6 %collective-permute-done.3.qb_ref = f32[8,80,128]{2,1,0:T(8,128)S(1)} collective-permute-done((f32[8,80,128]{2,1,0:T(8,128)S(1)}, f32[8,80,128]{2,1,0:T(8,128)S(1)}, u32[]{:S(2)}, u32[]{:S(2)}) %collective-permute-start.3) | collective-permute-done | bytes 327712 | tf_op jit(solution)/shard_map/ppermute | solution.py:402
  30.3 0.0 copy-done
  30.3 0.0 copy-done.1
  30.3 9.3 %shard_map.114 = (f32[75,8,128]{2,1,0:T(8,128)S(1)}, f32[32,128]{1,0:T(8,128)S(1)}) custom-call(s32[3]{0:T(128)S(1)} %pad_add_fusion.flags, f32[10,80,128]{2,1,0:T(8,128)S(1)} %get-tuple-element.14.own_ref, f32[2,9,80,128]{3,2,1,0:T(8,128)S(1)} %get-tuple-element.17.ns_ref, f32[8,80,128]{2,1,0:T(8,128)S(1)} %collective-permute-done.2.qa_ref, ...), custom_call_target="tpu_custom_call" | custom-call | tf_op jit(solution)/shard_map/pallas_call | solution.py:404
  39.6 14.2 %all_to_all.17 = f32[32,1,128]{2,1,0:T(1,128)S(1)} all-to-all(f32[32,1,128]{2,1,0:T(1,128)S(1)} %bitcast.14), channel_id=1, replica_groups=mesh['lon'=32,'lat'=16] {'lon'}, dimensions={0} | all-to-all | bytes 32768 | tf_op jit(solution)/shard_map/all_to_all | solution.py:418
  53.8 0.1 reduce_sum.9
  53.9 29.7 %all_to_all.18 = f32[16,1,128]{2,1,0:T(1,128)S(1)} all-to-all(f32[16,1,128]{2,1,0:T(1,128)S(1)} %broadcast_in_dim.2), channel_id=1, replica_groups=mesh['lon'=32,'lat'=16] {'lat'}, dimensions={0} | all-to-all | bytes 16384 | tf_op jit(solution)/shard_map/all_to_all | solution.py:420
  83.6 1.0 %shard_map.115 = (f32[75,8,128]{2,1,0:T(8,128)}, f32[75,8,128]{2,1,0:T(8,128)}, f32[1,1]{1,0:T(1,128)}) custom-call(f32[16,128]{1,0:T(8,128)S(1)} %bitcast.13, f32[75,8,128]{2,1,0:T(8,128)S(1)} %get-tuple-element.21.img_ref, f32[75,8,128]{2,1,0:T(8,128)S(1)} %copy-done.1, f32[75,8,128]{2,1,0:T(8,128)S(1)} %copy-done), custom_call_target="tpu_custom_call" | custom-call | tf_op jit(solution)/shard_map/pallas_call | solution.py:421
  (1 shorter events, 0.0 us)
Async XLA Ops:
  2.3 9.3 %collective-permute-start = (f32[9,80,128]{2,1,0:T(8,128)S(1)}, f32[9,80,128]{2,1,0:T(8,128)S(1)}, u32[]{:S(2)}, u32[]{:S(2)}) collective-permute-start(f32[9,80,128]{2,1,0:T(8,128)S(1)} %get-tuple-element.15), channel_id=1, source_target_pairs={{0,1},{1,0},{2,3},{3,2},{4,5},{5,4},{6,7},{7,6},{8,9},{9,8},{10,11... | collective-permute-start | bytes 1105928 | tf_op jit(solution)/shard_map/ppermute | solution.py:392
  6.7 4.9 %collective-permute-start.1 = (f32[9,80,128]{2,1,0:T(8,128)S(1)}, f32[9,80,128]{2,1,0:T(8,128)S(1)}, u32[]{:S(2)}, u32[]{:S(2)}) collective-permute-start(f32[9,80,128]{2,1,0:T(8,128)S(1)} %get-tuple-element.16), channel_id=1, source_target_pairs={{1,2},{2,1},{3,4},{4,3},{5,6},{6,5},{7,8},{8,7},{9,10},{10,9},{11,... | collective-permute-start | bytes 1105928 | tf_op jit(solution)/shard_map/ppermute | solution.py:391
  11.6 12.0 %copy-start.2 = (f32[75,75]{1,0:T(8,128)S(1)}, f32[75,75]{1,0:T(8,128)}, u32[]{:S(2)}) copy-start(f32[75,75]{1,0:T(8,128)} %refs_1_.1) | copy-start | bytes 67504
  11.6 18.7 %copy-start = (f32[75,8,128]{2,1,0:T(8,128)S(1)}, f32[75,8,128]{2,1,0:T(8,128)}, u32[]{:S(2)}) copy-start(f32[75,8,128]{2,1,0:T(8,128)} %dir_ref.3) | copy-start | bytes 921604
  11.6 18.7 %copy-start.1 = (f32[75,8,128]{2,1,0:T(8,128)S(1)}, f32[75,8,128]{2,1,0:T(8,128)}, u32[]{:S(2)}) copy-start(f32[75,8,128]{2,1,0:T(8,128)} %res_ref.3) | copy-start | bytes 921604
  12.7 10.9 %collective-permute-start.2 = (f32[8,80,128]{2,1,0:T(8,128)S(1)}, f32[8,80,128]{2,1,0:T(8,128)S(1)}, u32[]{:S(2)}, u32[]{:S(2)}) collective-permute-start(f32[8,80,128]{2,1,0:T(8,128)S(1)} %get-tuple-element.18), channel_id=1, source_target_pairs={{0,16},{16,0},{32,48},{48,32},{64,80},{80,64},{96,112},{112,96},{1... | collective-permute-start | bytes 983048 | tf_op jit(solution)/shard_map/ppermute | solution.py:403
  21.6 8.7 %collective-permute-start.3 = (f32[8,80,128]{2,1,0:T(8,128)S(1)}, f32[8,80,128]{2,1,0:T(8,128)S(1)}, u32[]{:S(2)}, u32[]{:S(2)}) collective-permute-start(f32[8,80,128]{2,1,0:T(8,128)S(1)} %get-tuple-element.19), channel_id=1, source_target_pairs={{0,496},{16,32},{32,16},{48,64},{64,48},{80,96},{96,80},{112,128},... | collective-permute-start | bytes 983048 | tf_op jit(solution)/shard_map/ppermute | solution.py:402

commit v6 on v5

--- a/solution.py
+++ b/solution.py
@@ -84,12 +84,12 @@
         near_ref[row] = jnp.where(northern, low, high)
 
 
-def row_tile(own_ref, ns_ref, index):
+def row_tile(own_ref, ns_ref, index, cut=slice(None)):
     if index in (0, BAND - 1):
         return None
     if index < ROWS:
-        return ns_ref[1, index - 1]
-    return own_ref[index - ROWS] if index < 2 * ROWS else ns_ref[0, index - 2 * ROWS]
+        return ns_ref[1, index - 1, cut, :]
+    return own_ref[index - ROWS, cut, :] if index < 2 * ROWS else ns_ref[0, index - 2 * ROWS, cut, :]
 
 
 def pack_columns(flags, own_ref, ra_ref, rb_ref, ns_ref, pa_ref, pb_ref):
@@ -154,53 +154,14 @@
             diffuse_row(src, dst, coef, index)
 
 
-def local_image(
-    flags,
-    own_ref,
-    ns_ref,
-    qa_ref,
-    qb_ref,
-    dir_ref,
-    res_ref,
-    eoft_ref,
-    img_ref,
-    part_ref,
-    field,
-    other,
-    adj,
-    coef,
-    obs,
-):
-    lon_even, is_top = flags[1] == 1, flags[2] == 1
-    levels = dir_ref.shape[0]
-    width = 2 * LANES
-    lane = lax.broadcasted_iota(jnp.int32, (PAD, LANES), 1)
-    for group in range(2):
-        first, second = qa_ref[group], qb_ref[group]
-        east = jnp.where(lon_even, first, second)
-        west = jnp.where(lon_even, second, first)
-        for slot in range(SLOTS):
-            index = group * SLOTS + slot
-            tile = row_tile(own_ref, ns_ref, index)
-            if tile is None:
-                field[index] = jnp.zeros((PAD, width), jnp.float32)
-                continue
-            start = HALO * slot
-            from_east = pltpu.roll(east, (LANES - start) % LANES, 1) if start else east
-            from_west = pltpu.roll(west, (LANES - HALO - start) % LANES, 1)
-            field[index, :, :LANES] = tile
-            field[index, :, LANES:] = jnp.where(
-                lane < HALO, from_east, jnp.where(lane >= LANES - HALO, from_west, 0.0)
-            )
-
-    ke, kn, wet = field[:, levels, :], field[:, levels + 1, :], field[:, levels + 2, :]
-    row = lax.broadcasted_iota(jnp.int32, (BAND, width), 0)
+def set_faces(coef, ke, kn, wet, top):
+    width = ke.shape[1]
+    row = lax.broadcasted_iota(jnp.int32, ke.shape, 0)
     up = lambda x: jnp.concatenate([x[1:], x[:1]], 0)
     down = lambda x: jnp.concatenate([x[-1:], x[:-1]], 0)
     right = lambda x: pltpu.roll(x, width - 1, 1)
     left = lambda x: pltpu.roll(x, 1, 1)
     seam = 2 * ROWS - 1
-    top = jnp.where(is_top, 1, 0)
     ke = jnp.where((row > seam) & (top == 1), right(ke), ke)
     kn_up = up(kn)
     kn = jnp.where(
@@ -215,8 +176,86 @@
     coef[3] = north_face
     coef[4] = south_face
 
-    diffuse_all(field, other, coef, 2, BAND - 2)
+
+def inner_tile(levels, flags, own_ref, ns_ref, out_ref, field, coef):
+    for index in range(BAND):
+        tile = row_tile(own_ref, ns_ref, index)
+        field[index] = jnp.zeros((PAD, LANES), jnp.float32) if tile is None else tile
+    ke, kn, wet = field[:, levels, :], field[:, levels + 1, :], field[:, levels + 2, :]
+    set_faces(coef, ke, kn, wet, flags[2])
+    diffuse_all(field, out_ref, coef, 2, BAND - 2)
+
+
+def local_image(
+    flags,
+    own_ref,
+    ns_ref,
+    qa_ref,
+    qb_ref,
+    dir_ref,
+    res_ref,
+    eof_ref,
+    inner_ref,
+    img_ref,
+    part_ref,
+    strip,
+    strip_next,
+    masks,
+    other,
+    adj,
+    coef,
+    strip_coef,
+    obs,
+):
+    lon_even, is_top = flags[1] == 1, flags[2] == 1
+    levels = dir_ref.shape[0]
+    width = 2 * LANES
+    lane = lax.broadcasted_iota(jnp.int32, (PAD, LANES), 1)
+    slab = slice(PAD - 8, PAD)
+    half_turn = LANES // 2
+    for group in range(2):
+        first, second = qa_ref[group], qb_ref[group]
+        east = jnp.where(lon_even, first, second)
+        west = jnp.where(lon_even, second, first)
+        for slot in range(SLOTS):
+            index = group * SLOTS + slot
+            tile = row_tile(own_ref, ns_ref, index)
+            if tile is None:
+                strip[index] = jnp.zeros((PAD, LANES), jnp.float32)
+                masks[index] = jnp.zeros((8, width), jnp.float32)
+                continue
+            start = HALO * slot
+            from_east = pltpu.roll(east, (half_turn + LANES - start) % LANES, 1)
+            from_west = pltpu.roll(west, (LANES - HALO - start) % LANES, 1)
+            turned = pltpu.roll(tile, half_turn, 1)
+            line = jnp.where(lane >= LANES - HALO, from_west, 0.0)
+            line = jnp.where((lane >= half_turn) & (lane < half_turn + HALO), from_east, line)
+            line = jnp.where((lane >= half_turn - HALO) & (lane < half_turn), turned, line)
+            strip[index] = jnp.where(lane < HALO, tile, line)
+            masks[index, :, :LANES] = tile[slab]
+            beyond = pltpu.roll(from_east[slab], half_turn, 1)
+            masks[index, :, LANES:] = jnp.where(
+                lane[slab] < HALO, beyond, jnp.where(lane[slab] >= LANES - HALO, from_west[slab], 0.0)
+            )
+
+    top = jnp.where(is_top, 1, 0)
+    at = levels - (PAD - 8)
+    set_faces(coef, masks[:, at, :], masks[:, at + 1, :], masks[:, at + 2, :], top)
+    line = lax.broadcasted_iota(jnp.int32, (BAND, LANES), 1)
+    for k in range(5):
+        here, beyond = coef[k, :, :LANES], coef[k, :, LANES:]
+        edge = jnp.where(line < half_turn, pltpu.roll(here, half_turn, 1), pltpu.roll(beyond, half_turn, 1))
+        edge = jnp.where(line < half_turn - HALO, here, edge)
+        strip_coef[k] = jnp.where(line >= LANES - HALO, beyond, edge)
+    diffuse_all(strip, strip_next, strip_coef, 2, BAND - 2)
     physical = other
+    for index in range(EDGE_ROW, EDGE_ROW + EDGE):
+        edge = strip_next[index]
+        turned = pltpu.roll(edge, half_turn, 1)
+        physical[index, :, :LANES] = jnp.where(
+            lane < 3, edge, jnp.where(lane >= LANES - 3, turned, inner_ref[index])
+        )
+        physical[index, :, LANES:] = jnp.where(lane < half_turn, turned, edge)
 
     for band in range(3):
         for half in range(2):
@@ -303,10 +342,10 @@
 
     diffuse_all(adj, other, coef, 6, BAND - 6)
 
-    eoft = split(eoft_ref[...])
+    eof = split(eof_ref[...])
     rr = dim = rim = imim = jnp.zeros((levels, LANES), jnp.float32)
     for r in range(ROWS):
-        back = dot3(eoft, split(other[ROWS + r, :levels, :LANES]), ((1,), (0,)))
+        back = dot3(eof, split(other[ROWS + r, :levels, :LANES]), ((0,), (0,)))
         d, res = dir_ref[:, r, :], res_ref[:, r, :]
         image = d + back
         img_ref[:, r, :] = image
@@ -399,22 +438,48 @@
         compiler_params=grant(8),
     )(flags, own, lat_a, lat_b)
     first, second = lon_pairs(lon_count)
+    tile = pltpu.VMEM((BAND, PAD, LANES), jnp.float32)
+    wide = pltpu.VMEM((BAND, PAD, 2 * LANES), jnp.float32)
+    inner = pl.pallas_call(
+        functools.partial(inner_tile, levels),
+        out_shape=local((BAND, PAD, LANES)),
+        in_specs=[SMEM] + [VMEM] * 2,
+        out_specs=VMEM,
+        scratch_shapes=[tile, pltpu.VMEM((5, BAND, LANES), jnp.float32)],
+        compiler_params=grant(8),
+        cost_estimate=pl.CostEstimate(
+            flops=10_000_000, bytes_accessed=2_000_000, transcendentals=0
+        ),
+    )(flags, own, near(north_south))
     lon_b = lax.ppermute(to_b, "lon", second)
     lon_a = lax.ppermute(to_a, "lon", first)
     image, part = pl.pallas_call(
         local_image,
         out_shape=(local(direction.shape), local((lon_count, LANES))),
-        in_specs=[SMEM] + [VMEM] * 7,
+        in_specs=[SMEM] + [VMEM] * 8,
         out_specs=(VMEM,) * 2,
         compiler_params=grant(28),
         scratch_shapes=[
-            pltpu.VMEM((BAND, PAD, 2 * LANES), jnp.float32),
-            pltpu.VMEM((BAND, PAD, 2 * LANES), jnp.float32),
-            pltpu.VMEM((BAND, PAD, 2 * LANES), jnp.float32),
+            tile,
+            tile,
+            pltpu.VMEM((BAND, 8, 2 * LANES), jnp.float32),
+            wide,
+            wide,
             pltpu.VMEM((5, BAND, 2 * LANES), jnp.float32),
+            pltpu.VMEM((5, BAND, LANES), jnp.float32),
             pltpu.VMEM((3, 3, PAD, 2 * LANES), jnp.float32),
         ],
-    )(flags, own, near(north_south), near(lon_a), near(lon_b), direction, residual, near(eof_basis.T))
+    )(
+        flags,
+        own,
+        near(north_south),
+        near(lon_a),
+        near(lon_b),
+        direction,
+        residual,
+        near(eof_basis),
+        near(inner),
+    )
     part = lax.all_to_all(part, "lon", 0, 0, tiled=True)
     part = jnp.broadcast_to(jnp.sum(part, axis=0, keepdims=True), (lat_count, LANES))
     part = lax.all_to_all(part, "lat", 0, 0, tiled=True)

time: 84.8 us -> 85.2 us (level)
  Pallas kernels: 13.1 us -> 15.2 us
  waiting for transfers between devices: 10.8 us -> 9.01 us
    pallas_call x0 -> x1, Pallas kernels: none -> 1.8 us  [per_device(): pl.pallas_call(functools.partial(inner_tile, levels), out_shape=local((BA...]
    ppermute x1, waiting for transfers between devices: 6.65 us -> 4.91 us  [per_device(): lon_b = lax.ppermute(to_b, 'lon', second)]
  transfers between devices with their start and end apart: 4 -> 4, of which waited for: 2 -> 2; matrix products, arithmetic and copies ran while one was open for 0% -> 0% of each run, Pallas kernels for 0% -> 2%
where the time goes in v6:
time: 85.2 us; the launch traced here: 84.9 us
  blocking collectives  43.9 us (52%)
  starting transfers between devices  15.9 us (19%)
  Pallas kernels  15.2 us (18%)
  waiting for transfers between devices  9.01 us (11%)
    all_to_all x1, blocking collectives, per_device(): part = lax.all_to_all(part, 'lat', 0, 0, tiled=True)  29.7 us
    all_to_all x1, blocking collectives, per_device(): part = lax.all_to_all(part, 'lon', 0, 0, tiled=True)  14.2 us
    pallas_call x1, Pallas kernels, per_device(): pl.pallas_call(local_image, out_shape=(local(direction.shape), local((lon...  9.67 us
    ppermute x1, starting transfers between devices, per_device(): lon_a = lax.ppermute(to_a, 'lon', first)  8.89 us
    ppermute x1, waiting for transfers between devices, per_device(): lon_b = lax.ppermute(to_b, 'lon', second)  4.91 us
    ppermute x1, starting transfers between devices, per_device(): lat_a = lax.ppermute(close, ('lon', 'lat'), first)  4.36 us
    ppermute x1, waiting for transfers between devices, per_device(): lat_a = lax.ppermute(close, ('lon', 'lat'), first)  4.1 us
    ppermute x1, starting transfers between devices, per_device(): lon_b = lax.ppermute(to_b, 'lon', second)  1.92 us
  transfers between devices with their start and end apart: 4, of which 2 were waited for; matrix products, arithmetic and copies ran while one was open for 0% of the time, Pallas kernels for 2%

profile of v6, /device:TPU:1, one launch (start us, length us, event | category | flops | bytes accessed | tf_op | source)
XLA Modules:
  0.0 84.9 jit_solution(6527376709367357805)
XLA Ops:
  0.6 1.7 %shard_map.112 = (f32[10,80,128]{2,1,0:T(8,128)S(1)}, f32[9,80,128]{2,1,0:T(8,128)S(1)}, f32[9,80,128]{2,1,0:T(8,128)S(1)}) custom-call(f32[75,8,128]{2,1,0:T(8,128)} %dir_ref.3, f32[75,75]{1,0:T(8,128)} %eof_ref.1, f32[8,128]{1,0:T(8,128)} %refs_2_.1, f32[8,128]{1,0:T(8,128)} %refs_3_.1, s32[8,128]{1,0:T(8,128)} %refs_4_.1, s32[1,256]{1,0:T(1,128)} %bitcast.15, ...), custom_call_target="tpu_custom_call" | custom-call | tf_op jit(solution)/shard_map/pallas_call | solution.py:415
  2.3 4.4 %collective-permute-start = (f32[9,80,128]{2,1,0:T(8,128)S(1)}, f32[9,80,128]{2,1,0:T(8,128)S(1)}, u32[]{:S(2)}, u32[]{:S(2)}) collective-permute-start(f32[9,80,128]{2,1,0:T(8,128)S(1)} %get-tuple-element.15), channel_id=1, source_target_pairs={{0,1},{1,0},{2,3},{3,2},{4,5},{5,4},{6,7},{7,6},{8,9},{9,8},{10,11... | collective-permute-start | bytes 1105928 | tf_op jit(solution)/shard_map/ppermute | solution.py:431
  6.7 0.7 collective-permute-start.1
  7.4 0.1 pad_add_fusion.flags
  7.5 4.1 %collective-permute-done.ra_ref = f32[9,80,128]{2,1,0:T(8,128)S(1)} collective-permute-done((f32[9,80,128]{2,1,0:T(8,128)S(1)}, f32[9,80,128]{2,1,0:T(8,128)S(1)}, u32[]{:S(2)}, u32[]{:S(2)}) %collective-permute-start) | collective-permute-done | bytes 368672 | tf_op jit(solution)/shard_map/ppermute | solution.py:431
  11.6 0.0 collective-permute-done.1.rb_ref
  11.6 1.1 %shard_map.113 = (f32[2,9,80,128]{3,2,1,0:T(8,128)S(1)}, f32[8,80,128]{2,1,0:T(8,128)S(1)}, f32[8,80,128]{2,1,0:T(8,128)S(1)}) custom-call(s32[3]{0:T(128)S(1)} %pad_add_fusion.flags, f32[10,80,128]{2,1,0:T(8,128)S(1)} %get-tuple-element.14.own_ref, f32[9,80,128]{2,1,0:T(8,128)S(1)} %collective-permute-done.ra_ref, ...), custom_call_target="tpu_custom_call" | custom-call | tf_op jit(solution)/shard_map/pallas_call | solution.py:433
  12.7 8.9 %collective-permute-start.2 = (f32[8,80,128]{2,1,0:T(8,128)S(1)}, f32[8,80,128]{2,1,0:T(8,128)S(1)}, u32[]{:S(2)}, u32[]{:S(2)}) collective-permute-start(f32[8,80,128]{2,1,0:T(8,128)S(1)} %get-tuple-element.18), channel_id=1, source_target_pairs={{0,16},{16,0},{32,48},{48,32},{64,80},{80,64},{96,112},{112,96},{1... | collective-permute-start | bytes 983048 | tf_op jit(solution)/shard_map/ppermute | solution.py:455
  21.6 1.9 %collective-permute-start.3 = (f32[8,80,128]{2,1,0:T(8,128)S(1)}, f32[8,80,128]{2,1,0:T(8,128)S(1)}, u32[]{:S(2)}, u32[]{:S(2)}) collective-permute-start(f32[8,80,128]{2,1,0:T(8,128)S(1)} %get-tuple-element.19), channel_id=1, source_target_pairs={{0,496},{16,32},{32,16},{48,64},{64,48},{80,96},{96,80},{112,128},... | collective-permute-start | bytes 983048 | tf_op jit(solution)/shard_map/ppermute | solution.py:454
  23.6 0.0 copy-start
  23.6 0.0 copy-start.1
  23.6 0.0 copy-start.2
  23.6 1.8 %shard_map.114.inner_ref = f32[24,80,128]{2,1,0:T(8,128)S(1)} custom-call(s32[3]{0:T(128)S(1)} %pad_add_fusion.flags, f32[10,80,128]{2,1,0:T(8,128)S(1)} %get-tuple-element.14.own_ref, f32[2,9,80,128]{3,2,1,0:T(8,128)S(1)} %get-tuple-element.17.ns_ref), custom_call_target="tpu_custom_call" | custom-call | flops 10000000 | bytes 2000000 | tf_op jit(solution)/shard_map/pallas_call | solution.py:443
  25.4 0.0 collective-permute-done.2.qa_ref
  25.4 4.9 %collective-permute-done.3.qb_ref = f32[8,80,128]{2,1,0:T(8,128)S(1)} collective-permute-done((f32[8,80,128]{2,1,0:T(8,128)S(1)}, f32[8,80,128]{2,1,0:T(8,128)S(1)}, u32[]{:S(2)}, u32[]{:S(2)}) %collective-permute-start.3) | collective-permute-done | bytes 327712 | tf_op jit(solution)/shard_map/ppermute | solution.py:454
  30.3 0.0 copy-done
  30.3 0.0 copy-done.1
  30.3 0.0 copy-done.2
  30.3 9.7 %shard_map.115 = (f32[75,8,128]{2,1,0:T(8,128)S(1)}, f32[32,128]{1,0:T(8,128)S(1)}) custom-call(s32[3]{0:T(128)S(1)} %pad_add_fusion.flags, f32[10,80,128]{2,1,0:T(8,128)S(1)} %get-tuple-element.14.own_ref, f32[2,9,80,128]{3,2,1,0:T(8,128)S(1)} %get-tuple-element.17.ns_ref, f32[8,80,128]{2,1,0:T(8,128)S(1)} %collective-permute-done.2.qa_ref, ...), custom_call_target="tpu_custom_call" | custom-call | tf_op jit(solution)/shard_map/pallas_call | solution.py:456
  40.0 14.2 %all_to_all.17 = f32[32,1,128]{2,1,0:T(1,128)S(1)} all-to-all(f32[32,1,128]{2,1,0:T(1,128)S(1)} %bitcast.12), channel_id=1, replica_groups=mesh['lon'=32,'lat'=16] {'lon'}, dimensions={0} | all-to-all | bytes 32768 | tf_op jit(solution)/shard_map/all_to_all | solution.py:483
  54.2 0.1 reduce_sum.9
  54.3 29.7 %all_to_all.18 = f32[16,1,128]{2,1,0:T(1,128)S(1)} all-to-all(f32[16,1,128]{2,1,0:T(1,128)S(1)} %broadcast_in_dim.2), channel_id=1, replica_groups=mesh['lon'=32,'lat'=16] {'lat'}, dimensions={0} | all-to-all | bytes 16384 | tf_op jit(solution)/shard_map/all_to_all | solution.py:485
  84.0 1.0 %shard_map.116 = (f32[75,8,128]{2,1,0:T(8,128)}, f32[75,8,128]{2,1,0:T(8,128)}, f32[1,1]{1,0:T(1,128)}) custom-call(f32[16,128]{1,0:T(8,128)S(1)} %bitcast.11, f32[75,8,128]{2,1,0:T(8,128)S(1)} %get-tuple-element.21.img_ref, f32[75,8,128]{2,1,0:T(8,128)S(1)} %copy-done.1, f32[75,8,128]{2,1,0:T(8,128)S(1)} %copy-done), custom_call_target="tpu_custom_call" | custom-call | tf_op jit(solution)/shard_map/pallas_call | solution.py:486
  (1 shorter events, 0.0 us)
Async XLA Ops:
  2.3 9.3 %collective-permute-start = (f32[9,80,128]{2,1,0:T(8,128)S(1)}, f32[9,80,128]{2,1,0:T(8,128)S(1)}, u32[]{:S(2)}, u32[]{:S(2)}) collective-permute-start(f32[9,80,128]{2,1,0:T(8,128)S(1)} %get-tuple-element.15), channel_id=1, source_target_pairs={{0,1},{1,0},{2,3},{3,2},{4,5},{5,4},{6,7},{7,6},{8,9},{9,8},{10,11... | collective-permute-start | bytes 1105928 | tf_op jit(solution)/shard_map/ppermute | solution.py:431
  6.7 4.9 %collective-permute-start.1 = (f32[9,80,128]{2,1,0:T(8,128)S(1)}, f32[9,80,128]{2,1,0:T(8,128)S(1)}, u32[]{:S(2)}, u32[]{:S(2)}) collective-permute-start(f32[9,80,128]{2,1,0:T(8,128)S(1)} %get-tuple-element.16), channel_id=1, source_target_pairs={{1,2},{2,1},{3,4},{4,3},{5,6},{6,5},{7,8},{8,7},{9,10},{10,9},{11,... | collective-permute-start | bytes 1105928 | tf_op jit(solution)/shard_map/ppermute | solution.py:430
  12.7 12.7 %collective-permute-start.2 = (f32[8,80,128]{2,1,0:T(8,128)S(1)}, f32[8,80,128]{2,1,0:T(8,128)S(1)}, u32[]{:S(2)}, u32[]{:S(2)}) collective-permute-start(f32[8,80,128]{2,1,0:T(8,128)S(1)} %get-tuple-element.18), channel_id=1, source_target_pairs={{0,16},{16,0},{32,48},{48,32},{64,80},{80,64},{96,112},{112,96},{1... | collective-permute-start | bytes 983048 | tf_op jit(solution)/shard_map/ppermute | solution.py:455
  21.6 8.7 %collective-permute-start.3 = (f32[8,80,128]{2,1,0:T(8,128)S(1)}, f32[8,80,128]{2,1,0:T(8,128)S(1)}, u32[]{:S(2)}, u32[]{:S(2)}) collective-permute-start(f32[8,80,128]{2,1,0:T(8,128)S(1)} %get-tuple-element.19), channel_id=1, source_target_pairs={{0,496},{16,32},{32,16},{48,64},{64,48},{80,96},{96,80},{112,128},... | collective-permute-start | bytes 983048 | tf_op jit(solution)/shard_map/ppermute | solution.py:454
  23.6 6.8 %copy-start = (f32[75,8,128]{2,1,0:T(8,128)S(1)}, f32[75,8,128]{2,1,0:T(8,128)}, u32[]{:S(2)}) copy-start(f32[75,8,128]{2,1,0:T(8,128)} %dir_ref.3) | copy-start | bytes 921604
  23.6 6.8 %copy-start.1 = (f32[75,8,128]{2,1,0:T(8,128)S(1)}, f32[75,8,128]{2,1,0:T(8,128)}, u32[]{:S(2)}) copy-start(f32[75,8,128]{2,1,0:T(8,128)} %res_ref.3) | copy-start | bytes 921604
  23.6 6.7 %copy-start.2 = (f32[75,75]{1,0:T(8,128)S(1)}, f32[75,75]{1,0:T(8,128)}, u32[]{:S(2)}) copy-start(f32[75,75]{1,0:T(8,128)} %eof_ref.1) | copy-start | bytes 67504

commit v7 on v5

--- a/solution.py
+++ b/solution.py
@@ -148,10 +148,26 @@
     dst[index] = out
 
 
-def diffuse_all(one, two, coef, low, high):
-    for src, dst, trim in ((one, two, 0), (two, one, 1), (one, two, 2)):
+def diffuse_own(src, dst, coef, index):
+    own, beyond = src[index, :, :LANES], src[index, :, LANES:]
+    lane = lax.broadcasted_iota(jnp.int32, own.shape, 1)
+    wide = lambda k: jnp.broadcast_to(coef[k, pl.ds(index, 1), :LANES], own.shape)
+    out = own * wide(0)
+    out = out + wide(1) * pltpu.roll(jnp.where(lane == 0, beyond, own), LANES - 1, 1)
+    out = out + wide(2) * pltpu.roll(jnp.where(lane == LANES - 1, beyond, own), 1, 1)
+    out = out + wide(3) * src[index + 1, :, :LANES]
+    out = out + wide(4) * src[index - 1, :, :LANES]
+    dst[index, :, :LANES] = out
+
+
+def diffuse_all(one, two, coef, low, high, last=diffuse_row):
+    for src, dst, trim, step in (
+        (one, two, 0, diffuse_row),
+        (two, one, 1, diffuse_row),
+        (one, two, 2, last),
+    ):
         for index in range(low + trim, high - trim):
-            diffuse_row(src, dst, coef, index)
+            step(src, dst, coef, index)
 
 
 def local_image(
@@ -246,17 +262,18 @@
     def weigh(side, band, profile):
         return jnp.where(keep, obs[side, band] * profile, 0.0)
 
-    place = lax.broadcasted_iota(jnp.int32, (PAD, width), 1)
-    packed = jnp.zeros((PAD, width), jnp.float32)
+    packed = [jnp.zeros((PAD, LANES), jnp.float32)] * 2
     for k in range(EDGE):
-        cell = physical[EDGE_ROW + k]
-        west = pltpu.roll(cell, (EDGE * k + 4) % width, 1)
-        east = pltpu.roll(cell, (EDGE * k + 140) % width, 1)
-        packed = jnp.where(
-            (place >= EDGE * k) & (place < EDGE * k + 8),
+        own, beyond = physical[EDGE_ROW + k, :, :LANES], physical[EDGE_ROW + k, :, LANES:]
+        west = pltpu.roll(jnp.where(lane < LANES // 2, own, beyond), (EDGE * k + 4) % LANES, 1)
+        east = pltpu.roll(jnp.where(lane < LANES // 2, beyond, own), (EDGE * k + 12) % LANES, 1)
+        half, first = k // 8, EDGE * (k % 8)
+        packed[half] = jnp.where(
+            (lane >= first) & (lane < first + 8),
             west,
-            jnp.where((place >= EDGE * k + 8) & (place < EDGE * k + EDGE), east, packed),
+            jnp.where((lane >= first + 8) & (lane < first + EDGE), east, packed[half]),
         )
+    packed = jnp.concatenate(packed, 1)
     packed = split(packed)
     edge_row, edge_col = cells >> 4, cells & (EDGE - 1)
 
@@ -275,13 +292,13 @@
     for step in range(6):
         total = beside(step, total)
     for k in range(1, EDGE - 1):
-        west = pltpu.roll(total, (width - EDGE * k - 4) % width, 1)
-        east = pltpu.roll(total, (2 * width - EDGE * k - 140) % width, 1)
-        adj[EDGE_ROW + k] = jnp.where(
-            (place < 4) | (place >= width - 4),
-            west,
-            jnp.where((place >= 124) & (place < 132), east, 0.0),
-        )
+        half = k // 8
+        here = total[:, half * LANES : (half + 1) * LANES]
+        west = pltpu.roll(here, (2 * LANES - EDGE * (k % 8) - 4) % LANES, 1)
+        east = pltpu.roll(here, (2 * LANES - EDGE * (k % 8) - 12) % LANES, 1)
+        low, high = lane < 4, lane >= LANES - 4
+        adj[EDGE_ROW + k, :, :LANES] = jnp.where(low, west, jnp.where(high, east, 0.0))
+        adj[EDGE_ROW + k, :, LANES:] = jnp.where(low, east, jnp.where(high, west, 0.0))
 
     for band, (begin, stop, lo, hi) in enumerate(((4, 9, 5, 9), (8, 17, 8, 17), (16, 20, 16, 19))):
         lhs = split(physical[begin:stop].reshape((stop - begin) * PAD, width))
@@ -301,7 +318,7 @@
         added = dot3(split(spread), rhs, ((1,), (1,)))
         adj[lo:hi] += added.reshape(hi - lo, PAD, width)
 
-    diffuse_all(adj, other, coef, 6, BAND - 6)
+    diffuse_all(adj, other, coef, 6, BAND - 6, diffuse_own)
 
     eoft = split(eoft_ref[...])
     rr = dim = rim = imim = jnp.zeros((levels, LANES), jnp.float32)

time: 84.8 us -> 84.2 us (level)
  no operation moved by 1% of the time
where the time goes in v7:
time: 84.2 us; the launch traced here: 83.9 us
  blocking collectives  43.9 us (52%)
  starting transfers between devices  15.9 us (19%)
  Pallas kernels  12.5 us (15%)
  waiting for transfers between devices  10.8 us (13%)
    all_to_all x1, blocking collectives, per_device(): part = lax.all_to_all(part, 'lat', 0, 0, tiled=True)  29.7 us
    all_to_all x1, blocking collectives, per_device(): part = lax.all_to_all(part, 'lon', 0, 0, tiled=True)  14.2 us
    ppermute x1, starting transfers between devices, per_device(): lon_a = lax.ppermute(to_a, 'lon', first)  8.9 us
    pallas_call x1, Pallas kernels, per_device(): pl.pallas_call(local_image, out_shape=(local(direction.shape), local((lon...  8.67 us
    ppermute x1, waiting for transfers between devices, per_device(): lon_b = lax.ppermute(to_b, 'lon', second)  6.65 us
    ppermute x1, starting transfers between devices, per_device(): lat_a = lax.ppermute(close, ('lon', 'lat'), first)  4.36 us
    ppermute x1, waiting for transfers between devices, per_device(): lat_a = lax.ppermute(close, ('lon', 'lat'), first)  4.1 us
    ppermute x1, starting transfers between devices, per_device(): lon_b = lax.ppermute(to_b, 'lon', second)  1.92 us
  transfers between devices with their start and end apart: 4, of which 2 were waited for; matrix products, arithmetic and copies ran while one was open for 0% of the time, Pallas kernels for 0%

profile of v7, /device:TPU:1, one launch (start us, length us, event | category | flops | bytes accessed | tf_op | source)
XLA Modules:
  0.0 83.9 jit_solution(3482010178581874896)
XLA Ops:
  0.6 1.7 %shard_map.112 = (f32[10,80,128]{2,1,0:T(8,128)S(1)}, f32[9,80,128]{2,1,0:T(8,128)S(1)}, f32[9,80,128]{2,1,0:T(8,128)S(1)}) custom-call(f32[75,8,128]{2,1,0:T(8,128)} %dir_ref.3, f32[75,75]{1,0:T(8,128)} %refs_1_.1, f32[8,128]{1,0:T(8,128)} %refs_2_.1, f32[8,128]{1,0:T(8,128)} %refs_3_.1, s32[8,128]{1,0:T(8,128)} %refs_4_.1, s32[1,256]{1,0:T(1,128)} %bitcast.17, ...), custom_call_target="tpu_custom_call" | custom-call | tf_op jit(solution)/shard_map/pallas_call | solution.py:393
  2.3 4.4 %collective-permute-start = (f32[9,80,128]{2,1,0:T(8,128)S(1)}, f32[9,80,128]{2,1,0:T(8,128)S(1)}, u32[]{:S(2)}, u32[]{:S(2)}) collective-permute-start(f32[9,80,128]{2,1,0:T(8,128)S(1)} %get-tuple-element.15), channel_id=1, source_target_pairs={{0,1},{1,0},{2,3},{3,2},{4,5},{5,4},{6,7},{7,6},{8,9},{9,8},{10,11... | collective-permute-start | bytes 1105928 | tf_op jit(solution)/shard_map/ppermute | solution.py:409
  6.7 0.7 collective-permute-start.1
  7.4 0.1 pad_add_fusion.flags
  7.5 4.1 %collective-permute-done.ra_ref = f32[9,80,128]{2,1,0:T(8,128)S(1)} collective-permute-done((f32[9,80,128]{2,1,0:T(8,128)S(1)}, f32[9,80,128]{2,1,0:T(8,128)S(1)}, u32[]{:S(2)}, u32[]{:S(2)}) %collective-permute-start) | collective-permute-done | bytes 368672 | tf_op jit(solution)/shard_map/ppermute | solution.py:409
  11.6 0.0 collective-permute-done.1.rb_ref
  11.6 0.0 copy-start.2
  11.6 0.0 copy-start
  11.6 0.0 copy-start.1
  11.6 1.1 %shard_map.113 = (f32[2,9,80,128]{3,2,1,0:T(8,128)S(1)}, f32[8,80,128]{2,1,0:T(8,128)S(1)}, f32[8,80,128]{2,1,0:T(8,128)S(1)}) custom-call(s32[3]{0:T(128)S(1)} %pad_add_fusion.flags, f32[10,80,128]{2,1,0:T(8,128)S(1)} %get-tuple-element.14.own_ref, f32[9,80,128]{2,1,0:T(8,128)S(1)} %collective-permute-done.ra_ref, ...), custom_call_target="tpu_custom_call" | custom-call | tf_op jit(solution)/shard_map/pallas_call | solution.py:411
  12.7 8.9 %collective-permute-start.2 = (f32[8,80,128]{2,1,0:T(8,128)S(1)}, f32[8,80,128]{2,1,0:T(8,128)S(1)}, u32[]{:S(2)}, u32[]{:S(2)}) collective-permute-start(f32[8,80,128]{2,1,0:T(8,128)S(1)} %get-tuple-element.18), channel_id=1, source_target_pairs={{0,16},{16,0},{32,48},{48,32},{64,80},{80,64},{96,112},{112,96},{1... | collective-permute-start | bytes 983048 | tf_op jit(solution)/shard_map/ppermute | solution.py:420
  21.6 1.9 %collective-permute-start.3 = (f32[8,80,128]{2,1,0:T(8,128)S(1)}, f32[8,80,128]{2,1,0:T(8,128)S(1)}, u32[]{:S(2)}, u32[]{:S(2)}) collective-permute-start(f32[8,80,128]{2,1,0:T(8,128)S(1)} %get-tuple-element.19), channel_id=1, source_target_pairs={{0,496},{16,32},{32,16},{48,64},{64,48},{80,96},{96,80},{112,128},... | collective-permute-start | bytes 983048 | tf_op jit(solution)/shard_map/ppermute | solution.py:419
  23.6 0.0 copy-done.2
  23.6 0.1 copy.13
  23.7 0.0 collective-permute-done.2.qa_ref
  23.7 6.6 %collective-permute-done.3.qb_ref = f32[8,80,128]{2,1,0:T(8,128)S(1)} collective-permute-done((f32[8,80,128]{2,1,0:T(8,128)S(1)}, f32[8,80,128]{2,1,0:T(8,128)S(1)}, u32[]{:S(2)}, u32[]{:S(2)}) %collective-permute-start.3) | collective-permute-done | bytes 327712 | tf_op jit(solution)/shard_map/ppermute | solution.py:419
  30.3 0.0 copy-done
  30.3 0.0 copy-done.1
  30.3 8.7 %shard_map.114 = (f32[75,8,128]{2,1,0:T(8,128)S(1)}, f32[32,128]{1,0:T(8,128)S(1)}) custom-call(s32[3]{0:T(128)S(1)} %pad_add_fusion.flags, f32[10,80,128]{2,1,0:T(8,128)S(1)} %get-tuple-element.14.own_ref, f32[2,9,80,128]{3,2,1,0:T(8,128)S(1)} %get-tuple-element.17.ns_ref, f32[8,80,128]{2,1,0:T(8,128)S(1)} %collective-permute-done.2.qa_ref, ...), custom_call_target="tpu_custom_call" | custom-call | tf_op jit(solution)/shard_map/pallas_call | solution.py:421
  39.0 14.2 %all_to_all.17 = f32[32,1,128]{2,1,0:T(1,128)S(1)} all-to-all(f32[32,1,128]{2,1,0:T(1,128)S(1)} %bitcast.14), channel_id=1, replica_groups=mesh['lon'=32,'lat'=16] {'lon'}, dimensions={0} | all-to-all | bytes 32768 | tf_op jit(solution)/shard_map/all_to_all | solution.py:435
  53.2 0.1 reduce_sum.9
  53.3 29.7 %all_to_all.18 = f32[16,1,128]{2,1,0:T(1,128)S(1)} all-to-all(f32[16,1,128]{2,1,0:T(1,128)S(1)} %broadcast_in_dim.2), channel_id=1, replica_groups=mesh['lon'=32,'lat'=16] {'lat'}, dimensions={0} | all-to-all | bytes 16384 | tf_op jit(solution)/shard_map/all_to_all | solution.py:437
  83.0 1.0 %shard_map.115 = (f32[75,8,128]{2,1,0:T(8,128)}, f32[75,8,128]{2,1,0:T(8,128)}, f32[1,1]{1,0:T(1,128)}) custom-call(f32[16,128]{1,0:T(8,128)S(1)} %bitcast.13, f32[75,8,128]{2,1,0:T(8,128)S(1)} %get-tuple-element.21.img_ref, f32[75,8,128]{2,1,0:T(8,128)S(1)} %copy-done.1, f32[75,8,128]{2,1,0:T(8,128)S(1)} %copy-done), custom_call_target="tpu_custom_call" | custom-call | tf_op jit(solution)/shard_map/pallas_call | solution.py:438
  (1 shorter events, 0.0 us)
Async XLA Ops:
  2.3 9.3 %collective-permute-start = (f32[9,80,128]{2,1,0:T(8,128)S(1)}, f32[9,80,128]{2,1,0:T(8,128)S(1)}, u32[]{:S(2)}, u32[]{:S(2)}) collective-permute-start(f32[9,80,128]{2,1,0:T(8,128)S(1)} %get-tuple-element.15), channel_id=1, source_target_pairs={{0,1},{1,0},{2,3},{3,2},{4,5},{5,4},{6,7},{7,6},{8,9},{9,8},{10,11... | collective-permute-start | bytes 1105928 | tf_op jit(solution)/shard_map/ppermute | solution.py:409
  6.7 4.9 %collective-permute-start.1 = (f32[9,80,128]{2,1,0:T(8,128)S(1)}, f32[9,80,128]{2,1,0:T(8,128)S(1)}, u32[]{:S(2)}, u32[]{:S(2)}) collective-permute-start(f32[9,80,128]{2,1,0:T(8,128)S(1)} %get-tuple-element.16), channel_id=1, source_target_pairs={{1,2},{2,1},{3,4},{4,3},{5,6},{6,5},{7,8},{8,7},{9,10},{10,9},{11,... | collective-permute-start | bytes 1105928 | tf_op jit(solution)/shard_map/ppermute | solution.py:408
  11.6 12.0 %copy-start.2 = (f32[75,75]{1,0:T(8,128)S(1)}, f32[75,75]{1,0:T(8,128)}, u32[]{:S(2)}) copy-start(f32[75,75]{1,0:T(8,128)} %refs_1_.1) | copy-start | bytes 67504
  11.6 18.7 %copy-start = (f32[75,8,128]{2,1,0:T(8,128)S(1)}, f32[75,8,128]{2,1,0:T(8,128)}, u32[]{:S(2)}) copy-start(f32[75,8,128]{2,1,0:T(8,128)} %dir_ref.3) | copy-start | bytes 921604
  11.6 18.7 %copy-start.1 = (f32[75,8,128]{2,1,0:T(8,128)S(1)}, f32[75,8,128]{2,1,0:T(8,128)}, u32[]{:S(2)}) copy-start(f32[75,8,128]{2,1,0:T(8,128)} %res_ref.3) | copy-start | bytes 921604
  12.7 10.9 %collective-permute-start.2 = (f32[8,80,128]{2,1,0:T(8,128)S(1)}, f32[8,80,128]{2,1,0:T(8,128)S(1)}, u32[]{:S(2)}, u32[]{:S(2)}) collective-permute-start(f32[8,80,128]{2,1,0:T(8,128)S(1)} %get-tuple-element.18), channel_id=1, source_target_pairs={{0,16},{16,0},{32,48},{48,32},{64,80},{80,64},{96,112},{112,96},{1... | collective-permute-start | bytes 983048 | tf_op jit(solution)/shard_map/ppermute | solution.py:420
  21.6 8.7 %collective-permute-start.3 = (f32[8,80,128]{2,1,0:T(8,128)S(1)}, f32[8,80,128]{2,1,0:T(8,128)S(1)}, u32[]{:S(2)}, u32[]{:S(2)}) collective-permute-start(f32[8,80,128]{2,1,0:T(8,128)S(1)} %get-tuple-element.19), channel_id=1, source_target_pairs={{0,496},{16,32},{32,16},{48,64},{64,48},{80,96},{96,80},{112,128},... | collective-permute-start | bytes 983048 | tf_op jit(solution)/shard_map/ppermute | solution.py:419

commit v8 on v7

--- a/solution.py
+++ b/solution.py
@@ -84,6 +84,12 @@
         near_ref[row] = jnp.where(northern, low, high)
 
 
+def by_rows(dir_ref, res_ref, dir_rows_ref, res_rows_ref):
+    for source, target in ((dir_ref, dir_rows_ref), (res_ref, res_rows_ref)):
+        for row in range(ROWS):
+            target[row, : source.shape[0], :] = source[:, row, :]
+
+
 def row_tile(own_ref, ns_ref, index):
     if index in (0, BAND - 1):
         return None
@@ -188,7 +194,7 @@
     obs,
 ):
     lon_even, is_top = flags[1] == 1, flags[2] == 1
-    levels = dir_ref.shape[0]
+    levels = img_ref.shape[0]
     width = 2 * LANES
     lane = lax.broadcasted_iota(jnp.int32, (PAD, LANES), 1)
     for group in range(2):
@@ -275,16 +281,20 @@
         )
     packed = jnp.concatenate(packed, 1)
     packed = split(packed)
-    edge_row, edge_col = cells >> 4, cells & (EDGE - 1)
+    edge_col = lax.broadcasted_iota(jnp.int32, (EDGE, width), 0)
 
     def beside(step, total):
         side, band = step & 1, step >> 1
         rows, cols, a0, a1, b0, b1 = places(side, band)
         rows = rows - EDGE_ROW
         cols = cols + jnp.where(side == 0, -124, 12)
-        row_weight = jnp.where(edge_row == rows, a0, jnp.where(edge_row == rows + 1, a1, 0.0))
         col_weight = jnp.where(edge_col == cols, b0, jnp.where(edge_col == cols + 1, b1, 0.0))
-        rhs = split(row_weight * col_weight)
+        rows, a0, a1 = (jnp.broadcast_to(x, (8, width)) for x in (rows, a0, a1))
+        parts = []
+        for k in range(EDGE):
+            row_weight = jnp.where(rows == k, a0, jnp.where(rows == k - 1, a1, 0.0))
+            parts += [row_weight * col_weight[:8], row_weight * col_weight[8:]]
+        rhs = split(jnp.concatenate(parts, 0))
         weighted = weigh(side, band, dot3(packed, rhs, ((1,), (0,))))
         return total + dot3(split(weighted), rhs, ((1,), (1,)))
 
@@ -324,7 +334,7 @@
     rr = dim = rim = imim = jnp.zeros((levels, LANES), jnp.float32)
     for r in range(ROWS):
         back = dot3(eoft, split(other[ROWS + r, :levels, :LANES]), ((1,), (0,)))
-        d, res = dir_ref[:, r, :], res_ref[:, r, :]
+        d, res = dir_ref[r, :levels, :], res_ref[r, :levels, :]
         image = d + back
         img_ref[:, r, :] = image
         rr, dim, rim, imim = rr + res * res, dim + d * image, rim + res * image, imim + image * image
@@ -405,6 +415,16 @@
     )(*(pltpu.with_memory_space_constraint(x, pltpu.HBM) for x in inputs))
     direction, residual = near(direction), near(residual)
     first, second = lat_pairs(lon_count, lat_count)
+    dir_rows, res_rows = pl.pallas_call(
+        by_rows,
+        out_shape=(local((ROWS, PAD, LANES)),) * 2,
+        in_specs=[VMEM] * 2,
+        out_specs=(VMEM,) * 2,
+        compiler_params=grant(8),
+        cost_estimate=pl.CostEstimate(
+            flops=0, bytes_accessed=1_300_000, transcendentals=0
+        ),
+    )(direction, residual)
     lat_b = lax.ppermute(far, ("lon", "lat"), second)
     lat_a = lax.ppermute(close, ("lon", "lat"), first)
     own, lat_a, lat_b = near(own), near(lat_a), near(lat_b)
@@ -431,7 +451,7 @@
             pltpu.VMEM((5, BAND, 2 * LANES), jnp.float32),
             pltpu.VMEM((3, 3, PAD, 2 * LANES), jnp.float32),
         ],
-    )(flags, own, near(north_south), near(lon_a), near(lon_b), direction, residual, near(eof_basis.T))
+    )(flags, own, near(north_south), near(lon_a), near(lon_b), near(dir_rows), near(res_rows), near(eof_basis.T))
     part = lax.all_to_all(part, "lon", 0, 0, tiled=True)
     part = jnp.broadcast_to(jnp.sum(part, axis=0, keepdims=True), (lat_count, LANES))
     part = lax.all_to_all(part, "lat", 0, 0, tiled=True)

time: 84.2 us -> 83.6 us (level)
  no operation moved by 1% of the time
where the time goes in v8:
time: 83.6 us; the launch traced here: 83.4 us
  blocking collectives  43.9 us (53%)
  starting transfers between devices  15.9 us (19%)
  Pallas kernels  12.2 us (15%)
  waiting for transfers between devices  10.4 us (12%)
    all_to_all x1, blocking collectives, per_device(): part = lax.all_to_all(part, 'lat', 0, 0, tiled=True)  29.7 us
    all_to_all x1, blocking collectives, per_device(): part = lax.all_to_all(part, 'lon', 0, 0, tiled=True)  14.2 us
    ppermute x1, starting transfers between devices, per_device(): lon_a = lax.ppermute(to_a, 'lon', first)  8.9 us
    pallas_call x1, Pallas kernels, per_device(): pl.pallas_call(local_image, out_shape=(local(direction.shape), local((lon...  8.08 us
    ppermute x1, waiting for transfers between devices, per_device(): lon_b = lax.ppermute(to_b, 'lon', second)  6.29 us
    ppermute x1, starting transfers between devices, per_device(): lat_a = lax.ppermute(close, ('lon', 'lat'), first)  4.36 us
    ppermute x1, waiting for transfers between devices, per_device(): lat_a = lax.ppermute(close, ('lon', 'lat'), first)  4.1 us
    ppermute x1, starting transfers between devices, per_device(): lon_b = lax.ppermute(to_b, 'lon', second)  1.92 us
  transfers between devices with their start and end apart: 4, of which 2 were waited for; matrix products, arithmetic and copies ran while one was open for 0% of the time, Pallas kernels for 0%

profile of v8, /device:TPU:1, one launch (start us, length us, event | category | flops | bytes accessed | tf_op | source)
XLA Modules:
  0.0 83.4 jit_solution(7138996315636312269)
XLA Ops:
  0.6 1.7 %shard_map.112 = (f32[10,80,128]{2,1,0:T(8,128)S(1)}, f32[9,80,128]{2,1,0:T(8,128)S(1)}, f32[9,80,128]{2,1,0:T(8,128)S(1)}) custom-call(f32[75,8,128]{2,1,0:T(8,128)} %dir_ref.3, f32[75,75]{1,0:T(8,128)} %refs_1_.1, f32[8,128]{1,0:T(8,128)} %refs_2_.1, f32[8,128]{1,0:T(8,128)} %refs_3_.1, s32[8,128]{1,0:T(8,128)} %refs_4_.1, s32[1,256]{1,0:T(1,128)} %bitcast.17, ...), custom_call_target="tpu_custom_call" | custom-call | tf_op jit(solution)/shard_map/pallas_call | solution.py:403
  2.3 4.4 %collective-permute-start = (f32[9,80,128]{2,1,0:T(8,128)S(1)}, f32[9,80,128]{2,1,0:T(8,128)S(1)}, u32[]{:S(2)}, u32[]{:S(2)}) collective-permute-start(f32[9,80,128]{2,1,0:T(8,128)S(1)} %get-tuple-element.17), channel_id=1, source_target_pairs={{0,1},{1,0},{2,3},{3,2},{4,5},{5,4},{6,7},{7,6},{8,9},{9,8},{10,11... | collective-permute-start | bytes 1105928 | tf_op jit(solution)/shard_map/ppermute | solution.py:429
  6.7 0.7 collective-permute-start.1
  7.4 0.1 pad_add_fusion.flags
  7.5 4.1 %collective-permute-done.ra_ref = f32[9,80,128]{2,1,0:T(8,128)S(1)} collective-permute-done((f32[9,80,128]{2,1,0:T(8,128)S(1)}, f32[9,80,128]{2,1,0:T(8,128)S(1)}, u32[]{:S(2)}, u32[]{:S(2)}) %collective-permute-start) | collective-permute-done | bytes 368672 | tf_op jit(solution)/shard_map/ppermute | solution.py:429
  11.6 0.0 collective-permute-done.1.rb_ref
  11.6 0.0 copy-start.2
  11.6 0.0 copy-start
  11.6 0.0 copy-start.1
  11.6 1.1 %shard_map.113 = (f32[2,9,80,128]{3,2,1,0:T(8,128)S(1)}, f32[8,80,128]{2,1,0:T(8,128)S(1)}, f32[8,80,128]{2,1,0:T(8,128)S(1)}) custom-call(s32[3]{0:T(128)S(1)} %pad_add_fusion.flags, f32[10,80,128]{2,1,0:T(8,128)S(1)} %get-tuple-element.16.own_ref, f32[9,80,128]{2,1,0:T(8,128)S(1)} %collective-permute-done.ra_ref, ...), custom_call_target="tpu_custom_call" | custom-call | tf_op jit(solution)/shard_map/pallas_call | solution.py:431
  12.7 8.9 %collective-permute-start.2 = (f32[8,80,128]{2,1,0:T(8,128)S(1)}, f32[8,80,128]{2,1,0:T(8,128)S(1)}, u32[]{:S(2)}, u32[]{:S(2)}) collective-permute-start(f32[8,80,128]{2,1,0:T(8,128)S(1)} %get-tuple-element.20), channel_id=1, source_target_pairs={{0,16},{16,0},{32,48},{48,32},{64,80},{80,64},{96,112},{112,96},{1... | collective-permute-start | bytes 983048 | tf_op jit(solution)/shard_map/ppermute | solution.py:440
  21.6 1.9 %collective-permute-start.3 = (f32[8,80,128]{2,1,0:T(8,128)S(1)}, f32[8,80,128]{2,1,0:T(8,128)S(1)}, u32[]{:S(2)}, u32[]{:S(2)}) collective-permute-start(f32[8,80,128]{2,1,0:T(8,128)S(1)} %get-tuple-element.21), channel_id=1, source_target_pairs={{0,496},{16,32},{32,16},{48,64},{64,48},{80,96},{96,80},{112,128},... | collective-permute-start | bytes 983048 | tf_op jit(solution)/shard_map/ppermute | solution.py:439
  23.6 0.0 copy-done.2
  23.6 0.1 copy.13
  23.7 0.0 copy-done
  23.7 0.0 copy-done.1
  23.7 0.3 shard_map.114
  24.0 0.0 collective-permute-done.2.qa_ref
  24.0 6.3 %collective-permute-done.3.qb_ref = f32[8,80,128]{2,1,0:T(8,128)S(1)} collective-permute-done((f32[8,80,128]{2,1,0:T(8,128)S(1)}, f32[8,80,128]{2,1,0:T(8,128)S(1)}, u32[]{:S(2)}, u32[]{:S(2)}) %collective-permute-start.3) | collective-permute-done | bytes 327712 | tf_op jit(solution)/shard_map/ppermute | solution.py:439
  30.3 8.1 %shard_map.115 = (f32[75,8,128]{2,1,0:T(8,128)S(1)}, f32[32,128]{1,0:T(8,128)S(1)}) custom-call(s32[3]{0:T(128)S(1)} %pad_add_fusion.flags, f32[10,80,128]{2,1,0:T(8,128)S(1)} %get-tuple-element.16.own_ref, f32[2,9,80,128]{3,2,1,0:T(8,128)S(1)} %get-tuple-element.19.ns_ref, f32[8,80,128]{2,1,0:T(8,128)S(1)} %collective-permute-done.2.qa_ref, ...), custom_call_target="tpu_custom_call" | custom-call | tf_op jit(solution)/shard_map/pallas_call | solution.py:441
  38.4 14.2 %all_to_all.17 = f32[32,1,128]{2,1,0:T(1,128)S(1)} all-to-all(f32[32,1,128]{2,1,0:T(1,128)S(1)} %bitcast.14), channel_id=1, replica_groups=mesh['lon'=32,'lat'=16] {'lon'}, dimensions={0} | all-to-all | bytes 32768 | tf_op jit(solution)/shard_map/all_to_all | solution.py:455
  52.6 0.1 reduce_sum.9
  52.7 29.7 %all_to_all.18 = f32[16,1,128]{2,1,0:T(1,128)S(1)} all-to-all(f32[16,1,128]{2,1,0:T(1,128)S(1)} %broadcast_in_dim.2), channel_id=1, replica_groups=mesh['lon'=32,'lat'=16] {'lat'}, dimensions={0} | all-to-all | bytes 16384 | tf_op jit(solution)/shard_map/all_to_all | solution.py:457
  82.4 1.0 %shard_map.116 = (f32[75,8,128]{2,1,0:T(8,128)}, f32[75,8,128]{2,1,0:T(8,128)}, f32[1,1]{1,0:T(1,128)}) custom-call(f32[16,128]{1,0:T(8,128)S(1)} %bitcast.13, f32[75,8,128]{2,1,0:T(8,128)S(1)} %get-tuple-element.25.img_ref, f32[75,8,128]{2,1,0:T(8,128)S(1)} %copy-done.1, f32[75,8,128]{2,1,0:T(8,128)S(1)} %copy-done), custom_call_target="tpu_custom_call" | custom-call | tf_op jit(solution)/shard_map/pallas_call | solution.py:458
  (1 shorter events, 0.0 us)
Async XLA Ops:
  2.3 9.3 %collective-permute-start = (f32[9,80,128]{2,1,0:T(8,128)S(1)}, f32[9,80,128]{2,1,0:T(8,128)S(1)}, u32[]{:S(2)}, u32[]{:S(2)}) collective-permute-start(f32[9,80,128]{2,1,0:T(8,128)S(1)} %get-tuple-element.17), channel_id=1, source_target_pairs={{0,1},{1,0},{2,3},{3,2},{4,5},{5,4},{6,7},{7,6},{8,9},{9,8},{10,11... | collective-permute-start | bytes 1105928 | tf_op jit(solution)/shard_map/ppermute | solution.py:429
  6.7 4.9 %collective-permute-start.1 = (f32[9,80,128]{2,1,0:T(8,128)S(1)}, f32[9,80,128]{2,1,0:T(8,128)S(1)}, u32[]{:S(2)}, u32[]{:S(2)}) collective-permute-start(f32[9,80,128]{2,1,0:T(8,128)S(1)} %get-tuple-element.18), channel_id=1, source_target_pairs={{1,2},{2,1},{3,4},{4,3},{5,6},{6,5},{7,8},{8,7},{9,10},{10,9},{11,... | collective-permute-start | bytes 1105928 | tf_op jit(solution)/shard_map/ppermute | solution.py:428
  11.6 12.0 %copy-start.2 = (f32[75,75]{1,0:T(8,128)S(1)}, f32[75,75]{1,0:T(8,128)}, u32[]{:S(2)}) copy-start(f32[75,75]{1,0:T(8,128)} %refs_1_.1) | copy-start | bytes 67504
  11.6 12.1 %copy-start = (f32[75,8,128]{2,1,0:T(8,128)S(1)}, f32[75,8,128]{2,1,0:T(8,128)}, u32[]{:S(2)}) copy-start(f32[75,8,128]{2,1,0:T(8,128)} %dir_ref.3) | copy-start | bytes 921604
  11.6 12.1 %copy-start.1 = (f32[75,8,128]{2,1,0:T(8,128)S(1)}, f32[75,8,128]{2,1,0:T(8,128)}, u32[]{:S(2)}) copy-start(f32[75,8,128]{2,1,0:T(8,128)} %res_ref.3) | copy-start | bytes 921604
  12.7 11.3 %collective-permute-start.2 = (f32[8,80,128]{2,1,0:T(8,128)S(1)}, f32[8,80,128]{2,1,0:T(8,128)S(1)}, u32[]{:S(2)}, u32[]{:S(2)}) collective-permute-start(f32[8,80,128]{2,1,0:T(8,128)S(1)} %get-tuple-element.20), channel_id=1, source_target_pairs={{0,16},{16,0},{32,48},{48,32},{64,80},{80,64},{96,112},{112,96},{1... | collective-permute-start | bytes 983048 | tf_op jit(solution)/shard_map/ppermute | solution.py:440
  21.6 8.7 %collective-permute-start.3 = (f32[8,80,128]{2,1,0:T(8,128)S(1)}, f32[8,80,128]{2,1,0:T(8,128)S(1)}, u32[]{:S(2)}, u32[]{:S(2)}) collective-permute-start(f32[8,80,128]{2,1,0:T(8,128)S(1)} %get-tuple-element.21), channel_id=1, source_target_pairs={{0,496},{16,32},{32,16},{48,64},{64,48},{80,96},{96,80},{112,128},... | collective-permute-start | bytes 983048 | tf_op jit(solution)/shard_map/ppermute | solution.py:439

commit v9 on v8

--- a/solution.py
+++ b/solution.py
@@ -20,6 +20,8 @@
 
 SMEM = pl.BlockSpec(memory_space=pltpu.SMEM)
 VMEM = pl.BlockSpec(memory_space=pltpu.VMEM)
+HBM = pl.BlockSpec(memory_space=pltpu.HBM)
+CHUNKS = 5
 
 
 def grant(mebibytes):
@@ -345,7 +347,9 @@
     part_ref[...] = out
 
 
-def finish(part_ref, img_ref, res_ref, dir_ref, new_res_ref, new_dir_ref, step_ref):
+def finish(
+    part_ref, img_ref, res_ref, dir_ref, new_res_ref, new_dir_ref, step_ref, res_buf, dir_buf, sems
+):
     total = jnp.sum(part_ref[...], axis=0, keepdims=True)
     lane = lax.broadcasted_iota(jnp.int32, total.shape, 1)
     rr, dim, rim, imim = (
@@ -355,9 +359,21 @@
     new_norm = rr + step * (step * imim - 2.0 * rim)
     beta = new_norm / rr
     step_ref[...] = step
-    new_res = res_ref[...] - step[None] * img_ref[...]
-    new_res_ref[...] = new_res
-    new_dir_ref[...] = new_res + beta[None] * dir_ref[...]
+    chunk = res_buf.shape[0] // CHUNKS
+    copies = []
+    for k in range(CHUNKS):
+        cut = slice(k * chunk, (k + 1) * chunk)
+        new_res = res_ref[cut] - step[None] * img_ref[cut]
+        res_buf[cut] = new_res
+        dir_buf[cut] = new_res + beta[None] * dir_ref[cut]
+        copies += [
+            pltpu.make_async_copy(res_buf.at[cut], new_res_ref.at[cut], sems.at[2 * k]),
+            pltpu.make_async_copy(dir_buf.at[cut], new_dir_ref.at[cut], sems.at[2 * k + 1]),
+        ]
+        copies[-2].start()
+        copies[-1].start()
+    for copy in copies:
+        copy.wait()
 
 
 def lat_pairs(lon_count, lat_count):
@@ -459,7 +475,12 @@
         finish,
         out_shape=(shape(direction.shape), shape(direction.shape), shape((1, 1))),
         in_specs=[VMEM] * 4,
-        out_specs=(VMEM,) * 3,
+        out_specs=(HBM, HBM, VMEM),
+        scratch_shapes=[
+            pltpu.VMEM(direction.shape, jnp.float32),
+            pltpu.VMEM(direction.shape, jnp.float32),
+            pltpu.SemaphoreType.DMA((2 * CHUNKS,)),
+        ],
         compiler_params=grant(8),
     )(near(part), near(image), residual, direction)
     return new_residual, new_direction, step_length.reshape(())

time: 83.6 us -> 84.2 us (level)
  no operation moved by 1% of the time
where the time goes in v9:
time: 84.2 us; the launch traced here: 83.9 us
  blocking collectives  43.9 us (52%)
  starting transfers between devices  15.9 us (19%)
  Pallas kernels  12.7 us (15%)
  waiting for transfers between devices  10.4 us (12%)
    all_to_all x1, blocking collectives, per_device(): part = lax.all_to_all(part, 'lat', 0, 0, tiled=True)  29.7 us
    all_to_all x1, blocking collectives, per_device(): part = lax.all_to_all(part, 'lon', 0, 0, tiled=True)  14.2 us
    ppermute x1, starting transfers between devices, per_device(): lon_a = lax.ppermute(to_a, 'lon', first)  8.9 us
    pallas_call x1, Pallas kernels, per_device(): pl.pallas_call(local_image, out_shape=(local(direction.shape), local((lon...  8.08 us
    ppermute x1, waiting for transfers between devices, per_device(): lon_b = lax.ppermute(to_b, 'lon', second)  6.29 us
    ppermute x1, starting transfers between devices, per_device(): lat_a = lax.ppermute(close, ('lon', 'lat'), first)  4.36 us
    ppermute x1, waiting for transfers between devices, per_device(): lat_a = lax.ppermute(close, ('lon', 'lat'), first)  4.1 us
    ppermute x1, starting transfers between devices, per_device(): lon_b = lax.ppermute(to_b, 'lon', second)  1.92 us
  transfers between devices with their start and end apart: 4, of which 2 were waited for; matrix products, arithmetic and copies ran while one was open for 0% of the time, Pallas kernels for 0%

profile of v9, /device:TPU:1, one launch (start us, length us, event | category | flops | bytes accessed | tf_op | source)
XLA Modules:
  0.0 83.9 jit_solution(9539245693240069029)
XLA Ops:
  0.6 1.7 %shard_map.112 = (f32[10,80,128]{2,1,0:T(8,128)S(1)}, f32[9,80,128]{2,1,0:T(8,128)S(1)}, f32[9,80,128]{2,1,0:T(8,128)S(1)}) custom-call(f32[75,8,128]{2,1,0:T(8,128)} %dir_ref.3, f32[75,75]{1,0:T(8,128)} %refs_1_.1, f32[8,128]{1,0:T(8,128)} %refs_2_.1, f32[8,128]{1,0:T(8,128)} %refs_3_.1, s32[8,128]{1,0:T(8,128)} %refs_4_.1, s32[1,256]{1,0:T(1,128)} %bitcast.17, ...), custom_call_target="tpu_custom_call" | custom-call | tf_op jit(solution)/shard_map/pallas_call | solution.py:419
  2.3 4.4 %collective-permute-start = (f32[9,80,128]{2,1,0:T(8,128)S(1)}, f32[9,80,128]{2,1,0:T(8,128)S(1)}, u32[]{:S(2)}, u32[]{:S(2)}) collective-permute-start(f32[9,80,128]{2,1,0:T(8,128)S(1)} %get-tuple-element.17), channel_id=1, source_target_pairs={{0,1},{1,0},{2,3},{3,2},{4,5},{5,4},{6,7},{7,6},{8,9},{9,8},{10,11... | collective-permute-start | bytes 1105928 | tf_op jit(solution)/shard_map/ppermute | solution.py:445
  6.7 0.7 collective-permute-start.1
  7.4 0.1 pad_add_fusion.flags
  7.5 4.1 %collective-permute-done.ra_ref = f32[9,80,128]{2,1,0:T(8,128)S(1)} collective-permute-done((f32[9,80,128]{2,1,0:T(8,128)S(1)}, f32[9,80,128]{2,1,0:T(8,128)S(1)}, u32[]{:S(2)}, u32[]{:S(2)}) %collective-permute-start) | collective-permute-done | bytes 368672 | tf_op jit(solution)/shard_map/ppermute | solution.py:445
  11.6 0.0 collective-permute-done.1.rb_ref
  11.6 0.0 copy-start.2
  11.6 0.0 copy-start
  11.6 0.0 copy-start.1
  11.6 1.1 %shard_map.113 = (f32[2,9,80,128]{3,2,1,0:T(8,128)S(1)}, f32[8,80,128]{2,1,0:T(8,128)S(1)}, f32[8,80,128]{2,1,0:T(8,128)S(1)}) custom-call(s32[3]{0:T(128)S(1)} %pad_add_fusion.flags, f32[10,80,128]{2,1,0:T(8,128)S(1)} %get-tuple-element.16.own_ref, f32[9,80,128]{2,1,0:T(8,128)S(1)} %collective-permute-done.ra_ref, ...), custom_call_target="tpu_custom_call" | custom-call | tf_op jit(solution)/shard_map/pallas_call | solution.py:447
  12.7 8.9 %collective-permute-start.2 = (f32[8,80,128]{2,1,0:T(8,128)S(1)}, f32[8,80,128]{2,1,0:T(8,128)S(1)}, u32[]{:S(2)}, u32[]{:S(2)}) collective-permute-start(f32[8,80,128]{2,1,0:T(8,128)S(1)} %get-tuple-element.20), channel_id=1, source_target_pairs={{0,16},{16,0},{32,48},{48,32},{64,80},{80,64},{96,112},{112,96},{1... | collective-permute-start | bytes 983048 | tf_op jit(solution)/shard_map/ppermute | solution.py:456
  21.6 1.9 %collective-permute-start.3 = (f32[8,80,128]{2,1,0:T(8,128)S(1)}, f32[8,80,128]{2,1,0:T(8,128)S(1)}, u32[]{:S(2)}, u32[]{:S(2)}) collective-permute-start(f32[8,80,128]{2,1,0:T(8,128)S(1)} %get-tuple-element.21), channel_id=1, source_target_pairs={{0,496},{16,32},{32,16},{48,64},{64,48},{80,96},{96,80},{112,128},... | collective-permute-start | bytes 983048 | tf_op jit(solution)/shard_map/ppermute | solution.py:455
  23.6 0.0 copy-done.2
  23.6 0.1 copy.13
  23.7 0.0 copy-done
  23.7 0.0 copy-done.1
  23.7 0.3 shard_map.114
  24.0 0.0 collective-permute-done.2.qa_ref
  24.0 6.3 %collective-permute-done.3.qb_ref = f32[8,80,128]{2,1,0:T(8,128)S(1)} collective-permute-done((f32[8,80,128]{2,1,0:T(8,128)S(1)}, f32[8,80,128]{2,1,0:T(8,128)S(1)}, u32[]{:S(2)}, u32[]{:S(2)}) %collective-permute-start.3) | collective-permute-done | bytes 327712 | tf_op jit(solution)/shard_map/ppermute | solution.py:455
  30.3 8.1 %shard_map.115 = (f32[75,8,128]{2,1,0:T(8,128)S(1)}, f32[32,128]{1,0:T(8,128)S(1)}) custom-call(s32[3]{0:T(128)S(1)} %pad_add_fusion.flags, f32[10,80,128]{2,1,0:T(8,128)S(1)} %get-tuple-element.16.own_ref, f32[2,9,80,128]{3,2,1,0:T(8,128)S(1)} %get-tuple-element.19.ns_ref, f32[8,80,128]{2,1,0:T(8,128)S(1)} %collective-permute-done.2.qa_ref, ...), custom_call_target="tpu_custom_call" | custom-call | tf_op jit(solution)/shard_map/pallas_call | solution.py:457
  38.4 14.2 %all_to_all.17 = f32[32,1,128]{2,1,0:T(1,128)S(1)} all-to-all(f32[32,1,128]{2,1,0:T(1,128)S(1)} %bitcast.14), channel_id=1, replica_groups=mesh['lon'=32,'lat'=16] {'lon'}, dimensions={0} | all-to-all | bytes 32768 | tf_op jit(solution)/shard_map/all_to_all | solution.py:471
  52.6 0.1 reduce_sum.9
  52.7 29.7 %all_to_all.18 = f32[16,1,128]{2,1,0:T(1,128)S(1)} all-to-all(f32[16,1,128]{2,1,0:T(1,128)S(1)} %broadcast_in_dim.2), channel_id=1, replica_groups=mesh['lon'=32,'lat'=16] {'lat'}, dimensions={0} | all-to-all | bytes 16384 | tf_op jit(solution)/shard_map/all_to_all | solution.py:473
  82.4 1.5 %shard_map.116 = (f32[75,8,128]{2,1,0:T(8,128)}, f32[75,8,128]{2,1,0:T(8,128)}, f32[1,1]{1,0:T(1,128)}) custom-call(f32[16,128]{1,0:T(8,128)S(1)} %bitcast.13, f32[75,8,128]{2,1,0:T(8,128)S(1)} %get-tuple-element.25.img_ref, f32[75,8,128]{2,1,0:T(8,128)S(1)} %copy-done.1, f32[75,8,128]{2,1,0:T(8,128)S(1)} %copy-done), custom_call_target="tpu_custom_call" | custom-call | tf_op jit(solution)/shard_map/pallas_call | solution.py:474
  (1 shorter events, 0.0 us)
Async XLA Ops:
  2.3 9.3 %collective-permute-start = (f32[9,80,128]{2,1,0:T(8,128)S(1)}, f32[9,80,128]{2,1,0:T(8,128)S(1)}, u32[]{:S(2)}, u32[]{:S(2)}) collective-permute-start(f32[9,80,128]{2,1,0:T(8,128)S(1)} %get-tuple-element.17), channel_id=1, source_target_pairs={{0,1},{1,0},{2,3},{3,2},{4,5},{5,4},{6,7},{7,6},{8,9},{9,8},{10,11... | collective-permute-start | bytes 1105928 | tf_op jit(solution)/shard_map/ppermute | solution.py:445
  6.7 4.9 %collective-permute-start.1 = (f32[9,80,128]{2,1,0:T(8,128)S(1)}, f32[9,80,128]{2,1,0:T(8,128)S(1)}, u32[]{:S(2)}, u32[]{:S(2)}) collective-permute-start(f32[9,80,128]{2,1,0:T(8,128)S(1)} %get-tuple-element.18), channel_id=1, source_target_pairs={{1,2},{2,1},{3,4},{4,3},{5,6},{6,5},{7,8},{8,7},{9,10},{10,9},{11,... | collective-permute-start | bytes 1105928 | tf_op jit(solution)/shard_map/ppermute | solution.py:444
  11.6 12.0 %copy-start.2 = (f32[75,75]{1,0:T(8,128)S(1)}, f32[75,75]{1,0:T(8,128)}, u32[]{:S(2)}) copy-start(f32[75,75]{1,0:T(8,128)} %refs_1_.1) | copy-start | bytes 67504
  11.6 12.1 %copy-start = (f32[75,8,128]{2,1,0:T(8,128)S(1)}, f32[75,8,128]{2,1,0:T(8,128)}, u32[]{:S(2)}) copy-start(f32[75,8,128]{2,1,0:T(8,128)} %dir_ref.3) | copy-start | bytes 921604
  11.6 12.1 %copy-start.1 = (f32[75,8,128]{2,1,0:T(8,128)S(1)}, f32[75,8,128]{2,1,0:T(8,128)}, u32[]{:S(2)}) copy-start(f32[75,8,128]{2,1,0:T(8,128)} %res_ref.3) | copy-start | bytes 921604
  12.7 11.3 %collective-permute-start.2 = (f32[8,80,128]{2,1,0:T(8,128)S(1)}, f32[8,80,128]{2,1,0:T(8,128)S(1)}, u32[]{:S(2)}, u32[]{:S(2)}) collective-permute-start(f32[8,80,128]{2,1,0:T(8,128)S(1)} %get-tuple-element.20), channel_id=1, source_target_pairs={{0,16},{16,0},{32,48},{48,32},{64,80},{80,64},{96,112},{112,96},{1... | collective-permute-start | bytes 983048 | tf_op jit(solution)/shard_map/ppermute | solution.py:456
  21.6 8.7 %collective-permute-start.3 = (f32[8,80,128]{2,1,0:T(8,128)S(1)}, f32[8,80,128]{2,1,0:T(8,128)S(1)}, u32[]{:S(2)}, u32[]{:S(2)}) collective-permute-start(f32[8,80,128]{2,1,0:T(8,128)S(1)} %get-tuple-element.21), channel_id=1, source_target_pairs={{0,496},{16,32},{32,16},{48,64},{64,48},{80,96},{96,80},{112,128},... | collective-permute-start | bytes 983048 | tf_op jit(solution)/shard_map/ppermute | solution.py:455
